TPU v7x, 32 devices: a whole 2x2x4 slice. The times are simulated.
32 devices in a mesh: shard: 4 (over z), ctx: 2 (over x), tp: 4 (over y, core).
Axes of the slice: x: 2, y: 2, z: 4, core: 2. Of those that a mesh axis runs over, the one named last changes fastest.
Arguments:
- inputs: bfloat16 [8, 1024, 1024], P('shard', 'ctx', 'tp'), may hold values from -6 to 6
- adapter_id: int32 [8], P('shard'), may hold values from 0 to 7
- cotangent: bfloat16 [8, 1024, 1024], P('shard', 'ctx', 'tp'), may hold values from -6 to 6
- ffn1_in: bfloat16 [1024, 4096], P('shard', 'tp'), may hold values from -0.1875 to 0.1875
- ffn1_out: bfloat16 [1024, 4096], P('shard', 'tp'), may hold values from -0.09375 to 0.09375
- query_w: bfloat16 [1024, 1024], P('shard', 'tp'), may hold values from -0.1875 to 0.1875
- key_w: bfloat16 [1024, 1024], P('shard', 'tp'), may hold values from -0.1875 to 0.1875
- value_w: bfloat16 [1024, 1024], P('shard', 'tp'), may hold values from -0.1875 to 0.1875
- out_w: bfloat16 [1024, 1024], P('shard', 'tp'), may hold values from -0.75 to 0.75
- conv_in_w: bfloat16 [1024, 2, 1024], P('shard', None, 'tp'), may hold values from -0.1875 to 0.1875
- conv_kernel: bfloat16 [31, 1024], P(None, 'tp'), may hold values from -1 to 1
- conv_out_w: bfloat16 [1024, 1024], P('shard', 'tp'), may hold values from -0.1875 to 0.1875
- ffn2_in: bfloat16 [1024, 4096], P('shard', 'tp'), may hold values from -0.1875 to 0.1875
- ffn2_out: bfloat16 [1024, 4096], P('shard', 'tp'), may hold values from -0.09375 to 0.09375
- distance_table: bfloat16 [73, 64], replicated, may hold values from -6 to 6
- adapt_down: bfloat16 [8, 1024, 128], replicated, may hold values from -0.1875 to 0.1875
- adapt_down_ff: bfloat16 [2, 4096, 128], replicated, may hold values from -0.09375 to 0.09375
- adapt_up: bfloat16 [9, 128, 1024], replicated, may hold values from -1.5 to 1.5
- adapt_up_ff: bfloat16 [2, 128, 4096], replicated, may hold values from -1.5 to 1.5
Outputs:
- output: bfloat16 [8, 1024, 1024], P('shard', 'ctx', 'tp')
- input_grad: float32 [8, 1024, 1024], P('shard', 'ctx', 'tp')
- down_grad: float32 [8, 1024, 128], replicated
- down_ff_grad: float32 [2, 4096, 128], replicated
- up_grad: float32 [9, 128, 1024], replicated
- up_ff_grad: float32 [2, 128, 4096], replicated
Inputs may be any that keep to these rules, and one draw needn't show every extreme that they name: adapter_id names one adapter for each sequence.
All inputs are finite; a program needn't handle non-finite values.
Results may differ from a plain program's by a relative error of at most 0.02.
Values may be sent and summed in bfloat16 or wider, within the bound.
No kernel may reach another device: no remote copies, remote signals or barrier semaphores. Data moves between devices by JAX's collectives and lax.ppermute only.
A program may use at most 256 MiB of HBM per device.

v0:
```python
import jax
import jax.numpy as jnp
from jax import lax
from jax.sharding import PartitionSpec as P

LEFT = 64
RIGHT = 8
NADAPT = 8
RANK = 16


eps = 1e-05


def shifted(block, axis, distance):
    devices = range(lax.axis_size(axis))
    route = [(i - distance, i) for i in devices if i - distance in devices]
    return lax.ppermute(block, axis, route)


def inner(first, second):
    return lax.dot_general(
        first, second, (((0,), (0,)), ((), ())), preferred_element_type=jnp.float32
    )


def against(first, second):
    return lax.dot_general(
        first, second, (((1,), (1,)), ((), ())), preferred_element_type=jnp.float32
    )


def plain(first, second):
    return jnp.dot(first, second, preferred_element_type=jnp.float32)


def swish_slope(value):
    sigma = jax.nn.sigmoid(value)
    return sigma + value * sigma * (1.0 - sigma)


def feature_sums(first, second):
    return lax.psum(
        (jnp.sum(first, axis=-1, keepdims=True), jnp.sum(second, axis=-1, keepdims=True)), "tp"
    )


def normalize(value):
    total, square = feature_sums(value, value * value)
    width = value.shape[-1] * lax.axis_size("tp")
    mean = total / width
    scale = lax.rsqrt(square / width - mean * mean + eps)
    return ((value - mean) * scale, scale)


def normalize_back(grad, normed, scale):
    total, cross = feature_sums(grad, grad * normed)
    width = grad.shape[-1] * lax.axis_size("tp")
    return scale * (grad - total / width - normed * (cross / width))


def whole_rows(value):
    full = lax.all_gather(value, "tp", axis=2, tiled=True)
    return full.reshape(-1, full.shape[-1])


def own_share(partial_value, shape):
    return lax.psum_scatter(
        partial_value.reshape(shape[0], shape[1], -1), "tp", scatter_dimension=2, tiled=True
    )


def tp_part(value, axis, count):
    return lax.dynamic_slice_in_dim(value, lax.axis_index("tp") * count, count, axis)


def spread(value, axis, parts):
    shape = list(value.shape)
    shape[axis] = shape[axis] * parts
    return lax.dynamic_update_slice_in_dim(
        jnp.zeros(shape, jnp.float32), value, lax.axis_index("tp") * value.shape[axis], axis
    )


def column_forward(rows, weight, down, up, mask):
    reduced = (plain(rows, down) * mask).astype(jnp.bfloat16)
    return (plain(rows, weight) + plain(reduced, up), reduced)


def column_back(rows, reduced, grad, weight, down, up, mask):
    grad_reduced = (against(grad, up) * mask).astype(jnp.bfloat16)
    partial_value = against(grad, weight) + against(grad_reduced, down)
    return (partial_value, inner(rows, grad_reduced), inner(reduced, grad))


def row_forward(pieces, weight, down, up, mask):
    reduced = (plain(pieces, down) * mask).astype(jnp.bfloat16)
    return (against(pieces, weight) + plain(reduced, up), reduced)


def row_back(pieces, reduced, grad_full, weight, down, up, mask):
    grad_reduced = (against(grad_full, up) * mask).astype(jnp.bfloat16)
    grad_pieces = plain(grad_full, weight) + against(grad_reduced, down)
    return (grad_pieces, inner(pieces, grad_reduced), inner(reduced, grad_full))


def ffn_forward(resid, weight_in, weight_out, down_in, up_in, down_out, up_out, mask):
    normed, scale = normalize(resid)
    rows = whole_rows(normed.astype(jnp.bfloat16))
    pre, reduced_in = column_forward(rows, weight_in, down_in, up_in, mask)
    active = (pre * jax.nn.sigmoid(pre)).astype(jnp.bfloat16)
    partial_value, reduced_out = row_forward(active, weight_out, down_out, up_out, mask)
    result = resid + 0.5 * own_share(partial_value, resid.shape)
    return (result, (normed, scale, rows, pre, active, reduced_in, reduced_out))


def ffn_back(grad, kept, weight_in, weight_out, down_in, up_in, down_out, up_out, mask):
    normed, scale, rows, pre, active, reduced_in, reduced_out = kept
    grad_full = whole_rows((0.5 * grad).astype(jnp.bfloat16))
    grad_active, grad_down_out, grad_up_out = row_back(
        active, reduced_out, grad_full, weight_out, down_out, up_out, mask
    )
    grad_pre = (grad_active * swish_slope(pre)).astype(jnp.bfloat16)
    partial_value, grad_down_in, grad_up_in = column_back(
        rows, reduced_in, grad_pre, weight_in, down_in, up_in, mask
    )
    result = grad + normalize_back(own_share(partial_value, grad.shape), normed, scale)
    return (result, grad_down_in, grad_up_in, grad_down_out, grad_up_out)


def relative_terms(near, anchor, length):
    heads_here, count, distances = near.shape
    span_cols = length + count
    columns = jnp.arange(span_cols, dtype=jnp.int32)
    distance = jnp.clip(columns - count - anchor, -LEFT, RIGHT) + LEFT
    selector = (distance[:, None] == jnp.arange(distances, dtype=jnp.int32)[None, :]).astype(
        jnp.float32
    )
    widened = jnp.einsum("hlr,cr->hlc", near, selector, precision=lax.Precision.HIGHEST)
    flattened = widened.reshape(heads_here, count * span_cols)
    banded = flattened[:, count : count + count * (span_cols - 1)].reshape(
        heads_here, count, span_cols - 1
    )
    return banded[:, :, :length]


def score_block(queries, keys, table, anchor):
    near = jnp.einsum("lhe,re->hlr", queries, table, preferred_element_type=jnp.float32)
    direct = jnp.einsum("lhe,mhe->hlm", queries, keys, preferred_element_type=jnp.float32)
    scale = queries.shape[-1] ** (-0.5)
    return ((direct + relative_terms(near, anchor, keys.shape[0])) * scale, near)


def attention_forward(resid, weights, downs, ups, down_rows, up_rows, table, mask):
    w_query, w_key, w_value, w_out = weights
    seqs_here, piece_len = (resid.shape[0], resid.shape[1])
    normed, scale = normalize(resid)
    rows = whole_rows(normed.astype(jnp.bfloat16))
    projected = []
    reduced = []
    for weight, down, up in zip((w_query, w_key, w_value), downs, ups):
        value, low_rank = column_forward(rows, weight, down, up, mask)
        projected.append(value.astype(jnp.bfloat16).reshape(seqs_here, piece_len, -1))
        reduced.append(low_rank)
    keys_all, values_all = (
        lax.all_gather(projected[1], "ctx", axis=1, tiled=True),
        lax.all_gather(projected[2], "ctx", axis=1, tiled=True),
    )
    head_size = table.shape[1]
    heads_here = projected[0].shape[-1] // head_size
    length = keys_all.shape[1]
    anchor = lax.axis_index("ctx") * piece_len
    queries = projected[0].reshape(seqs_here, piece_len, heads_here, head_size)
    keys = keys_all.reshape(seqs_here, length, heads_here, head_size)
    values = values_all.reshape(seqs_here, length, heads_here, head_size)

    def attend(item):
        scores, near = score_block(item[0], item[1], table, anchor)
        top = jnp.max(scores, axis=-1, keepdims=True)
        total = top + jnp.log(jnp.sum(jnp.exp(scores - top), axis=-1, keepdims=True))
        weights_soft = jnp.exp(scores - total).astype(jnp.bfloat16)
        mixed = jnp.einsum(
            "hlm,mhe->lhe", weights_soft, item[2], preferred_element_type=jnp.float32
        )
        return (mixed, total)

    mixed, totals = lax.map(attend, (queries, keys, values))
    mixed_rows = mixed.reshape(seqs_here * piece_len, -1).astype(jnp.bfloat16)
    partial_value, reduced_out = row_forward(mixed_rows, w_out, down_rows, up_rows, mask)
    result = resid + own_share(partial_value, resid.shape)
    return (
        result,
        (
            normed,
            scale,
            rows,
            queries,
            keys,
            values,
            totals,
            mixed_rows,
            reduced,
            reduced_out,
            anchor,
        ),
    )


def attention_back(grad, kept, weights, downs, ups, down_rows, up_rows, table, mask):
    w_query, w_key, w_value, w_out = weights
    normed, scale, rows, queries, keys, values, totals, mixed_rows, reduced, reduced_out, anchor = (
        kept
    )
    grad_full = whole_rows(grad.astype(jnp.bfloat16))
    grad_mixed, grad_down_out, grad_up_out = row_back(
        mixed_rows, reduced_out, grad_full, w_out, down_rows, up_rows, mask
    )
    grad_mixed = grad_mixed.astype(jnp.bfloat16).reshape(queries.shape)
    table_wide = table.astype(jnp.float32)
    length = keys.shape[1]

    def place(part):
        return relative_terms(part, anchor, length)

    def attend_back(item):
        query, key, value, total, grad_out = item
        scores, near = score_block(query, key, table, anchor)
        probs = jnp.exp(scores - total)
        weights_soft = probs.astype(jnp.bfloat16)
        grad_weights = jnp.einsum(
            "lhe,mhe->hlm", grad_out, value, preferred_element_type=jnp.float32
        )
        grad_scores = (
            probs * (grad_weights - jnp.sum(probs * grad_weights, axis=-1, keepdims=True))
        ).astype(jnp.bfloat16)
        factor = query.shape[-1] ** (-0.5)
        grad_value = jnp.einsum(
            "hlm,lhe->mhe", weights_soft, grad_out, preferred_element_type=jnp.float32
        )
        grad_key = (
            jnp.einsum("hlm,lhe->mhe", grad_scores, query, preferred_element_type=jnp.float32)
            * factor
        )
        grad_query = (
            jnp.einsum("hlm,mhe->lhe", grad_scores, key, preferred_element_type=jnp.float32)
            * factor
        )
        pull = jax.vjp(place, near)[1]
        grad_near = pull(grad_scores.astype(jnp.float32) * factor)[0]
        grad_query = grad_query + jnp.einsum(
            "hlr,re->lhe", grad_near, table_wide, precision=lax.Precision.HIGHEST
        )
        return (grad_query, grad_key, grad_value)

    grad_q, grad_k, grad_v = lax.map(attend_back, (queries, keys, values, totals, grad_mixed))
    seqs_here = keys.shape[0]
    grad_k, grad_v = (
        lax.psum_scatter(
            grad_k.reshape(seqs_here, length, -1), "ctx", scatter_dimension=1, tiled=True
        ),
        lax.psum_scatter(
            grad_v.reshape(seqs_here, length, -1), "ctx", scatter_dimension=1, tiled=True
        ),
    )
    count = rows.shape[0]
    grads = (
        grad_q.reshape(count, -1).astype(jnp.bfloat16),
        grad_k.reshape(count, -1).astype(jnp.bfloat16),
        grad_v.reshape(count, -1).astype(jnp.bfloat16),
    )
    partial_value = jnp.zeros(rows.shape, jnp.float32)
    down_grads = []
    up_grads = []
    for weight, down, up, low_rank, grad_proj in zip(
        (w_query, w_key, w_value), downs, ups, reduced, grads
    ):
        part, grad_down, grad_up = column_back(rows, low_rank, grad_proj, weight, down, up, mask)
        partial_value = partial_value + part
        down_grads.append(grad_down)
        up_grads.append(grad_up)
    result = grad + normalize_back(own_share(partial_value, grad.shape), normed, scale)
    return (result, down_grads, up_grads, grad_down_out, grad_up_out)


def conv_forward(resid, weight_in, weight_out, down_in, up_pair, down_rows, up_rows, kernel, mask):
    seqs_here, piece_len, own_width = resid.shape
    normed, scale = normalize(resid)
    rows = whole_rows(normed.astype(jnp.bfloat16))
    pair, reduced_in = column_forward(rows, weight_in, down_in, up_pair, mask)
    pair = pair.reshape(seqs_here, piece_len, 2, own_width)
    value_half = pair[:, :, 0]
    gate_half = pair[:, :, 1]
    gated = value_half * jax.nn.sigmoid(gate_half)
    reach = kernel.shape[0] - 1
    edge = shifted(gated[:, piece_len - reach :], "ctx", 1)
    padded = jnp.concatenate([edge, gated], axis=1)
    mixed = kernel[0] * padded[:, 0:piece_len]
    for tap in range(1, reach + 1):
        mixed = mixed + kernel[tap] * padded[:, tap : tap + piece_len]
    inner_normed, inner_scale = normalize(mixed)
    active = (
        (inner_normed * jax.nn.sigmoid(inner_normed))
        .astype(jnp.bfloat16)
        .reshape(seqs_here * piece_len, own_width)
    )
    partial_value, reduced_out = row_forward(active, weight_out, down_rows, up_rows, mask)
    result = resid + own_share(partial_value, resid.shape)
    return (
        result,
        (
            normed,
            scale,
            rows,
            value_half,
            gate_half,
            inner_normed,
            inner_scale,
            active,
            reduced_in,
            reduced_out,
        ),
    )


def conv_back(
    grad, kept, weight_in, weight_out, down_in, up_pair, down_rows, up_rows, kernel, mask
):
    (
        normed,
        scale,
        rows,
        value_half,
        gate_half,
        inner_normed,
        inner_scale,
        active,
        reduced_in,
        reduced_out,
    ) = kept
    seqs_here, piece_len, own_width = grad.shape
    grad_full = whole_rows(grad.astype(jnp.bfloat16))
    grad_active, grad_down_out, grad_up_out = row_back(
        active, reduced_out, grad_full, weight_out, down_rows, up_rows, mask
    )
    grad_inner = grad_active.reshape(grad.shape) * swish_slope(inner_normed)
    grad_mixed = normalize_back(grad_inner, inner_normed, inner_scale)
    reach = kernel.shape[0] - 1
    after = shifted(grad_mixed[:, :reach], "ctx", -1)
    padded = jnp.concatenate([grad_mixed, after], axis=1)
    grad_gated = kernel[0] * padded[:, reach : reach + piece_len]
    for tap in range(1, reach + 1):
        grad_gated = grad_gated + kernel[tap] * padded[:, reach - tap : reach - tap + piece_len]
    sigma = jax.nn.sigmoid(gate_half)
    grad_pair = jnp.stack(
        [grad_gated * sigma, grad_gated * value_half * sigma * (1.0 - sigma)], axis=2
    )
    grad_pair = grad_pair.astype(jnp.bfloat16).reshape(seqs_here * piece_len, 2 * own_width)
    partial_value, grad_down_in, grad_up_pair = column_back(
        rows, reduced_in, grad_pair, weight_in, down_in, up_pair, mask
    )
    result = grad + normalize_back(own_share(partial_value, grad.shape), normed, scale)
    return (result, grad_down_in, grad_up_pair, grad_down_out, grad_up_out)


def on_device(
    inputs,
    adapter_id,
    cotangent,
    ffn1_in,
    ffn1_out,
    query_w,
    key_w,
    value_w,
    out_w,
    conv_in_w,
    conv_kernel,
    conv_out_w,
    ffn2_in,
    ffn2_out,
    distance_table,
    adapt_down,
    adapt_down_ff,
    adapt_up,
    adapt_up_ff,
):
    seqs_here, piece_len, own_width = inputs.shape
    tp_count = lax.axis_size("tp")
    width = own_width * tp_count
    hidden_here = ffn1_in.shape[1]
    heads_width = query_w.shape[1]
    chosen = (adapter_id[:, None] == jnp.arange(NADAPT, dtype=jnp.int32)[None, :]).astype(
        jnp.float32
    )
    mask = jnp.repeat(jnp.repeat(chosen, RANK, axis=1), piece_len, axis=0)
    frozen = (
        lax.all_gather(ffn1_in, "shard", axis=0, tiled=True),
        lax.all_gather(ffn1_out, "shard", axis=0, tiled=True),
        lax.all_gather(query_w, "shard", axis=0, tiled=True),
        lax.all_gather(key_w, "shard", axis=0, tiled=True),
        lax.all_gather(value_w, "shard", axis=0, tiled=True),
        lax.all_gather(out_w, "shard", axis=0, tiled=True),
        lax.all_gather(conv_in_w, "shard", axis=0, tiled=True),
        lax.all_gather(conv_out_w, "shard", axis=0, tiled=True),
        lax.all_gather(ffn2_in, "shard", axis=0, tiled=True),
        lax.all_gather(ffn2_out, "shard", axis=0, tiled=True),
    )
    (
        w_ffn1_in,
        w_ffn1_out,
        w_query,
        w_key,
        w_value,
        w_out,
        w_conv_in,
        w_conv_out,
        w_ffn2_in,
        w_ffn2_out,
    ) = frozen
    up_ffn = [tp_part(adapt_up_ff[item], 1, hidden_here) for item in range(2)]
    down_ffn = [tp_part(adapt_down_ff[item], 0, hidden_here) for item in range(2)]
    up_heads = [tp_part(adapt_up[item], 1, heads_width) for item in range(3)]
    up_pair = jnp.concatenate(
        [tp_part(adapt_up[3], 1, own_width), tp_part(adapt_up[4], 1, own_width)], axis=1
    )
    down_attn = tp_part(adapt_down[6], 0, heads_width)
    down_conv = tp_part(adapt_down[7], 0, own_width)
    down_heads_in = (adapt_down[1], adapt_down[2], adapt_down[3])
    kernel = conv_kernel.astype(jnp.float32)
    resid = inputs.astype(jnp.float32)
    first, kept_one = ffn_forward(
        resid, w_ffn1_in, w_ffn1_out, adapt_down[0], up_ffn[0], down_ffn[0], adapt_up[7], mask
    )
    second, kept_two = attention_forward(
        first,
        (w_query, w_key, w_value, w_out),
        down_heads_in,
        up_heads,
        down_attn,
        adapt_up[5],
        distance_table,
        mask,
    )
    third, kept_three = conv_forward(
        second,
        w_conv_in.reshape(width, -1),
        w_conv_out,
        adapt_down[4],
        up_pair,
        down_conv,
        adapt_up[6],
        kernel,
        mask,
    )
    fourth, kept_four = ffn_forward(
        third, w_ffn2_in, w_ffn2_out, adapt_down[5], up_ffn[1], down_ffn[1], adapt_up[8], mask
    )
    final_normed, final_scale = normalize(fourth)
    output = final_normed.astype(jnp.bfloat16)
    frozen_back = (
        lax.all_gather(ffn1_in, "shard", axis=0, tiled=True),
        lax.all_gather(ffn1_out, "shard", axis=0, tiled=True),
        lax.all_gather(query_w, "shard", axis=0, tiled=True),
        lax.all_gather(key_w, "shard", axis=0, tiled=True),
        lax.all_gather(value_w, "shard", axis=0, tiled=True),
        lax.all_gather(out_w, "shard", axis=0, tiled=True),
        lax.all_gather(conv_in_w, "shard", axis=0, tiled=True),
        lax.all_gather(conv_out_w, "shard", axis=0, tiled=True),
        lax.all_gather(ffn2_in, "shard", axis=0, tiled=True),
        lax.all_gather(ffn2_out, "shard", axis=0, tiled=True),
    )
    (
        b_ffn1_in,
        b_ffn1_out,
        b_query,
        b_key,
        b_value,
        b_out,
        b_conv_in,
        b_conv_out,
        b_ffn2_in,
        b_ffn2_out,
    ) = frozen_back
    grad = normalize_back(cotangent.astype(jnp.float32), final_normed, final_scale)
    grad, down_ffn2_in, up_ffn2_in, down_ffn2_out, up_ffn2_out = ffn_back(
        grad,
        kept_four,
        b_ffn2_in,
        b_ffn2_out,
        adapt_down[5],
        up_ffn[1],
        down_ffn[1],
        adapt_up[8],
        mask,
    )
    grad, down_pair, up_pair_grad, down_conv_out, up_conv_out = conv_back(
        grad,
        kept_three,
        b_conv_in.reshape(width, -1),
        b_conv_out,
        adapt_down[4],
        up_pair,
        down_conv,
        adapt_up[6],
        kernel,
        mask,
    )
    grad, down_heads, up_heads_grad, down_attn_out, up_attn_out = attention_back(
        grad,
        kept_two,
        (b_query, b_key, b_value, b_out),
        down_heads_in,
        up_heads,
        down_attn,
        adapt_up[5],
        distance_table,
        mask,
    )
    grad, down_ffn1_in, up_ffn1_in, down_ffn1_out, up_ffn1_out = ffn_back(
        grad,
        kept_one,
        b_ffn1_in,
        b_ffn1_out,
        adapt_down[0],
        up_ffn[0],
        down_ffn[0],
        adapt_up[7],
        mask,
    )
    column_down = jnp.stack(
        [down_ffn1_in, down_heads[0], down_heads[1], down_heads[2], down_pair, down_ffn2_in]
    )
    row_down = jnp.stack([down_attn_out, down_conv_out])
    hidden_down = jnp.stack([down_ffn1_out, down_ffn2_out])
    column_up = jnp.stack(
        [
            up_heads_grad[0],
            up_heads_grad[1],
            up_heads_grad[2],
            up_pair_grad[:, :own_width],
            up_pair_grad[:, own_width:],
        ]
    )
    row_up = jnp.stack([up_attn_out, up_conv_out, up_ffn1_out, up_ffn2_out])
    hidden_up = jnp.stack([up_ffn1_in, up_ffn2_in])
    full_down = jnp.concatenate([column_down, spread(row_down, 1, tp_count)], axis=0)
    full_up = jnp.concatenate([spread(column_up, 2, tp_count), row_up], axis=0)
    down_grad, down_ff_grad, up_grad, up_ff_grad = lax.psum(
        (full_down, spread(hidden_down, 1, tp_count), full_up, spread(hidden_up, 2, tp_count)),
        ("shard", "ctx", "tp"),
    )
    return (output, grad, down_grad, down_ff_grad, up_grad, up_ff_grad)


def solution(mesh):
    placed = (
        P("shard", "ctx", "tp"),
        P("shard"),
        P("shard", "ctx", "tp"),
        P("shard", "tp"),
        P("shard", "tp"),
        P("shard", "tp"),
        P("shard", "tp"),
        P("shard", "tp"),
        P("shard", "tp"),
        P("shard", None, "tp"),
        P(None, "tp"),
        P("shard", "tp"),
        P("shard", "tp"),
        P("shard", "tp"),
        P(),
        P(),
        P(),
        P(),
        P(),
    )
    return jax.shard_map(
        on_device,
        mesh=mesh,
        in_specs=placed,
        out_specs=(P("shard", "ctx", "tp"), P("shard", "ctx", "tp"), P(), P(), P(), P()),
        check_vma=False,
    )
```

profile of v0, /device:TPU:1, one launch (start us, length us, event | category | flops | bytes accessed | tf_op | source)
XLA Modules:
  0.0 1931.2 jit_solution(7108903710034704580)
XLA Ops:
  23.3 19.9 %all-gather.16.cloned.1.call-done = bf16[2,512,1024]{2,1,0:T(8,128)(2,1)} async-done(((bf16[2,512,256]{2,1,0:T(8,128)(2,1)}), bf16[2,512,1024]{2,1,0:T(8,128)(2,1)}) %all-gather.16.cloned.1.call-update) | async-done | bytes 2097168 | tf_op jit(solution)/shard_map/all_gather | solution.py:63
  45.7 44.7 %all-gather.18.cloned.1.call-done = bf16[1024,1024]{1,0:T(8,128)(2,1)} async-done(((bf16[256,1024]{1,0:T(8,128)(2,1)}), bf16[1024,1024]{1,0:T(8,128)(2,1)}) %all-gather.18.cloned.1.call-update) | async-done | bytes 2097168 | tf_op jit(solution)/shard_map/all_gather | solution.py:396
  99.4 37.2 %all-gather.20.cloned.1.call-done = bf16[1024,1024]{1,0:T(8,128)(2,1)} async-done(((bf16[256,1024]{1,0:T(8,128)(2,1)}), bf16[1024,1024]{1,0:T(8,128)(2,1)}) %all-gather.20.cloned.1.call-update) | async-done | bytes 2097168 | tf_op jit(solution)/shard_map/all_gather | solution.py:397
  144.3 43.3 %reduce-scatter.11.cloned.1.call-done = f32[2,512,256]{2,1,0:T(8,128)} async-done(((f32[2,512,1024]{2,1,0:T(8,128)}), f32[2,512,256]{2,1,0:T(8,128)}) %reduce-scatter.11.cloned.1.call-update) | async-done | bytes 1048592 | tf_op jit(solution)/shard_map/reduce_scatter | solution.py:68
  196.3 13.9 all_gather.77
  225.3 15.0 all_gather.74
  244.0 12.4 all_gather.76
  256.4 13.6 all_gather.79
  278.8 147.1 %while.30 = (s32[]{:T(128)}, bf16[2,512,4,64]{1,3,2,0:T(8,128)(2,1)S(1)}, f32[2,4,512,1]{2,1,3,0:T(4,128)}, bf16[2,1024,4,64]{1,3,2,0:T(8,128)(2,1)S(1)}, bf16[2...) while((s32[]{:T(128)}, ...), condition=%wide.region_12.13_spmd, body=%wide.region_9.12_spmd.sunk | while | flops 3326461440 | bytes 150141040 | solution.py:187
  284.3 19.9 %copy.113 = f32[1,4,512,1536]{3,1,2,0:T(4,128)S(1)} copy(f32[1,4,512,1536]{3,2,1,0:T(8,128)S(1)} %convolution_bitcast_fusion.30) | data formatting | bytes 25165824 | tf_op jit(solution)/shard_map/while
  309.4 14.2 reshape.304
  323.6 19.7 %reshape.305 = f32[4,512,1535]{2,1,0:T(8,128)} reshape(f32[3143680]{0:T(1024)} %reshape.304) | data formatting | bytes 25149440 | tf_op jit(solution)/shard_map/while/body/eval_jaxpr/reshape | solution.py:141
  357.8 19.9 %copy.113 = f32[1,4,512,1536]{3,1,2,0:T(4,128)S(1)} copy(f32[1,4,512,1536]{3,2,1,0:T(8,128)S(1)} %convolution_bitcast_fusion.30) | data formatting | bytes 25165824 | tf_op jit(solution)/shard_map/while
  382.9 14.2 reshape.304
  397.1 19.7 %reshape.305 = f32[4,512,1535]{2,1,0:T(8,128)} reshape(f32[3143680]{0:T(1024)} %reshape.304) | data formatting | bytes 25149440 | tf_op jit(solution)/shard_map/while/body/eval_jaxpr/reshape | solution.py:141
  432.6 50.8 %reduce-scatter.13.cloned.1.call-done = f32[2,512,256]{2,1,0:T(8,128)} async-done(((f32[2,512,1024]{2,1,0:T(8,128)}), f32[2,512,256]{2,1,0:T(8,128)}) %reduce-scatter.13.cloned.1.call-update) | async-done | bytes 1048592 | tf_op jit(solution)/shard_map/reduce_scatter | solution.py:68
  496.6 16.2 all-gather.30.cloned.1.call-done
  515.3 22.4 %all-gather.28.cloned.1.call-done = bf16[2,512,1024]{2,1,0:T(8,128)(2,1)} async-done(((bf16[2,512,256]{2,1,0:T(8,128)(2,1)}), bf16[2,512,1024]{2,1,0:T(8,128)(2,1)}) %all-gather.28.cloned.1.call-update) | async-done | bytes 2097168 | tf_op jit(solution)/shard_map/all_gather | solution.py:63
  556.6 14.2 all_gather.82
  593.2 44.7 %reduce-scatter.15.cloned.1.call-done = f32[2,512,256]{2,1,0:T(8,128)} async-done(((f32[2,512,1024]{2,1,0:T(8,128)}), f32[2,512,256]{2,1,0:T(8,128)}) %reduce-scatter.15.cloned.1.call-update) | async-done | bytes 1048592 | tf_op jit(solution)/shard_map/reduce_scatter | solution.py:68
  650.1 23.2 %all-gather.32.cloned.1.call-done = bf16[2,512,1024]{2,1,0:T(8,128)(2,1)} async-done(((bf16[2,512,256]{2,1,0:T(8,128)(2,1)}), bf16[2,512,1024]{2,1,0:T(8,128)(2,1)}) %all-gather.32.cloned.1.call-update) | async-done | bytes 2097168 | tf_op jit(solution)/shard_map/all_gather | solution.py:63
  675.7 44.9 %all-gather.34.cloned.1.call-done = bf16[1024,1024]{1,0:T(8,128)(2,1)} async-done(((bf16[256,1024]{1,0:T(8,128)(2,1)}), bf16[1024,1024]{1,0:T(8,128)(2,1)}) %all-gather.34.cloned.1.call-update) | async-done | bytes 2097168 | tf_op jit(solution)/shard_map/all_gather | solution.py:404
  732.3 34.4 %all-gather.36.cloned.1.call-done = bf16[1024,1024]{1,0:T(8,128)(2,1)} async-done(((bf16[256,1024]{1,0:T(8,128)(2,1)}), bf16[1024,1024]{1,0:T(8,128)(2,1)}) %all-gather.36.cloned.1.call-update) | async-done | bytes 2097168 | tf_op jit(solution)/shard_map/all_gather | solution.py:405
  775.1 43.3 %reduce-scatter.17.cloned.1.call-done = f32[2,512,256]{2,1,0:T(8,128)} async-done(((f32[2,512,1024]{2,1,0:T(8,128)}), f32[2,512,256]{2,1,0:T(8,128)}) %reduce-scatter.17.cloned.1.call-update) | async-done | bytes 1048592 | tf_op jit(solution)/shard_map/reduce_scatter | solution.py:68
  843.4 24.4 %all-gather.38.cloned.1.call-done = bf16[2,512,1024]{2,1,0:T(8,128)(2,1)} async-done(((bf16[2,512,256]{2,1,0:T(8,128)(2,1)}), bf16[2,512,1024]{2,1,0:T(8,128)(2,1)}) %all-gather.38.cloned.1.call-update) | async-done | bytes 2097168 | tf_op jit(solution)/shard_map/all_gather | solution.py:63
  885.8 44.2 %reduce-scatter.19.cloned.1.call-done = f32[2,512,256]{2,1,0:T(8,128)} async-done(((f32[2,512,1024]{2,1,0:T(8,128)}), f32[2,512,256]{2,1,0:T(8,128)}) %reduce-scatter.19.cloned.1.call-update) | async-done | bytes 1048592 | tf_op jit(solution)/shard_map/reduce_scatter | solution.py:68
  945.2 24.6 %all-gather.40.cloned.1.call-done = bf16[2,512,1024]{2,1,0:T(8,128)(2,1)} async-done(((bf16[2,512,256]{2,1,0:T(8,128)(2,1)}), bf16[2,512,1024]{2,1,0:T(8,128)(2,1)}) %all-gather.40.cloned.1.call-update) | async-done | bytes 2097168 | tf_op jit(solution)/shard_map/all_gather | solution.py:63
  1005.0 46.2 %reduce-scatter.21.cloned.1.call-done = f32[2,512,256]{2,1,0:T(8,128)} async-done(((f32[2,512,1024]{2,1,0:T(8,128)}), f32[2,512,256]{2,1,0:T(8,128)}) %reduce-scatter.21.cloned.1.call-update) | async-done | bytes 1048592 | tf_op jit(solution)/shard_map/reduce_scatter | solution.py:68
  1062.4 24.5 %all-gather.42.cloned.1.call-done = bf16[2,512,1024]{2,1,0:T(8,128)(2,1)} async-done(((bf16[2,512,256]{2,1,0:T(8,128)(2,1)}), bf16[2,512,1024]{2,1,0:T(8,128)(2,1)}) %all-gather.42.cloned.1.call-update) | async-done | bytes 2097168 | tf_op jit(solution)/shard_map/all_gather | solution.py:63
  1094.2 301.5 %while.31 = (s32[]{:T(128)}, bf16[2,512,4,64]{1,3,2,0:T(8,128)(2,1)}, f32[2,1024,4,64]{1,3,2,0:T(8,128)}, f32[2,1024,4,64]{1,3,2,0:T(8,128)}, bf16[2,1024,4,64]{...) while((s32[]{:T(128)}, ...), condition=%wide.region_52.53_spmd, body=%wide.region_50.52_spmd.sunk | while | flops 7011269632 | bytes 365463104 | solution.py:255
  1104.5 20.3 %copy.115 = f32[1,4,512,1536]{3,1,2,0:T(4,128)S(1)} copy(f32[1,4,512,1536]{3,2,1,0:T(8,128)S(1)} %convolution_bitcast_fusion.32) | data formatting | bytes 25165824 | tf_op jit(solution)/shard_map/while
  1129.9 14.2 reshape.306
  1144.2 19.7 %reshape.307 = f32[4,512,1535]{2,1,0:T(8,128)} reshape(f32[3143680]{0:T(1024)} %reshape.306) | data formatting | bytes 25149440 | tf_op jit(solution)/shard_map/while/body/eval_jaxpr/reshape | solution.py:141
  1187.9 18.9 reshape.308
  1206.8 15.0 reshape.309
  1228.8 10.1 fusion.632
  1252.3 20.0 %copy.115 = f32[1,4,512,1536]{3,1,2,0:T(4,128)S(1)} copy(f32[1,4,512,1536]{3,2,1,0:T(8,128)S(1)} %convolution_bitcast_fusion.32) | data formatting | bytes 25165824 | tf_op jit(solution)/shard_map/while
  1277.6 14.2 reshape.306
  1291.8 19.7 %reshape.307 = f32[4,512,1535]{2,1,0:T(8,128)} reshape(f32[3143680]{0:T(1024)} %reshape.306) | data formatting | bytes 25149440 | tf_op jit(solution)/shard_map/while/body/eval_jaxpr/reshape | solution.py:141
  1335.5 18.9 reshape.308
  1354.4 15.0 reshape.309
  1376.6 10.1 fusion.632
  1405.9 21.4 %reduce-scatter.25.cloned.1.call-done = f32[2,512,256]{1,2,0:T(8,128)} async-done(((f32[2,1024,256]{1,2,0:T(8,128)}), f32[2,512,256]{1,2,0:T(8,128)}) %reduce-scatter.25.cloned.1.call-update) | async-done | bytes 1048592 | tf_op jit(solution)/shard_map/reduce_scatter | solution.py:261
  1432.8 28.7 %reduce-scatter.23.cloned.1.call-done = f32[2,512,256]{1,2,0:T(8,128)} async-done(((f32[2,1024,256]{1,2,0:T(8,128)}), f32[2,512,256]{1,2,0:T(8,128)}) %reduce-scatter.23.cloned.1.call-update) | async-done | bytes 1048592 | tf_op jit(solution)/shard_map/reduce_scatter | solution.py:258
  1474.1 44.6 %reduce-scatter.27.cloned.1.call-done = f32[2,512,256]{2,1,0:T(8,128)} async-done(((f32[2,512,1024]{2,1,0:T(8,128)}), f32[2,512,256]{2,1,0:T(8,128)}) %reduce-scatter.27.cloned.1.call-update) | async-done | bytes 1048592 | tf_op jit(solution)/shard_map/reduce_scatter | solution.py:68
  1530.9 24.3 %all-gather.44.cloned.1.call-done = bf16[2,512,1024]{2,1,0:T(8,128)(2,1)} async-done(((bf16[2,512,256]{2,1,0:T(8,128)(2,1)}), bf16[2,512,1024]{2,1,0:T(8,128)(2,1)}) %all-gather.44.cloned.1.call-update) | async-done | bytes 2097168 | tf_op jit(solution)/shard_map/all_gather | solution.py:63
  1605.8 11.6 reduce-scatter.29.cloned.1.call-done
  1627.7 282.7 %all-reduce.17.cloned.1.call-done = (f32[8,1024,128]{2,1,0:T(8,128)}, f32[2,4096,128]{2,1,0:T(8,128)}, f32[9,128,1024]{2,1,0:T(8,128)}, f32[2,128,4096]{2,1,0:T(8,128)}) async-done(((f32[8,1024,128]{2,1,0:T(8,128)}, f32[2,4096,128]{2,1,0:T(8,128)}, f32[9,128,1024]{2,1,0:T(8,128)}, f32[2,128,4096]{2,1,0:T(8,128)}), (f32[8,1024,128]{2,1,0:T(8,128)}, f32[2,4096,128]{2,1,0:T(8,128)}, f32[9,128,1024]{2,1,0:T(8,128)}, ...) | async-done | bytes 17301520 | tf_op jit(solution)/shard_map/psum | solution.py:547
  (763 shorter events, 531.3 us)
Async XLA Ops:
  7.2 36.0 %all-gather.16.cloned.1.call-start = ((), (), s32[]{:S(2)}) async-start(), calls=%async_computation.10 | async-start | bytes 2621440 | tf_op jit(solution)/shard_map/all_gather | solution.py:63
  18.1 72.3 %all-gather.18.cloned.1.call-start = ((), (), s32[]{:S(2)}) async-start(), calls=%async_computation.11 | async-start | bytes 2621440 | tf_op jit(solution)/shard_map/all_gather | solution.py:396
  18.8 117.8 %all-gather.20.cloned.1.call-start = ((), (), s32[]{:S(2)}) async-start(), calls=%async_computation.12 | async-start | bytes 2621440 | tf_op jit(solution)/shard_map/all_gather | solution.py:397
  19.6 168.1 %reduce-scatter.11.cloned.1.call-start = ((), (), s32[]{:S(2)}) async-start(), calls=%async_computation.13 | async-start | bytes 5242880 | tf_op jit(solution)/shard_map/reduce_scatter | solution.py:68
  19.9 252.1 %copy-start.114 = (f32[2,128]{1,0:T(2,128)}, f32[2,128]{1,0:T(2,128)S(1)}, u32[]{:S(2)}) copy-start(f32[2,128]{1,0:T(2,128)S(1)} %reshape.257) | copy-start | bytes 3076
  23.3 70.9 %copy-start.102 = (bf16[1,128,4096]{2,1,0:T(8,128)(2,1)}, bf16[1,128,4096]{2,1,0:T(8,128)(2,1)S(1)}, u32[]{:S(2)}) copy-start(bf16[1,128,4096]{2,1,0:T(8,128)(2,1)S(1)} %get-tuple-element.464) | copy-start | bytes 3145732
  43.2 47.1 %copy-start.15 = (bf16[2,512,1024]{2,1,0:T(8,128)(2,1)S(1)}, bf16[2,512,1024]{2,1,0:T(8,128)(2,1)}, u32[]{:S(2)}) copy-start(bf16[2,512,1024]{2,1,0:T(8,128)(2,1)} %all-gather.16.cloned.1.call-done) | copy-start | bytes 6291460
  45.7 48.6 %copy-start.106 = (bf16[1024,128]{1,0:T(8,128)(2,1)}, bf16[1024,128]{1,0:T(8,128)(2,1)S(1)}, u32[]{:S(2)}) copy-start(bf16[1024,128]{1,0:T(8,128)(2,1)S(1)} %fusion.89) | copy-start | bytes 786436
  144.3 52.0 %copy-start.122 = (bf16[256,256]{1,0:T(8,128)(2,1)S(1)}, bf16[256,256]{1,0:T(8,128)(2,1)}, u32[]{:S(2)}) copy-start(bf16[256,256]{1,0:T(8,128)(2,1)} %param.29) | copy-start | bytes 393220
  144.3 76.6 %all-gather.22.cloned.1.call-start = ((), (), s32[]{:S(2)}) async-start(), calls=%async_computation.14 | async-start | bytes 2621440 | tf_op jit(solution)/shard_map/all_gather | solution.py:63
  196.3 79.5 %all-gather.26.cloned.1.call-start = ((), (), s32[]{:S(2)}) async-start(), calls=%async_computation.16 | async-start | bytes 1572864 | tf_op jit(solution)/shard_map/all_gather | solution.py:166
  212.6 61.7 %copy-start.112 = (bf16[1,128,1024]{2,1,0:T(8,128)(2,1)}, bf16[1,128,1024]{2,1,0:T(8,128)(2,1)S(1)}, u32[]{:S(2)}) copy-start(bf16[1,128,1024]{2,1,0:T(8,128)(2,1)S(1)} %get-tuple-element.459) | copy-start | bytes 786436
  225.2 52.0 %all-gather.24.cloned.1.call-start = ((), (), s32[]{:S(2)}) async-start(), calls=%async_computation.15 | async-start | bytes 1572864 | tf_op jit(solution)/shard_map/all_gather | solution.py:167
  244.0 239.4 %reduce-scatter.13.cloned.1.call-start = ((), (), s32[]{:S(2)}) async-start(), calls=%async_computation.17 | async-start | bytes 5242880 | tf_op jit(solution)/shard_map/reduce_scatter | solution.py:68
  278.8 147.8 %copy-start.113 = (bf16[1,1024,128]{2,1,0:T(8,128)(2,1)S(1)}, bf16[1,1024,128]{2,1,0:T(8,128)(2,1)}, u32[]{:S(2)}) copy-start(bf16[1,1024,128]{2,1,0:T(8,128)(2,1)} %get-tuple-element.466) | copy-start | bytes 786436
  278.8 147.8 %copy-start.115 = (f32[2,128]{1,0:T(2,128)S(1)}, f32[2,128]{1,0:T(2,128)}, u32[]{:S(2)}) copy-start(f32[2,128]{1,0:T(2,128)} %copy-done.114) | copy-start | bytes 3076
  431.8 81.0 %all-gather.30.cloned.1.call-start = ((), (), s32[]{:S(2)}) async-start(), calls=%async_computation.19 | async-start | bytes 1310720 | tf_op jit(solution)/shard_map/all_gather | solution.py:402
  432.6 62.7 %copy-start.152 = (bf16[31,256]{1,0:T(8,128)(2,1)S(1)}, bf16[31,256]{1,0:T(8,128)(2,1)}, u32[]{:S(2)}) copy-start(bf16[31,256]{1,0:T(8,128)(2,1)} %param.33) | copy-start | bytes 47620
  432.6 105.2 %all-gather.28.cloned.1.call-start = ((), (), s32[]{:S(2)}) async-start(), calls=%async_computation.18 | async-start | bytes 2621440 | tf_op jit(solution)/shard_map/all_gather | solution.py:63
  486.1 51.7 %copy-start.116 = (f32[2,128]{1,0:T(2,128)S(1)}, f32[2,128]{1,0:T(2,128)}, u32[]{:S(2)}) copy-start(f32[2,128]{1,0:T(2,128)} %copy-done.114) | copy-start | bytes 3076
  494.3 143.5 %reduce-scatter.15.cloned.1.call-start = ((), (), s32[]{:S(2)}) async-start(), calls=%async_computation.20 | async-start | bytes 5242880 | tf_op jit(solution)/shard_map/reduce_scatter | solution.py:68
  553.5 17.3 collective-permute-start
  593.1 80.2 %copy-start.117 = (f32[2,128]{1,0:T(2,128)S(1)}, f32[2,128]{1,0:T(2,128)}, u32[]{:S(2)}) copy-start(f32[2,128]{1,0:T(2,128)} %copy-done.114) | copy-start | bytes 3076
  593.1 80.2 %all-gather.32.cloned.1.call-start = ((), (), s32[]{:S(2)}) async-start(), calls=%async_computation.21 | async-start | bytes 2621440 | tf_op jit(solution)/shard_map/all_gather | solution.py:63
  648.8 71.8 %all-gather.34.cloned.1.call-start = ((), (), s32[]{:S(2)}) async-start(), calls=%async_computation.22 | async-start | bytes 2621440 | tf_op jit(solution)/shard_map/all_gather | solution.py:404
  649.5 117.2 %all-gather.36.cloned.1.call-start = ((), (), s32[]{:S(2)}) async-start(), calls=%async_computation.23 | async-start | bytes 2621440 | tf_op jit(solution)/shard_map/all_gather | solution.py:405
  650.1 168.3 %reduce-scatter.17.cloned.1.call-start = ((), (), s32[]{:S(2)}) async-start(), calls=%async_computation.24 | async-start | bytes 5242880 | tf_op jit(solution)/shard_map/reduce_scatter | solution.py:68
  675.7 49.4 %copy-start.108 = (bf16[1024,128]{1,0:T(8,128)(2,1)}, bf16[1024,128]{1,0:T(8,128)(2,1)S(1)}, u32[]{:S(2)}) copy-start(bf16[1024,128]{1,0:T(8,128)(2,1)S(1)} %fusion.97) | copy-start | bytes 786436
  775.0 54.4 %copy-start.51 = (bf16[2,512,256]{2,1,0:T(8,128)(2,1)S(1)}, bf16[2,512,256]{2,1,0:T(8,128)(2,1)}, u32[]{:S(2)}) copy-start(bf16[2,512,256]{2,1,0:T(8,128)(2,1)} %param.25) | copy-start | bytes 1572868
  775.0 92.7 %all-gather.38.cloned.1.call-start = ((), (), s32[]{:S(2)}) async-start(), calls=%async_computation.25 | async-start | bytes 2621440 | tf_op jit(solution)/shard_map/all_gather | solution.py:63
  843.0 87.1 %reduce-scatter.19.cloned.1.call-start = ((), (), s32[]{:S(2)}) async-start(), calls=%async_computation.26 | async-start | bytes 5242880 | tf_op jit(solution)/shard_map/reduce_scatter | solution.py:68
  885.8 84.0 %all-gather.40.cloned.1.call-start = ((), (), s32[]{:S(2)}) async-start(), calls=%async_computation.27 | async-start | bytes 2621440 | tf_op jit(solution)/shard_map/all_gather | solution.py:63
  945.2 106.1 %reduce-scatter.21.cloned.1.call-start = ((), (), s32[]{:S(2)}) async-start(), calls=%async_computation.28 | async-start | bytes 5242880 | tf_op jit(solution)/shard_map/reduce_scatter | solution.py:68
  983.6 5.1 collective-permute-start.1
  1004.9 46.3 %copy-start.132 = (f32[2,512]{1,0:T(2,128)S(1)}, f32[2,512]{1,0:T(2,128)}, u32[]{:S(2)}) copy-start(f32[2,512]{1,0:T(2,128)} %copy-done.131) | copy-start | bytes 12292
  1005.0 81.9 %all-gather.42.cloned.1.call-start = ((), (), s32[]{:S(2)}) async-start(), calls=%async_computation.29 | async-start | bytes 2621440 | tf_op jit(solution)/shard_map/all_gather | solution.py:63
  1062.3 365.0 %reduce-scatter.25.cloned.1.call-start = ((), (), s32[]{:S(2)}) async-start(), calls=%async_computation.31 | async-start | bytes 3145728 | tf_op jit(solution)/shard_map/reduce_scatter | solution.py:261
  1395.7 65.8 %reduce-scatter.23.cloned.1.call-start = ((), (), s32[]{:S(2)}) async-start(), calls=%async_computation.30 | async-start | bytes 3145728 | tf_op jit(solution)/shard_map/reduce_scatter | solution.py:258
  1396.5 122.2 %reduce-scatter.27.cloned.1.call-start = ((), (), s32[]{:S(2)}) async-start(), calls=%async_computation.32 | async-start | bytes 5242880 | tf_op jit(solution)/shard_map/reduce_scatter | solution.py:68
  1473.9 52.5 %copy-start.4 = (f32[2,512,256]{2,1,0:T(8,128)S(1)}, f32[2,512,256]{2,1,0:T(8,128)}, u32[]{:S(2)}) copy-start(f32[2,512,256]{2,1,0:T(8,128)} %get-tuple-element.450) | copy-start | bytes 3145732
  1473.9 52.5 %copy-start.28 = (f32[2,512,256]{2,1,0:T(8,128)S(1)}, f32[2,512,256]{2,1,0:T(8,128)}, u32[]{:S(2)}) copy-start(f32[2,512,256]{2,1,0:T(8,128)} %reduce-scatter.21.cloned.1.call-done) | copy-start | bytes 3145732
  1474.0 52.5 %copy-start.130 = (f32[2,512]{1,0:T(2,128)S(1)}, f32[2,512]{1,0:T(2,128)}, u32[]{:S(2)}) copy-start(f32[2,512]{1,0:T(2,128)} %copy-done.128) | copy-start | bytes 12292
  1474.0 52.5 %copy-start.133 = (f32[2,512]{1,0:T(2,128)S(1)}, f32[2,512]{1,0:T(2,128)}, u32[]{:S(2)}) copy-start(f32[2,512]{1,0:T(2,128)} %copy-done.131) | copy-start | bytes 12292
  1474.0 52.5 %copy-start.154 = (f32[2,512]{1,0:T(2,128)S(1)}, f32[2,512]{1,0:T(2,128)}, u32[]{:S(2)}) copy-start(f32[2,512]{1,0:T(2,128)} %copy-done.153) | copy-start | bytes 12292
  1474.0 52.5 %copy-start.156 = (f32[2,512]{1,0:T(2,128)S(1)}, f32[2,512]{1,0:T(2,128)}, u32[]{:S(2)}) copy-start(f32[2,512]{1,0:T(2,128)} %copy-done.155) | copy-start | bytes 12292
  1474.0 81.2 %all-gather.44.cloned.1.call-start = ((), (), s32[]{:S(2)}) async-start(), calls=%async_computation.33 | async-start | bytes 2621440 | tf_op jit(solution)/shard_map/all_gather | solution.py:63
  1530.6 86.8 %reduce-scatter.29.cloned.1.call-start = ((), (), s32[]{:S(2)}) async-start(), calls=%async_computation.34 | async-start | bytes 5242880 | tf_op jit(solution)/shard_map/reduce_scatter | solution.py:68
  1573.1 337.2 %all-reduce.17.cloned.1.call-start = ((), (), s32[]{:S(2)}) async-start(), calls=%async_computation.35 | async-start | bytes 34603008 | tf_op jit(solution)/shard_map/psum | solution.py:547
  (214 other events, 2168.5 us)
Sparse Core Ops, SparseCore 0:
  18.2 24.9 all-gather.15
  44.8 45.5 all-gather.17
  91.9 44.6 all-gather.19
  144.4 43.2 reduce-scatter.10
  196.4 24.4 all-gather.21
  225.4 20.8 all-gather.25
  248.5 21.2 all-gather.23
  431.9 51.4 reduce-scatter.12
  485.0 27.7 all-gather.29
  514.8 22.8 all-gather.27
  593.2 44.6 reduce-scatter.14
  648.9 24.4 all-gather.31
  675.0 45.5 all-gather.33
  722.0 44.6 all-gather.35
  775.1 43.2 reduce-scatter.16
  843.1 24.6 all-gather.37
  885.9 44.0 reduce-scatter.18
  945.3 24.4 all-gather.39
  1005.1 46.1 reduce-scatter.20
  1062.4 24.4 all-gather.41
  1395.8 31.3 reduce-scatter.24
  1429.6 31.8 reduce-scatter.22
  1474.1 44.5 reduce-scatter.26
  1530.7 24.4 all-gather.43
  1573.3 44.0 reduce-scatter.28
  1624.3 286.0 all-reduce.16
where the time goes:
time: 1940 us; the launch traced here: 1930 us
  waiting for transfers between devices  1020 us (53%)
  local copies, waits for them, and re-layouts  407 us (21%)
  matrix products  242 us (12%)
  blocking collectives  143 us (7%)
  other arithmetic  88.6 us (5%)
    reduce_scatter x8, waiting for transfers between devices, own_share(): lax.psum_scatter(partial_value.reshape(shape[0], shape[1], -1), 'tp', sca...  329 us
    psum x1, waiting for transfers between devices, on_device(): lax.psum((full_down, spread(hidden_down, 1, tp_count), full_up, spread(hi...  283 us
    while x34, local copies, waits for them, and re-layouts  183 us
    all_gather x8, waiting for transfers between devices, whole_rows(): full = lax.all_gather(value, 'tp', axis=2, tiled=True)  172 us
    reshape x6, local copies, waits for them, and re-layouts, relative_terms(): flattened[:, count:count + count * (span_cols - 1)]  109 us
    psum x12, blocking collectives, feature_sums(): lax.psum((jnp.sum(first, axis=-1, keepdims=True), jnp.sum(second, axis=-1...  74.1 us
    dot_general x30, matrix products, against(): lax.dot_general(first, second, (((1,), (1,)), ((), ())), preferred_elemen...  70.4 us
    dot_general x30, matrix products, plain(): return jnp.dot(first, second, preferred_element_type=jnp.float32)  67.3 us
  transfers between devices with their start and end apart: 28, of which 25 were waited for; matrix products, arithmetic and copies ran while one was open for 5% of the time, Pallas kernels for 0%

commit v1 on v0

v1 whole, which is shorter than its diff:
```python
import jax
import jax.numpy as jnp
from jax import lax
from jax.experimental import pallas as pl
from jax.experimental.pallas import tpu as pltpu
from jax.sharding import PartitionSpec as P

LEFT = 64
RIGHT = 8
NADAPT = 8
RANK = 16
HEAD = 64
LANES = 128
eps = 1e-05
BF = jnp.bfloat16
F32 = jnp.float32

CORE = [(0, 1), (1, 0), (2, 3), (3, 2)]
PAIR = [(0, 2), (2, 0), (1, 3), (3, 1)]
SIDE = [(0, 1), (1, 0)]
ACROSS = [(s * 4 + t, (1 - s) * 4 + (t ^ 2)) for s in range(2) for t in range(4)]


def block_at(block, core):
    return (block // 2) * 4 + (block % 2) * 2 + core


NEXT = [(block_at(n, k), block_at(n + 1, k)) for n in range(3) for k in range(2)]
BEFORE = [(block_at(n + 1, k), block_at(n, k)) for n in range(3) for k in range(2)]


def by_core(value):
    return lax.ppermute(value, "tp", CORE)


def by_pair(value):
    return lax.ppermute(value, "tp", PAIR)


def by_side(value):
    return lax.ppermute(value, "ctx", SIDE)


def across(value):
    return lax.ppermute(value, ("ctx", "tp"), ACROSS)


def wide_table(table):
    place = jnp.arange(4*LANES, dtype=jnp.int32)
    index = jnp.where(place < 3*LANES, jnp.clip(place - LEFT, 0, LEFT+RIGHT), 0)
    pick = (index[:, None] == jnp.arange(table.shape[0], dtype=jnp.int32)[None, :]).astype(BF)
    rows = jnp.dot(pick, table, preferred_element_type=F32).astype(BF)
    return jnp.concatenate([rows, rows], axis=1)

def load_blocks(b_ref, sources, target, sems, parts):
    copies=[]
    for j, source in enumerate(sources):
        rows = source.shape[0]; cols = source.shape[1]//parts
        for part in range(parts):
            copies.append(pltpu.make_async_copy(
                source.at[:, part*cols:(part+1)*cols],
                target.at[part, pl.ds(pl.multiple_of((b_ref[0] ^ j)*rows, rows), rows), :],
                sems.at[j*parts+part]))
    for c in copies: c.start()
    for c in copies: c.wait()

def window(r0, length):
    lo=max(r0-LANES,0); hi=min(r0+2*LANES,length)
    return lo,hi

def biased(s, near, p, rows, length):
    parts=[]
    for sub in range(rows//LANES):
        r0=p*rows+sub*LANES
        e=near[sub*LANES:(sub+1)*LANES]
        band=pltpu.roll(e, 0, 1, stride=1, stride_axis=0)
        lo,hi=window(r0,length)
        pieces=[]
        if lo>0: pieces.append(jnp.broadcast_to(e[:,0:1],(LANES,lo)))
        pieces.append(band[:, lo-r0+LANES:hi-r0+LANES])
        if hi<length: pieces.append(jnp.broadcast_to(e[:,2*LANES-1:2*LANES],(LANES,length-hi)))
        parts.append(jnp.concatenate(pieces,axis=1))
    return s+jnp.concatenate(parts,axis=0)


def fwd_kernel(b_ref, s0,s1,s2,s3, text_ref, o_ref, lse_ref, qkv, sems):
    dc=pl.program_id(0); k=pl.program_id(1)
    @pl.when((dc==0)&(k==0))
    def _(): load_blocks(b_ref,(s0,s1,s2,s3),qkv,sems,2)
    rows=o_ref.shape[1]; length=qkv.shape[1]
    own=(lax.broadcasted_iota(jnp.int32,(rows,LANES),1)//64)==k
    key=qkv[dc,:,LANES:2*LANES]; val=qkv[dc,:,2*LANES:]
    for p in range(length//rows):
        q=qkv[dc,p*rows:(p+1)*rows,0:LANES].astype(F32)*0.125
        q=jnp.where(own,q,0.0).astype(BF)
        s=biased(nt(q,key),nt(q,text_ref[...]),p,rows,length)
        top=jnp.max(s,axis=-1,keepdims=True)
        e=jnp.exp(s-top)
        tot=jnp.sum(e,axis=-1,keepdims=True)
        o=jnp.dot(e.astype(BF),val,preferred_element_type=F32)/tot
        o=o.astype(BF)
        slot=p^b_ref[0]
        @pl.when(k==0)
        def _(): o_ref[slot]=o
        @pl.when(k==1)
        def _(): o_ref[slot]=jnp.where(own,o,o_ref[slot])
        lse_ref[0,p*rows:(p+1)*rows,:]=top+jnp.log(tot)

def attend(b, slots, text):
    rows=slots[0].shape[0]; n=len(slots); length=rows*n
    anys=[pl.BlockSpec(memory_space=pl.ANY)]*n
    return pl.pallas_call(
        fwd_kernel,
        grid_spec=pltpu.PrefetchScalarGridSpec(
            num_scalar_prefetch=1, grid=(2,2),
            in_specs=anys+[pl.BlockSpec(text.shape,lambda d,k,b:(0,0))],
            out_specs=(pl.BlockSpec((n,rows,LANES),lambda d,k,b:(0,0,d)),
                       pl.BlockSpec((1,length,1),lambda d,k,b:(2*d+k,0,0))),
            scratch_shapes=[pltpu.VMEM((2,length,3*LANES),BF),pltpu.SemaphoreType.DMA((2*n,))]),
        out_shape=(jax.ShapeDtypeStruct((n,rows,2*LANES),BF),jax.ShapeDtypeStruct((4,length,1),F32)),
        compiler_params=pltpu.CompilerParams(vmem_limit_bytes=48<<20),
        name="attend",
        cost_estimate=pl.CostEstimate(flops=4*4*length*length*64,bytes_accessed=length*8*LANES*2,transcendentals=4*length*length),
    )(b,*slots,text)

def bwd_kernel(b_ref, s0,s1,s2,s3, g0,g1,g2,g3, text_ref, lse_ref, out_ref, qkv, gout, dq_acc, dk_acc, dv_acc, sems, gsems):
    dc=pl.program_id(0); k=pl.program_id(1)
    @pl.when((dc==0)&(k==0))
    def _():
        load_blocks(b_ref,(s0,s1,s2,s3),qkv,sems,2)
        load_blocks(b_ref,(g0,g1,g2,g3),gout,gsems,2)
    rows=out_ref.shape[1]; length=qkv.shape[1]
    own=(lax.broadcasted_iota(jnp.int32,(rows,LANES),1)//64)==k
    key=qkv[dc,:,LANES:2*LANES]; val=qkv[dc,:,2*LANES:]
    text=text_ref[...]
    turn=((lax.broadcasted_iota(jnp.int32,(LANES,LANES),0)+lax.broadcasted_iota(jnp.int32,(LANES,LANES),1))==LANES-1).astype(BF)
    @pl.when(k==0)
    def _():
        dk_acc[...]=jnp.zeros_like(dk_acc); dv_acc[...]=jnp.zeros_like(dv_acc)
    for p in range(length//rows):
        span=slice(p*rows,(p+1)*rows)
        q=qkv[dc,span,0:LANES].astype(F32)*0.125
        q=jnp.where(own,q,0.0).astype(BF)
        g=jnp.where(own,gout[dc,span,:].astype(F32),0.0).astype(BF)
        s=biased(nt(q,key),nt(q,text),p,rows,length)
        pr=jnp.exp(s-lse_ref[0,span,:])
        dp=nt(g,val)
        w=pr*dp
        ds=(w-pr*jnp.sum(w,axis=-1,keepdims=True)).astype(BF)
        dv_acc[...]+=tn(g,pr.astype(BF))
        dk_acc[...]+=tn(q,ds)
        dq=jnp.dot(ds,key,preferred_element_type=F32)
        extra=[]
        t_lo=text[0:1,:].astype(F32); t_hi=text[2*LANES-1:2*LANES,:].astype(F32)
        for sub in range(rows//LANES):
            r0=p*rows+sub*LANES
            lo,hi=window(r0,length)
            d=ds[sub*LANES:(sub+1)*LANES].astype(F32)
            pieces=[]
            if lo-r0+LANES>0: pieces.append(jnp.zeros((LANES,lo-r0+LANES),F32))
            pieces.append(d[:,lo:hi])
            pieces.append(jnp.zeros((LANES,4*LANES-(hi-r0+LANES)),F32))
            w=jnp.concatenate(pieces,axis=1)
            w=jnp.dot(turn,w.astype(BF),preferred_element_type=F32)
            w=pltpu.roll(w,3*LANES+1,1,stride=1,stride_axis=0)
            w=jnp.dot(turn,w.astype(BF),preferred_element_type=F32)
            x=jnp.dot(w.astype(BF),text,preferred_element_type=F32)
            if lo>0: x+=jnp.sum(d[:,:lo],axis=-1,keepdims=True)*t_lo
            if hi<length: x+=jnp.sum(d[:,hi:],axis=-1,keepdims=True)*t_hi
            extra.append(x)
        dq=(dq+jnp.concatenate(extra,axis=0))*0.125
        dq_acc[span,:]=jnp.where(own,dq,dq_acc[span,:])
    @pl.when(k==1)
    def _():
        for p in range(length//rows):
            slot=p^b_ref[0]; span=slice(p*rows,(p+1)*rows)
            out_ref[slot,:,0:LANES]=dq_acc[span,:].astype(BF)
            out_ref[slot,:,LANES:2*LANES]=dk_acc[:,span].T.astype(BF)
            out_ref[slot,:,2*LANES:]=dv_acc[:,span].T.astype(BF)

def attend_back(b, slots, grads, text, lse):
    rows=slots[0].shape[0]; n=len(slots); length=rows*n
    anys=[pl.BlockSpec(memory_space=pl.ANY)]*(2*n)
    return pl.pallas_call(
        bwd_kernel,
        grid_spec=pltpu.PrefetchScalarGridSpec(
            num_scalar_prefetch=1, grid=(2,2),
            in_specs=anys+[pl.BlockSpec(text.shape,lambda d,k,b:(0,0)),pl.BlockSpec((1,length,1),lambda d,k,b:(2*d+k,0,0))],
            out_specs=pl.BlockSpec((n,rows,3*LANES),lambda d,k,b:(0,0,d)),
            scratch_shapes=[pltpu.VMEM((2,length,3*LANES),BF),pltpu.VMEM((2,length,LANES),BF),
              pltpu.VMEM((length,LANES),F32),pltpu.VMEM((LANES,length),F32),pltpu.VMEM((LANES,length),F32),
              pltpu.SemaphoreType.DMA((2*n,)),pltpu.SemaphoreType.DMA((2*n,))]),
        out_shape=jax.ShapeDtypeStruct((n,rows,6*LANES),BF),
        compiler_params=pltpu.CompilerParams(vmem_limit_bytes=56<<20),
        name="attend_back",
        cost_estimate=pl.CostEstimate(flops=10*4*length*length*64,bytes_accessed=length*14*LANES*2,transcendentals=4*length*length),
    )(b,*slots,*grads,text,lse)


def nn(first, second):
    return jnp.dot(first, second, preferred_element_type=F32)


def nt(first, second):
    return lax.dot_general(first, second, (((1,), (1,)), ((), ())), preferred_element_type=F32)


def tn(first, second):
    return lax.dot_general(first, second, (((0,), (0,)), ((), ())), preferred_element_type=F32)


def normalize(value):
    mean = jnp.mean(value, axis=-1, keepdims=True)
    square = jnp.mean(value * value, axis=-1, keepdims=True)
    scale = lax.rsqrt(square - mean * mean + eps)
    return ((value - mean) * scale, scale)


def normalize_back(grad, normed, scale):
    mean = jnp.mean(grad, axis=-1, keepdims=True)
    cross = jnp.mean(grad * normed, axis=-1, keepdims=True)
    return scale * (grad - mean - normed * cross)


def swish_slope(value, sigma):
    return sigma + value * sigma * (1.0 - sigma)


def mask_row(adapter):
    lanes = lax.broadcasted_iota(jnp.int32, (1, NADAPT * RANK), 1)
    return (lanes // RANK == adapter).astype(F32)


def chosen_rows(adapter):
    shape = (RANK, NADAPT * RANK)
    lanes = lax.broadcasted_iota(jnp.int32, shape, 1)
    rows = lax.broadcasted_iota(jnp.int32, shape, 0)
    return (lanes == rows + adapter * RANK).astype(BF)


def compact(pick, value):
    return nt(pick, value).astype(BF)


class Fetches:
    def __init__(self, sems):
        self.sems = sems
        self.used = 0

    def __call__(self, source, target):
        copy = pltpu.make_async_copy(source, target, self.sems.at[self.used])
        self.used += 1
        copy.start()
        return copy


def wait_all(copies):
    for copy in copies:
        copy.wait()


def block_of(where, number):
    side, pair, core = number // 4, (number // 2) % 2, number % 2
    return ((where[0] ^ pair) * 2 + (where[1] ^ core)) * 2 + (where[2] ^ side)


def fetch_columns(fetch, where, source, target):
    found = []
    for number in range(8):
        start = pl.multiple_of(block_of(where, number) * LANES, LANES)
        place = pl.ds(number * LANES, LANES)
        found.append(fetch(source.at[:, pl.ds(start, LANES)], target.at[:, place]))
    return found


def fetch_rows(fetch, where, source, target):
    found = []
    for number in range(8):
        start = pl.multiple_of(block_of(where, number) * LANES, LANES)
        place = pl.ds(number * LANES, LANES)
        found.append(fetch(source.at[pl.ds(start, LANES), :], target.at[place, :]))
    return found


def store_absolute(where, out, first, value):
    rows = value.shape[0]
    for number in range(8):
        pair, side, half = number // 4, (number // 2) % 2, number % 2
        out[side ^ where[2], pair ^ where[0], half, first : first + rows, :] = value[
            :, number * LANES : (number + 1) * LANES
        ]


def store_relative(where, out, first, value, number):
    side, pair, core = number // 4, (number // 2) % 2, number % 2
    out[(where[1] ^ core) ^ where[2], pair, where[2] ^ side, first : first + value.shape[0], :] = value


def store_edge(out, value, flip_side):
    rows = value.shape[0]
    width = value.shape[1] // 4
    for side in range(2):
        for pair in range(2):
            start = (2 * side + pair) * width
            out[side ^ flip_side, 1 - pair] = value[:, start : start + width]


def read_edge(edge):
    return jnp.concatenate([edge[s, p] for s in range(2) for p in range(2)], axis=1)


VMEM_SPEC = pl.BlockSpec(memory_space=pltpu.VMEM)
ANY_SPEC = pl.BlockSpec(memory_space=pltpu.HBM)
SMEM_SPEC = pl.BlockSpec(memory_space=pltpu.SMEM)


def run(body, name, places, outs, scratch, operands, flops=0, room=44, out_specs=None):
    specs = [SMEM_SPEC] + [VMEM_SPEC if p == "v" else ANY_SPEC for p in places]
    moved = sum(o.size * o.dtype.itemsize for o in list(operands[1:]) + list(outs))
    return pl.pallas_call(
        body,
        name=name,
        in_specs=specs,
        out_specs=out_specs or [VMEM_SPEC] * len(outs),
        out_shape=outs,
        scratch_shapes=scratch,
        compiler_params=pltpu.CompilerParams(vmem_limit_bytes=room << 20),
        cost_estimate=pl.CostEstimate(
            flops=flops, bytes_accessed=min(moved, 16 << 20), transcendentals=0
        ),
    )(*operands)


def shape(dims, dtype):
    return jax.ShapeDtypeStruct(dims, dtype)


def fetch_ffn_adapters(fetch, where, which, column, up_ff, down_ff, p_in, q_in, p_out):
    found = []
    for number in range(4):
        side, core = number // 2, number % 2
        start = (2 * where[0] + (where[1] ^ core)) * (2 * column) + (where[2] ^ side) * column
        start = pl.multiple_of(start, column)
        place = pl.ds(number * column, column)
        found.append(fetch(up_ff.at[which, :, pl.ds(start, column)], q_in.at[:, place]))
        found.append(fetch(down_ff.at[which, pl.ds(start, column), :], p_out.at[place, :]))
    return found


def ffn_body(which, down_at, up_at, column, where, own, following, *refs):
    ins, outs, ups = refs[:4], refs[4:8], refs[8:12]
    down, down_ff, up, up_ff = ups
    part, send, pre_out, t_in_out, t_out_out = refs[12:17]
    rows, w_in, w_out, p_in, q_in, p_out, q_out, pre, active, sems = refs[17:]
    fetch = Fetches(sems)
    count = own.shape[0]
    small = [fetch(down.at[down_at], p_in), fetch(up.at[up_at], q_out)]
    small += fetch_ffn_adapters(fetch, where, which, column, up_ff, down_ff, p_in, q_in, p_out)
    first = [
        fetch(r.at[:, pl.ds(0, column)], w_in.at[:, pl.ds(n * column, column)])
        for n, r in enumerate(ins)
    ]
    second = [
        fetch(r.at[:, pl.ds(r.shape[1] - column, column)], w_out.at[:, pl.ds(n * column, column)])
        for n, r in enumerate(outs)
    ]
    mask = mask_row(where[3])
    rows[:count] = own[...]
    rows[count:] = following[...]
    wait_all(small)
    t_in = (nn(rows[...], p_in[...]) * mask).astype(BF)
    t_in_out[...] = t_in
    t_out = jnp.zeros(t_in.shape, F32)
    saved = []
    for n in range(4):
        span = slice(n * column, (n + 1) * column)
        first[n].wait()
        value = nn(rows[...], w_in[:, span]) + nn(t_in, q_in[:, span])
        pre[n] = value
        saved.append(fetch(pre.at[n], pre_out.at[n]))
        act = (value * jax.nn.sigmoid(value)).astype(BF)
        active[:, span] = act
        t_out = t_out + nn(act, p_out[span, :])
    t_out = (t_out * mask).astype(BF)
    t_out_out[...] = t_out
    wait_all(second)
    width = w_out.shape[0] // 2
    for n in range(2):
        span = slice(n * width, (n + 1) * width)
        total = nt(active[...], w_out[span, :]) + nn(t_out, q_out[:, span])
        part[:, span] = total[:count]
        send[:, span] = total[count:].astype(BF)
    wait_all(saved)


def ffn(which, down_at, up_at, where, own, following, w_in, w_out, adapters):
    count, width = own.shape
    column = adapters[3].shape[2] // 8
    hidden = 4 * column
    ranks = NADAPT * RANK

    def body(*refs):
        ffn_body(which, down_at, up_at, column, *refs)

    return run(
        body,
        "hidden_forward",
        "vv" + "a" * 12,
        [
            shape((count, width), F32),
            shape((count, width), BF),
            shape((4, 2 * count, column), F32),
            shape((2 * count, ranks), BF),
            shape((2 * count, ranks), BF),
        ],
        [
            pltpu.VMEM((2 * count, width), BF),
            pltpu.VMEM((width, hidden), BF),
            pltpu.VMEM((width, hidden), BF),
            pltpu.VMEM((width, ranks), BF),
            pltpu.VMEM((ranks, hidden), BF),
            pltpu.VMEM((hidden, ranks), BF),
            pltpu.VMEM((ranks, width), BF),
            pltpu.VMEM((4, 2 * count, column), F32),
            pltpu.VMEM((2 * count, hidden), BF),
            pltpu.SemaphoreType.DMA((22,)),
        ],
        [where, own, following, *w_in, *w_out, *adapters],
        flops=8 * count * width * hidden,
        out_specs=[VMEM_SPEC, VMEM_SPEC, ANY_SPEC, VMEM_SPEC, VMEM_SPEC],
    )


def ffn_back_body(which, down_at, up_at, column, where, own, following, u_own, u_next, t_in, t_out, *refs):
    pre_in = refs[0]
    ins, outs, ups = refs[1:5], refs[5:9], refs[9:13]
    down, down_ff, up, up_ff = ups
    part, send, grads = refs[13:16]
    full, rows, w_in, w_out, p_in, q_in, p_out, q_out, pre, active, slope, sems = refs[16:]
    fetch = Fetches(sems)
    count = own.shape[0]
    small = [fetch(down.at[down_at], p_in), fetch(up.at[up_at], q_out)]
    small += fetch_ffn_adapters(fetch, where, which, column, up_ff, down_ff, p_in, q_in, p_out)
    second = []
    kept = []
    for n, r in enumerate(outs):
        source = r.at[:, pl.ds(r.shape[1] - column, column)]
        second.append(fetch(source, w_out.at[:, pl.ds(n * column, column)]))
        kept.append(fetch(pre_in.at[n], pre.at[n]))
    first = [
        fetch(r.at[:, pl.ds(0, column)], w_in.at[:, pl.ds(n * column, column)])
        for n, r in enumerate(ins)
    ]
    mask = mask_row(where[3])
    pick = chosen_rows(where[3])
    full[:count] = own[...]
    full[count:] = following[...]
    rows[:count] = u_own[...]
    rows[count:] = u_next[...]
    wait_all(small)
    r_out = (nt(full[...], q_out[...]) * mask).astype(BF)
    c_out = compact(pick, r_out)
    c_t_in = compact(pick, t_in[...])
    r_in = jnp.zeros(r_out.shape, F32)
    for n in range(4):
        span = slice(n * column, (n + 1) * column)
        second[n].wait()
        kept[n].wait()
        grad = nn(full[...], w_out[:, span]) + nt(r_out, p_out[span, :])
        value = pre[n]
        sigma = jax.nn.sigmoid(value)
        act = (value * sigma).astype(BF)
        grad = (grad * swish_slope(value, sigma)).astype(BF)
        slope[:, span] = grad
        r_in = r_in + nt(grad, q_in[:, span])
        side, core = n // 2, n % 2
        near = (where[1] ^ core) ^ where[2]
        far = where[2] ^ side
        both = jnp.concatenate([nn(c_out, act), nn(c_t_in, grad)], axis=0)
        for piece in range(column // LANES):
            grads[near, 4 + far * (column // LANES) + piece] = both[
                :, piece * LANES : (piece + 1) * LANES
            ]
    r_in = (r_in * mask).astype(BF)
    wait_all(first)
    width = w_in.shape[0] // 2
    for n in range(2):
        span = slice(n * width, (n + 1) * width)
        total = nt(slope[...], w_in[span, :]) + nt(r_in, p_in[span, :])
        part[:, span] = total[:count]
        send[:, span] = total[count:].astype(BF)
    narrow = jnp.concatenate(
        [nn(compact(pick, r_in), rows[...]), nn(compact(pick, t_out[...]), full[...])], axis=0
    )
    for number in range(8):
        pair, side, half = number // 4, (number // 2) % 2, number % 2
        grads[side ^ where[2], 2 * (pair ^ where[0]) + half] = narrow[
            :, number * LANES : (number + 1) * LANES
        ]


def ffn_back(which, down_at, up_at, where, own, following, u_own, u_next, kept, w_in, w_out, adapters):
    pre, t_in, t_out = kept
    count, width = own.shape
    column = adapters[3].shape[2] // 8
    hidden = 4 * column
    ranks = NADAPT * RANK

    def body(*refs):
        ffn_back_body(which, down_at, up_at, column, *refs)

    return run(
        body,
        "hidden_backward",
        "vvvvvv" + "a" * 13,
        [
            shape((count, width), F32),
            shape((count, width), BF),
            shape((2, 4 + 2 * column // LANES, 2 * RANK, LANES), F32),
        ],
        [
            pltpu.VMEM((2 * count, width), BF),
            pltpu.VMEM((2 * count, width), BF),
            pltpu.VMEM((width, hidden), BF),
            pltpu.VMEM((width, hidden), BF),
            pltpu.VMEM((width, ranks), BF),
            pltpu.VMEM((ranks, hidden), BF),
            pltpu.VMEM((hidden, ranks), BF),
            pltpu.VMEM((ranks, width), BF),
            pltpu.VMEM((4, 2 * count, column), F32),
            pltpu.VMEM((2 * count, hidden), BF),
            pltpu.VMEM((2 * count, hidden), BF),
            pltpu.SemaphoreType.DMA((22,)),
        ],
        [where, own, following, u_own, u_next, t_in, t_out, pre, *w_in, *w_out, *adapters],
        flops=8 * count * width * hidden,
    )


def fetch_heads(fetch, where, pieces, up, wide):
    width = pieces[0].shape[0]
    three = 3 * LANES
    found = []
    for number, piece in enumerate(pieces):
        slot, core = number // 2, number % 2
        found.append(
            fetch(
                piece.at[:, pl.ds(0, three)],
                wide.at[slot, pl.ds(0, width), pl.ds(core * three, three)],
            )
        )
        start = pl.multiple_of(block_of(where, number) * LANES, LANES)
        for kind in range(3):
            found.append(
                fetch(
                    up.at[kind, :, pl.ds(start, LANES)],
                    wide.at[
                        slot,
                        pl.ds(width + kind * LANES, LANES),
                        pl.ds(core * three + kind * LANES, LANES),
                    ],
                )
            )
    return found


def clear_heads(wide, width):
    for kind in range(3):
        span = slice(width + kind * LANES, width + (kind + 1) * LANES)
        for core in range(2):
            for other in range(3):
                if other != kind:
                    at = (core * 3 + other) * LANES
                    for slot in range(4):
                        wide[slot, span, at : at + LANES] = jnp.zeros((LANES, LANES), BF)


def heads_body(where, resid, part, other, *refs):
    pieces = refs[:8]
    down, up = refs[8:10]
    first = refs[10]
    slots = refs[11:15]
    t_out = refs[15]
    wide, thin, sems = refs[16:]
    width = resid.shape[1]
    fetch = Fetches(sems)
    small = [
        fetch(down.at[1 + kind], thin.at[:, pl.ds(kind * LANES, LANES)]) for kind in range(3)
    ]
    large = fetch_heads(fetch, where, pieces, up, wide)
    clear_heads(wide, width)
    value = resid[...] + 0.5 * (part[...] + other[...].astype(F32))
    first[...] = value
    rows = normalize(value)[0].astype(BF)
    mask = jnp.concatenate([mask_row(where[3])] * 3, axis=1)
    wait_all(small)
    reduced = (nn(rows, thin[...]) * mask).astype(BF)
    t_out[...] = reduced
    both = jnp.concatenate([rows, reduced], axis=1)
    for slot in range(4):
        wait_all(large[slot * 8 : slot * 8 + 8])
        slots[slot][...] = nn(both, wide[slot]).astype(BF)


def heads_forward(where, resid, part, other, pieces, down, up):
    count, width = resid.shape
    three = 3 * LANES
    found = run(
        heads_body,
        "heads_forward",
        "vvv" + "a" * 10,
        [shape((count, width), F32)]
        + [shape((count, 2 * three), BF)] * 4
        + [shape((count, three), BF)],
        [
            pltpu.VMEM((4, width + three, 2 * three), BF),
            pltpu.VMEM((width, three), BF),
            pltpu.SemaphoreType.DMA((35,)),
        ],
        [where, resid, part, other, *pieces, down, up],
        flops=2 * count * width * 3 * width,
    )
    return (found[0], found[1:5], found[5])


def heads_back_body(where, grad, first, t_in, g0, g1, g2, g3, partial, *refs):
    pieces = refs[:8]
    down, up = refs[8:10]
    result, half, grads = refs[10:13]
    wide, thin, sems = refs[13:]
    width = grad.shape[1]
    three = 3 * LANES
    fetch = Fetches(sems)
    small = [
        fetch(down.at[1 + kind], thin.at[:, pl.ds(kind * LANES, LANES)]) for kind in range(3)
    ]
    large = fetch_heads(fetch, where, pieces, up, wide)
    clear_heads(wide, width)
    normed, scale = normalize(first[...])
    rows = normed.astype(BF)
    pick = chosen_rows(where[3])
    mask = jnp.concatenate([mask_row(where[3])] * 3, axis=1)
    ranks = [compact(pick, t_in[:, k * LANES : (k + 1) * LANES]) for k in range(3)]
    total = None
    for slot, g in enumerate((g0, g1, g2, g3)):
        wait_all(large[slot * 8 : slot * 8 + 8])
        term = nt(g[...], wide[slot])
        total = term if total is None else total + term
        for core in range(2):
            for kind in range(3):
                at = core * three + kind * LANES
                store_relative(
                    where, grads, (4 + kind) * RANK, nn(ranks[kind], g[:, at : at + LANES]),
                    2 * slot + core,
                )
    reduced = (total[:, width:] * mask).astype(BF)
    wait_all(small)
    total = total[:, :width] + nt(reduced, thin[...])
    value = grad[...] + normalize_back(total, normed, scale)
    result[...] = value
    half[...] = (0.5 * value).astype(BF)
    for kind in range(3):
        found = nn(compact(pick, reduced[:, kind * LANES : (kind + 1) * LANES]), rows)
        store_absolute(where, grads, kind * RANK, found)
    for side in range(2):
        for pair in range(2):
            for piece in range(2):
                grads[side, pair, piece, 3 * RANK : 4 * RANK, :] = partial[
                    side, pair, piece, :RANK, :
                ]
                grads[side, pair, piece, 7 * RANK :, :] = partial[side, pair, piece, RANK:, :]


def heads_back(where, grad, first, t_in, slots, partial, pieces, down, up):
    count, width = grad.shape
    three = 3 * LANES
    return run(
        heads_back_body,
        "heads_backward",
        "v" * 8 + "a" * 10,
        [
            shape((count, width), F32),
            shape((count, width), BF),
            shape((2, 2, 2, 8 * RANK, LANES), F32),
        ],
        [
            pltpu.VMEM((4, width + three, 2 * three), BF),
            pltpu.VMEM((width, three), BF),
            pltpu.SemaphoreType.DMA((35,)),
        ],
        [where, grad, first, t_in, *slots, partial, *pieces, down, up],
        flops=2 * count * width * 3 * width,
    )


def fetch_piece_columns(fetch, pieces, at, target):
    found = []
    for number, piece in enumerate(pieces):
        found.append(
            fetch(piece.at[:, pl.ds(at, LANES)], target.at[:, pl.ds(number * LANES, LANES)])
        )
    return found


def pair_body(where, first, m0, m1, m2, m3, *refs):
    heads, convs = refs[:8], refs[8:16]
    down, up = refs[16:18]
    second, value_out, gate_out, edge, t_mix_out, t_pair_out = refs[18:24]
    w_mix, w_value, w_gate, p_mix, q_mix, p_pair, q_value, q_gate, sems = refs[24:]
    fetch = Fetches(sems)
    mixing = fetch_rows(fetch, where, down.at[6], p_mix) + [fetch(up.at[5], q_mix)]
    mixing += fetch_piece_columns(fetch, heads, 3 * LANES, w_mix)
    pairs = [fetch(down.at[4], p_pair)]
    pairs += fetch_columns(fetch, where, up.at[3], q_value)
    pairs += fetch_columns(fetch, where, up.at[4], q_gate)
    pairs += fetch_piece_columns(fetch, convs, 0, w_value)
    gates = fetch_piece_columns(fetch, convs, LANES, w_gate)
    mask = mask_row(where[3])
    mixed = jnp.concatenate([m0[...], m1[...], m2[...], m3[...]], axis=1)
    wait_all(mixing)
    t_mix = (nn(mixed, p_mix[...]) * mask).astype(BF)
    t_mix_out[...] = t_mix
    value = first[...] + nt(mixed, w_mix[...]) + nn(t_mix, q_mix[...])
    second[...] = value
    rows = normalize(value)[0].astype(BF)
    wait_all(pairs)
    t_pair = (nn(rows, p_pair[...]) * mask).astype(BF)
    t_pair_out[...] = t_pair
    value = nn(rows, w_value[...]) + nn(t_pair, q_value[...])
    value_out[...] = value
    wait_all(gates)
    gate = nn(rows, w_gate[...]) + nn(t_pair, q_gate[...])
    gate_out[...] = gate
    last = value.shape[0] - edge.shape[2]
    store_edge(edge, value[last:] * jax.nn.sigmoid(gate[last:]), where[0])


def pair_forward(where, first, mixed, heads, convs, down, up):
    count, width = first.shape
    ranks = NADAPT * RANK
    square = pltpu.VMEM((width, width), BF)
    return run(
        pair_body,
        "pair_forward",
        "v" * 5 + "a" * 18,
        [
            shape((count, width), F32),
            shape((count, width), F32),
            shape((count, width), F32),
            shape((2, 2, 32, width // 4), F32),
            shape((count, ranks), BF),
            shape((count, ranks), BF),
        ],
        [
            square,
            square,
            square,
            pltpu.VMEM((width, ranks), BF),
            pltpu.VMEM((ranks, width), BF),
            pltpu.VMEM((width, ranks), BF),
            pltpu.VMEM((ranks, width), BF),
            pltpu.VMEM((ranks, width), BF),
            pltpu.SemaphoreType.DMA((50,)),
        ],
        [where, first, *mixed, *heads, *convs, down, up],
        flops=6 * count * width * width,
    )


def tap_sums(padded, taps, kernel, count, starts):
    found = []
    for number in range(padded.shape[0]):
        span = slice(number * LANES, (number + 1) * LANES)
        total = None
        for tap in range(taps):
            term = kernel[tap : tap + 1, span] * padded[number, starts[tap] : starts[tap] + count, :]
            total = term if total is None else total + term
        found.append(total)
    return jnp.concatenate(found, axis=1)


def conv_body(taps, where, second, value, gate, edge, kernel, *refs):
    convs = refs[:8]
    down, up = refs[8:10]
    conv_out, third, rows_out, t_out = refs[10:14]
    w_out, p_out, q_out, padded, sems = refs[14:]
    fetch = Fetches(sems)
    small = fetch_rows(fetch, where, down.at[7], p_out) + [fetch(up.at[6], q_out)]
    small += fetch_piece_columns(fetch, convs, 2 * LANES, w_out)
    count = second.shape[0]
    early = edge.shape[2]
    before = read_edge(edge)
    gated = value[...] * jax.nn.sigmoid(gate[...])
    for number in range(padded.shape[0]):
        span = slice(number * LANES, (number + 1) * LANES)
        padded[number, :early, :] = before[:, span]
        padded[number, early:, :] = gated[:, span]
    conv = tap_sums(padded, taps, kernel, count, [early - taps + 1 + k for k in range(taps)])
    conv_out[...] = conv
    normed = normalize(conv)[0]
    active = (normed * jax.nn.sigmoid(normed)).astype(BF)
    mask = mask_row(where[3])
    wait_all(small)
    reduced = (nn(active, p_out[...]) * mask).astype(BF)
    t_out[...] = reduced
    result = second[...] + nt(active, w_out[...]) + nn(reduced, q_out[...])
    third[...] = result
    rows_out[...] = normalize(result)[0].astype(BF)


def conv_forward(taps, where, second, value, gate, edge, kernel, convs, down, up):
    count, width = second.shape
    ranks = NADAPT * RANK

    def body(*refs):
        conv_body(taps, *refs)

    return run(
        body,
        "conv_forward",
        "v" * 5 + "a" * 10,
        [
            shape((count, width), F32),
            shape((count, width), F32),
            shape((count, width), BF),
            shape((count, ranks), BF),
        ],
        [
            pltpu.VMEM((width, width), BF),
            pltpu.VMEM((width, ranks), BF),
            pltpu.VMEM((ranks, width), BF),
            pltpu.VMEM((width // LANES, count + 32, LANES), F32),
            pltpu.SemaphoreType.DMA((17,)),
        ],
        [where, second, value, gate, edge, kernel, *convs, down, up],
        flops=2 * count * width * width,
    )


def conv_back_body(taps, where, grad, part, other, third, conv, t_in, *refs):
    convs = refs[:8]
    down, up = refs[8:10]
    result, grad_conv, edge, grads = refs[10:14]
    w_out, p_out, q_out, sems = refs[14:]
    fetch = Fetches(sems)
    small = fetch_rows(fetch, where, down.at[7], p_out) + [fetch(up.at[6], q_out)]
    small += fetch_piece_columns(fetch, convs, 2 * LANES, w_out)
    normed, scale = normalize(third[...])
    value = grad[...] + normalize_back(part[...] + other[...].astype(F32), normed, scale)
    result[...] = value
    full = value.astype(BF)
    mask = mask_row(where[3])
    pick = chosen_rows(where[3])
    wait_all(small)
    reduced = (nt(full, q_out[...]) * mask).astype(BF)
    active_grad = nn(full, w_out[...]) + nt(reduced, p_out[...])
    normed, scale = normalize(conv[...])
    sigma = jax.nn.sigmoid(normed)
    active = (normed * sigma).astype(BF)
    inner = normalize_back(active_grad * swish_slope(normed, sigma), normed, scale)
    grad_conv[...] = inner
    store_edge(edge, inner[: edge.shape[2]], 1 - where[0])
    store_absolute(where, grads, 0, nn(compact(pick, t_in[...]), full))
    found = nn(compact(pick, reduced), active)
    for number in range(8):
        store_relative(where, grads, RANK, found[:, number * LANES : (number + 1) * LANES], number)


def conv_back(taps, where, grad, part, other, third, conv, t_in, convs, down, up):
    count, width = grad.shape
    ranks = NADAPT * RANK

    def body(*refs):
        conv_back_body(taps, *refs)

    return run(
        body,
        "conv_backward",
        "v" * 6 + "a" * 10,
        [
            shape((count, width), F32),
            shape((count, width), F32),
            shape((2, 2, 32, width // 4), F32),
            shape((2, 2, 2, 2 * RANK, LANES), F32),
        ],
        [
            pltpu.VMEM((width, width), BF),
            pltpu.VMEM((width, ranks), BF),
            pltpu.VMEM((ranks, width), BF),
            pltpu.SemaphoreType.DMA((17,)),
        ],
        [where, grad, part, other, third, conv, t_in, *convs, down, up],
        flops=2 * count * width * width,
    )


def pair_back_body(
    taps, where, grad, grad_conv, edge, value, gate, kernel, second, t_pair, t_mix,
    m0, m1, m2, m3, partial, *refs
):
    heads, convs = refs[:8], refs[8:16]
    down, up = refs[16:18]
    result = refs[18]
    slots = refs[19:23]
    grads, mix_grads = refs[23:25]
    w_mix, w_value, w_gate, p_mix, q_mix, p_pair, q_value, q_gate, padded, sems = refs[25:]
    fetch = Fetches(sems)
    pairs = [fetch(down.at[4], p_pair)]
    pairs += fetch_columns(fetch, where, up.at[3], q_value)
    pairs += fetch_columns(fetch, where, up.at[4], q_gate)
    pairs += fetch_piece_columns(fetch, convs, 0, w_value)
    pairs += fetch_piece_columns(fetch, convs, LANES, w_gate)
    mixing = fetch_rows(fetch, where, down.at[6], p_mix) + [fetch(up.at[5], q_mix)]
    mixing += fetch_piece_columns(fetch, heads, 3 * LANES, w_mix)
    count = grad.shape[0]
    after = read_edge(edge)
    inner = grad_conv[...]
    for number in range(padded.shape[0]):
        span = slice(number * LANES, (number + 1) * LANES)
        padded[number, :count, :] = inner[:, span]
        padded[number, count:, :] = after[:, span]
    gated = tap_sums(padded, taps, kernel, count, [taps - 1 - k for k in range(taps)])
    sigma = jax.nn.sigmoid(gate[...])
    half = gated * sigma
    g_value = half.astype(BF)
    g_gate = (half * value[...] * (1.0 - sigma)).astype(BF)
    mask = mask_row(where[3])
    pick = chosen_rows(where[3])
    normed, scale = normalize(second[...])
    rows = normed.astype(BF)
    wait_all(pairs)
    reduced = ((nt(g_value, q_value[...]) + nt(g_gate, q_gate[...])) * mask).astype(BF)
    total = nt(g_value, w_value[...]) + nt(g_gate, w_gate[...]) + nt(reduced, p_pair[...])
    value_now = grad[...] + normalize_back(total, normed, scale)
    result[...] = value_now
    store_absolute(where, grads, 0, nn(compact(pick, reduced), rows))
    rank = compact(pick, t_pair[...])
    up_value = nn(rank, g_value)
    up_gate = nn(rank, g_gate)
    for number in range(8):
        span = slice(number * LANES, (number + 1) * LANES)
        store_relative(where, grads, 3 * RANK, up_value[:, span], number)
        store_relative(where, grads, 4 * RANK, up_gate[:, span], number)
    for side in range(2):
        for pair in range(2):
            for piece in range(2):
                grads[side, pair, piece, RANK : 3 * RANK, :] = partial[side, pair, piece]
    full = value_now.astype(BF)
    wait_all(mixing)
    reduced = (nt(full, q_mix[...]) * mask).astype(BF)
    mixed_grad = (nn(full, w_mix[...]) + nt(reduced, p_mix[...])).astype(BF)
    width = mixed_grad.shape[1] // 4
    for slot in range(4):
        slots[slot][...] = mixed_grad[:, slot * width : (slot + 1) * width]
    store_absolute(where, mix_grads, 0, nn(compact(pick, t_mix[...]), full))
    mixed = jnp.concatenate([m0[...], m1[...], m2[...], m3[...]], axis=1)
    found = nn(compact(pick, reduced), mixed)
    for number in range(8):
        span = slice(number * LANES, (number + 1) * LANES)
        store_relative(where, mix_grads, RANK, found[:, span], number)


def pair_back(
    taps, where, grad, grad_conv, edge, value, gate, kernel, second, t_pair, t_mix, mixed,
    partial, heads, convs, down, up
):
    count, width = grad.shape
    ranks = NADAPT * RANK
    square = pltpu.VMEM((width, width), BF)

    def body(*refs):
        pair_back_body(taps, *refs)

    found = run(
        body,
        "pair_backward",
        "v" * 14 + "a" * 18,
        [shape((count, width), F32)]
        + [shape((count, width // 4), BF)] * 4
        + [
            shape((2, 2, 2, 5 * RANK, LANES), F32),
            shape((2, 2, 2, 2 * RANK, LANES), F32),
        ],
        [
            square,
            square,
            square,
            pltpu.VMEM((width, ranks), BF),
            pltpu.VMEM((ranks, width), BF),
            pltpu.VMEM((width, ranks), BF),
            pltpu.VMEM((ranks, width), BF),
            pltpu.VMEM((ranks, width), BF),
            pltpu.VMEM((width // LANES, count + 32, LANES), F32),
            pltpu.SemaphoreType.DMA((50,)),
        ],
        [
            where, grad, grad_conv, edge, value, gate, kernel, second, t_pair, t_mix, *mixed,
            partial, *heads, *convs, down, up,
        ],
        flops=6 * count * width * width,
        room=52,
    )
    return (found[0], found[1:5], found[5], found[6])


def start_body(where, own, following, own_out, next_out):
    own_out[...] = normalize(own[...].astype(F32))[0].astype(BF)
    next_out[...] = normalize(following[...].astype(F32))[0].astype(BF)


def start_rows(where, own, following):
    count, width = own.shape
    return run(
        start_body, "start_rows", "vv", [shape((count, width), BF)] * 2, [], [where, own, following]
    )


def turn_body(where, third, part, other, cotangent, output, grad, half):
    fourth = third[...] + 0.5 * (part[...] + other[...].astype(F32))
    normed, scale = normalize(fourth)
    output[...] = normed.astype(BF)
    value = normalize_back(cotangent[...].astype(F32), normed, scale)
    grad[...] = value
    half[...] = (0.5 * value).astype(BF)


def turn(where, third, part, other, cotangent):
    count, width = third.shape
    return run(
        turn_body,
        "turn",
        "vvvv",
        [shape((count, width), BF), shape((count, width), F32), shape((count, width), BF)],
        [],
        [where, third, part, other, cotangent],
    )


def finish_body(where, grad, part, other, own, result):
    normed, scale = normalize(own[...].astype(F32))
    total = part[...] + other[...].astype(F32)
    result[...] = (grad[...] + normalize_back(total, normed, scale)).astype(BF)


def finish(where, grad, part, other, own):
    count, width = grad.shape
    return run(
        finish_body, "finish", "vvvv", [shape((count, width), BF)], [], [where, grad, part, other, own]
    )[0]


def expand_body(plan, spread, turned, found, *refs):
    kinds = sorted({kind for kind, _, _ in plan})
    outs = refs[-len(kinds) - len(plan) - 1 : -len(plan) - 1]
    held = refs[-len(plan) - 1 : -1]
    sems = refs[-1]
    copies = []
    for item, (kind, slot, starts) in enumerate(plan):
        column = len(starts) * LANES
        for pair in range(2):
            for side in range(2):
                parts = [
                    found[:, side, pair, :, row : row + RANK, :].reshape(-1, LANES)
                    for row in starts
                ]
                value = jnp.concatenate(parts, axis=1)
                start = (2 * pair + side) * column
                if kind % 2 == 0:
                    held[item][start : start + column, :] = tn(value, spread[...])
                else:
                    held[item][:, start : start + column] = nn(turned[...], value)
        copy = pltpu.make_async_copy(held[item], outs[kinds.index(kind)].at[slot], sems.at[item])
        copy.start()
        copies.append(copy)
    wait_all(copies)


def expand_near_body(plan, near_count, where, spread, turned, *refs):
    pieces = refs[: 2 * near_count]
    kinds = len({kind for _, kind, _, _ in plan})
    outs = refs[-kinds - len(plan) - 1 : -len(plan) - 1]
    held = refs[-len(plan) - 1 : -1]
    sems = refs[-1]
    copies = []
    for item, (wide, kind, slot, group) in enumerate(plan):
        rows = slice(group * RANK, (group + 1) * RANK)
        order = [0, 1] if not wide else list(range(2, pieces[0].shape[1]))
        column = len(order) * LANES
        for near in range(near_count):
            parts = [
                jnp.concatenate(
                    [pieces[2 * near + core][:, n, rows, :].reshape(-1, LANES) for core in range(2)],
                    axis=0,
                )
                for n in order
            ]
            value = jnp.concatenate(parts, axis=1)
            pair, side = where[0] ^ (near % 2), where[2] ^ (near // 2)
            place = pl.ds(pl.multiple_of((2 * pair + side) * column, column), column)
            if kind % 2 == 0:
                held[item][place, :] = tn(value, spread[...])
            else:
                held[item][:, place] = nn(turned[...], value)
        at = sorted({k for _, k, _, _ in plan}).index(kind)
        copy = pltpu.make_async_copy(held[item], outs[at].at[slot], sems.at[item])
        copy.start()
        copies.append(copy)
    wait_all(copies)


def expand_near(plan, where, spread, turned, pieces, outs):
    kinds = sorted({kind for _, kind, _, _ in plan})
    held = [outs[kind].shape[1:] for _, kind, _, _ in plan]
    passed = [outs[k] for k in kinds]
    start = 3 + len(pieces)

    def body(*refs):
        expand_near_body(plan, len(pieces) // 2, *refs)

    result = pl.pallas_call(
        body,
        name="expand_near",
        in_specs=[SMEM_SPEC] + [VMEM_SPEC] * (2 + len(pieces)) + [ANY_SPEC] * len(passed),
        out_specs=[ANY_SPEC] * len(kinds),
        out_shape=[shape(outs[k].shape, F32) for k in kinds],
        scratch_shapes=[pltpu.VMEM(h, F32) for h in held]
        + [pltpu.SemaphoreType.DMA((len(plan),))],
        input_output_aliases={start + n: n for n in range(len(kinds))},
        compiler_params=pltpu.CompilerParams(vmem_limit_bytes=44 << 20),
        cost_estimate=pl.CostEstimate(flops=0, bytes_accessed=8 << 20, transcendentals=0),
    )(where, spread, turned, *pieces, *passed)
    outs = list(outs)
    for n, k in enumerate(kinds):
        outs[k] = result[n]
    return outs


def rows_of(base, blocks, rows, group, first=0):
    return [base + n * rows + group * RANK for n in range(first, blocks)]


def expand(plan, spread, turned, found, outs):
    kinds = sorted({kind for kind, _, _ in plan})
    fresh = [isinstance(outs[k], jax.ShapeDtypeStruct) for k in kinds]
    held = [shape(outs[kind].shape[1:], F32) for kind, _, _ in plan]
    passed = [outs[k] for k, f in zip(kinds, fresh) if not f]
    aliases = {}
    for n, k in enumerate(kinds):
        if not fresh[n]:
            aliases[3 + len(aliases)] = n

    def body(*refs):
        expand_body(plan, *refs)

    result = pl.pallas_call(
        body,
        name="expand",
        in_specs=[VMEM_SPEC] * 3 + [ANY_SPEC] * len(passed),
        out_specs=[ANY_SPEC] * len(kinds),
        out_shape=[shape(outs[k].shape, F32) for k in kinds],
        scratch_shapes=[pltpu.VMEM(h.shape, F32) for h in held]
        + [pltpu.SemaphoreType.DMA((len(plan),))],
        input_output_aliases=aliases,
        compiler_params=pltpu.CompilerParams(vmem_limit_bytes=44 << 20),
        cost_estimate=pl.CostEstimate(flops=0, bytes_accessed=8 << 20, transcendentals=0),
    )(spread, turned, found, *passed)
    outs = list(outs)
    for n, k in enumerate(kinds):
        outs[k] = result[n]
    return outs


def join(own, other, bit, axis):
    return jnp.where(
        bit == 0,
        jnp.concatenate([own, other], axis=axis),
        jnp.concatenate([other, own], axis=axis),
    )


def part_of(value, index, count, axis):
    size = value.shape[axis] // count
    return lax.dynamic_slice_in_dim(value, index * size, size, axis)


class Place:
    def __init__(self):
        self.side = lax.axis_index("ctx")
        index = lax.axis_index("tp")
        self.pair = index // 2
        self.core = index % 2
        self.block = 2 * self.side + self.pair


def sequence_rows(value, place):
    own = lax.dynamic_index_in_dim(value, place.core, 0, keepdims=False)
    other = lax.dynamic_index_in_dim(value, 1 - place.core, 0, keepdims=False)
    return join(own, by_core(other), place.core, 1)


def own_rows(value, place):
    half = sequence_rows(value, place)
    mine = part_of(half, place.pair, 2, 0)
    theirs = part_of(half, 1 - place.pair, 2, 0)
    return join(mine, by_pair(theirs), place.pair, 1)


def all_rows(value, place):
    half = sequence_rows(value, place)
    full = join(half, by_pair(half), place.pair, 1)
    return part_of(full, place.pair, 2, 0), part_of(full, 1 - place.pair, 2, 0)


def feature_parts(value, place):
    mine = part_of(value, place.pair, 2, 1)
    theirs = part_of(value, 1 - place.pair, 2, 1)
    half = join(mine, by_pair(theirs), place.pair, 0)
    kept = part_of(half, place.core, 2, 1)[None]
    given = part_of(half, 1 - place.core, 2, 1)[None]
    return join(kept, by_core(given), place.core, 0)


def side_half(weight, place):
    return part_of(weight, place.side, 2, weight.ndim - 1)


def gathered(weight):
    return lax.all_gather(weight, "shard", axis=0, tiled=True)


def hidden_pieces(base):
    over = by_side(base)
    return [base, by_core(base), over, by_core(over)]


def whole_pieces(base):
    over = by_side(base)
    found = []
    for near in (base, over):
        far = by_pair(near)
        found += [near, by_core(near), far, by_core(far)]
    return found


def after(value, other):
    return lax.optimization_barrier((value, other))[0]


def line_order():
    count = lax.axis_size("shard")
    index = jnp.arange(count)
    return index if count > 8 else jnp.mod(lax.axis_index("shard") - index, count)


def around_shard(value):
    count = lax.axis_size("shard")
    if count > 8:
        return lax.all_gather(value, "shard", axis=0, tiled=False)
    found = [value]
    for shift in range(1, count):
        route = [(n, (n + shift) % count) for n in range(count)]
        found.append(lax.ppermute(value, "shard", route))
    return jnp.stack(found, axis=0)


def everywhere(value):
    flat = value.astype(BF).reshape(-1, LANES)
    found = lax.all_gather(flat, ("shard", "ctx", "tp"), axis=0, tiled=True)
    return found.reshape((-1, 2, 2, 2) + flat.shape)


def exchanged(slots):
    return [slots[0], by_pair(slots[1]), by_side(slots[2]), across(slots[3])]


def on_device(
    inputs,
    adapter_id,
    cotangent,
    ffn1_in,
    ffn1_out,
    query_w,
    key_w,
    value_w,
    out_w,
    conv_in_w,
    conv_kernel,
    conv_out_w,
    ffn2_in,
    ffn2_out,
    distance_table,
    adapt_down,
    adapt_down_ff,
    adapt_up,
    adapt_up_ff,
):
    place = Place()
    mine = lax.dynamic_index_in_dim(adapter_id, place.core, 0, keepdims=False)
    where = jnp.stack([place.pair, place.core, place.side, mine]).astype(jnp.int32)
    block = place.block.astype(jnp.int32)[None]
    adapters = (adapt_down, adapt_down_ff, adapt_up, adapt_up_ff)

    taps = conv_kernel.shape[0]
    core_kernel = jnp.concatenate([conv_kernel, by_core(conv_kernel)], axis=1)
    kernel = jnp.stack([core_kernel, by_pair(core_kernel)], axis=1).reshape(taps, 4, 2, -1)
    kernel = join(kernel[:, :, :1], kernel[:, :, 1:], place.side, 2)
    kernel = kernel.transpose(0, 2, 1, 3).reshape(taps, -1).astype(F32)

    ids = lax.all_gather(adapter_id, "shard", axis=0, tiled=True)
    eye = jnp.eye(RANK, dtype=BF)

    def spread_of(order):
        chosen = (order[:, None] == jnp.arange(NADAPT, dtype=jnp.int32)[None, :]).astype(BF)
        return (chosen[:, None, :, None] * eye[None, :, None, :]).reshape(-1, NADAPT * RANK)

    index = line_order()
    picked = index[:, None] == jnp.arange(index.shape[0])[None, :]
    near_ids = jnp.sum(jnp.where(picked[:, :, None], ids.reshape(1, -1, 2), 0), axis=1)
    near_ids = join(near_ids[:, :1], near_ids[:, 1:], place.core, 1).T.reshape(-1)
    spread, spread_near = spread_of(ids), spread_of(near_ids)
    turned, turned_near = spread.T, spread_near.T
    text = wide_table(distance_table)

    turning = own_rows(cotangent, place)
    settled = (kernel, text, spread, spread_near, turned, turned_near, turning)
    (kernel, text, spread, spread_near, turned, turned_near, turning) = lax.optimization_barrier(
        settled
    )

    base_in = gathered(side_half(ffn1_in, place))
    own, following = all_rows(inputs, place)
    rows_own, rows_next = start_rows(where, own, following)
    base_out = gathered(after(side_half(ffn1_out, place), (base_in, rows_own, rows_next)))
    in_side, in_core = by_side(base_in), by_core(base_in)
    local = jnp.concatenate(
        [side_half(w, place) for w in (query_w, key_w, value_w, out_w)], axis=1
    )
    base_heads = gathered(after(local, (base_out, in_side, in_core, turning, spread, kernel)))
    out_side, out_core = by_side(base_out), by_core(base_out)
    w1_in = [base_in, in_core, in_side, by_core(in_side)]
    pair_local = side_half(conv_in_w, place)
    local = jnp.concatenate(
        [pair_local[:, 0], pair_local[:, 1], side_half(conv_out_w, place)], axis=1
    )
    step = local.shape[1]
    local = jnp.concatenate([local, jnp.zeros_like(local[:, : step // 3])], axis=1)
    base_convs = gathered(after(local, (base_heads, out_side, out_core, w1_in[3])))
    w1_out = [base_out, out_core, out_side, by_core(out_side)]
    heads_side, heads_pair = by_side(base_heads), by_pair(base_heads)
    heads_core = by_core(base_heads)
    local = jnp.concatenate([side_half(w, place) for w in (ffn2_in, ffn2_out)], axis=1)
    part, send, pre, t_in, t_out = ffn(
        0, 0, 7, where, rows_own, rows_next, w1_in, w1_out, adapters
    )
    kept_one = (rows_own, rows_next, (pre, t_in, t_out))
    base_two = gathered(after(local, (base_convs, heads_side, heads_pair, heads_core, send)))
    heads_far = by_side(heads_pair)
    heads = [base_heads, heads_core, heads_pair, by_core(heads_pair)]
    heads += [heads_side, by_core(heads_side), heads_far, by_core(heads_far)]
    base_convs = base_convs[:, :step]
    convs_pair = by_pair(after(base_convs, heads_pair))
    convs_side = by_side(after(base_convs, heads_far))

    first, slots, t_heads = heads_forward(
        where, own.astype(F32), part, by_pair(send), heads, adapt_down, adapt_up
    )
    slots = exchanged(slots)
    convs_far = by_pair(after(convs_side, tuple(slots)))
    two_side = by_side(after(base_two, tuple(slots)))
    mixed, logs = attend(block, slots, text)
    convs = [base_convs, convs_pair, convs_side, convs_far]
    convs = [v for piece in convs for v in (piece, by_core(after(piece, mixed)))]
    mixed = exchanged([mixed[n] for n in range(4)])
    second, value, gate, edge, t_mix, t_pair = pair_forward(
        where, first, mixed, heads, convs, adapt_down, adapt_up
    )
    w2 = [base_two, by_core(after(base_two, mixed[0])), two_side, by_core(after(two_side, edge))]
    edge = lax.ppermute(edge, ("ctx", "tp"), NEXT)
    conv, third, rows_own, t_conv = conv_forward(
        taps, where, second, value, gate, edge, kernel, convs, adapt_down, adapt_up
    )
    rows_next = by_pair(rows_own)
    part, send, pre, t_in, t_out = ffn(1, 5, 8, where, rows_own, rows_next, w2, w2, adapters)
    kept_two = (rows_own, rows_next, (pre, t_in, t_out))

    output, grad, half = turn(where, third, part, by_pair(send), turning)
    part, send, sums_two = ffn_back(
        1, 5, 8, where, half, by_pair(half), *kept_two, w2, w2, adapters
    )
    grad, grad_conv, edge, partial = conv_back(
        taps, where, grad, part, by_pair(send), third, conv, t_conv, convs, adapt_down, adapt_up
    )
    came = after(by_side(after(sums_two[1], send)), grad_conv)
    sums_two = sums_two[0] + came
    edge = lax.ppermute(edge, ("ctx", "tp"), BEFORE)
    grad, grad_slots, conv_sums, partial = pair_back(
        taps, where, grad, grad_conv, edge, value, gate, kernel, second, t_pair, t_mix, mixed,
        partial, heads, convs, adapt_down, adapt_up,
    )
    came = after(by_pair(sums_two[2:4]), grad)
    sums_two = jnp.concatenate([sums_two[:2] + came, sums_two[4:]], axis=0)
    grad_slots = exchanged(grad_slots)
    conv_sums = conv_sums[0] + by_side(conv_sums[1])
    conv_sums = conv_sums[0] + by_pair(after(conv_sums[1], grad_slots[1]))
    payload = jnp.concatenate(
        [sums_two.astype(BF).reshape(-1, LANES), conv_sums.astype(BF).reshape(-1, LANES)], axis=0
    )
    found = everywhere(payload)
    back = attend_back(after(block, payload), slots, grad_slots, text, logs)
    output = feature_parts(output, place)
    back = exchanged([back[n] for n in range(4)])
    grad, half, head_sums = heads_back(
        after(where, output), grad, first, t_heads, back, partial, heads, adapt_down, adapt_up
    )
    other_half = by_pair(half)
    head_sums = head_sums[0] + by_side(head_sums[1])
    head_sums = head_sums[0] + by_pair(head_sums[1])
    found_heads = everywhere(after(head_sums, other_half))
    part, send, sums_one = ffn_back(
        0, 0, 7, where, half, other_half, *kept_one, w1_in, w1_out, adapters
    )
    sums_one = sums_one[0] + by_side(sums_one[1].astype(BF)).astype(F32)
    sums_one = jnp.concatenate([sums_one[:2] + by_pair(sums_one[2:4]), sums_one[4:]], axis=0)
    line = around_shard(sums_one.astype(BF))
    pieces = [line, by_pair(line), by_side(line)]
    pieces.append(by_pair(pieces[2]))
    pieces = [v for piece in pieces for v in (piece, by_core(piece))]
    input_grad = finish(where, grad, part, by_pair(send), own)
    input_grad = feature_parts(input_grad, place).astype(F32)

    outs = [shape(v.shape, F32) for v in (adapt_down, adapt_up, adapt_down_ff, adapt_up_ff)]
    ffn_blocks, ffn_rows = sums_two.shape[:2]
    conv_blocks, conv_rows = conv_sums.shape[:2]
    base = ffn_blocks * ffn_rows
    plan = [(kind, slot, rows_of(0, 2, ffn_rows, g)) for kind, slot, g in ((0, 5, 0), (1, 8, 1))]
    plan += [
        (kind, 1, rows_of(0, ffn_blocks, ffn_rows, g, 2)) for kind, g in ((2, 0), (3, 1))
    ]
    plan += [
        (kind, slot, rows_of(base, conv_blocks, conv_rows, g))
        for kind, slot, g in ((0, 4, 0), (1, 6, 1), (0, 7, 2), (1, 3, 3), (1, 4, 4))
    ]
    outs = expand(plan, spread, turned, after(found, send), outs)
    head_blocks, head_rows = head_sums.shape[:2]
    places = ((0, 1), (0, 2), (0, 3), (1, 5), (1, 0), (1, 1), (1, 2), (0, 6))
    plan = [
        (kind, slot, rows_of(0, head_blocks, head_rows, g))
        for g, (kind, slot) in enumerate(places)
    ]
    outs = expand(plan, spread, turned, found_heads, outs)
    outs = expand_near(
        [(False, 0, 0, 0), (False, 1, 7, 1), (True, 2, 0, 0), (True, 3, 0, 1)],
        where, spread_near, turned_near, pieces, outs,
    )
    return (output, input_grad, outs[0], outs[2], outs[1], outs[3])


def solution(mesh):
    placed = (
        P("shard", "ctx", "tp"),
        P("shard"),
        P("shard", "ctx", "tp"),
        P("shard", "tp"),
        P("shard", "tp"),
        P("shard", "tp"),
        P("shard", "tp"),
        P("shard", "tp"),
        P("shard", "tp"),
        P("shard", None, "tp"),
        P(None, "tp"),
        P("shard", "tp"),
        P("shard", "tp"),
        P("shard", "tp"),
        P(),
        P(),
        P(),
        P(),
        P(),
    )
    return jax.shard_map(
        on_device,
        mesh=mesh,
        in_specs=placed,
        out_specs=(P("shard", "ctx", "tp"), P("shard", "ctx", "tp"), P(), P(), P(), P()),
        check_vma=False,
    )
```

time: 1940 us -> 573 us (0.30)
  waiting for transfers between devices: 1020 us -> 203 us
  local copies, waits for them, and re-layouts: 407 us -> 55.4 us
  matrix products: 242 us -> 0.27 us
  Pallas kernels: 0 us -> 152 us
  blocking collectives: 143 us -> 7.87 us
  starting transfers between devices: 6.72 us -> 115 us
  other arithmetic: 88.6 us -> 12.8 us
    reduce_scatter x10 -> x0, waiting for transfers between devices: 379 us -> none  [the longest x8 329 us: own_share(): lax.psum_scatter(partial_value.reshape(shape[0], shape[1], -1), 'tp', sca...]
    all_gather x15 -> x7, waiting for transfers between devices: 349 us -> 10.3 us  [the longest x5 10.2 us: gathered(): return lax.all_gather(weight, 'shard', axis=0, tiled=True)]
    psum x1 -> x0, waiting for transfers between devices: 283 us -> none  [on_device(): lax.psum((full_down, spread(hidden_down, 1, tp_count), full_up, spread(hi...]
    dot_general x106 -> x1, matrix products: 242 us -> 0.27 us  [wide_table(): rows = jnp.dot(pick, table, preferred_element_type=F32).astype(BF)]
    ppermute x2 -> x72, waiting for transfers between devices: 3.54 us -> 193 us  [the longest x25 98.2 us: by_pair(): return lax.ppermute(value, 'tp', PAIR)]
    while x36 -> x0, local copies, waits for them, and re-layouts: 185 us -> none
    pallas_call x0 -> x18, Pallas kernels: none -> 152 us  [the longest x13 93.4 us: run(): pl.pallas_call(body, name=name, in_specs=specs, out_specs=out_specs or [V...]
    reshape x9 -> x1, local copies, waits for them, and re-layouts: 114 us -> 0.05 us  [on_device(): jnp.stack([core_kernel, by_pair(core_kernel)], axis=1)]
  transfers between devices with their start and end apart: 28 -> 79, of which waited for: 25 -> 39; matrix products, arithmetic and copies ran while one was open for 5% -> 5% of each run, Pallas kernels for 0% -> 22%
where the time goes in v1:
time: 573 us; the launch traced here: 563 us
  waiting for transfers between devices  203 us (35%)
  Pallas kernels  152 us (27%)
  starting transfers between devices  115 us (20%)
  local copies, waits for them, and re-layouts  55.4 us (10%)
  between operations  16.7 us (3%)
  other arithmetic  12.8 us (2%)
  blocking collectives  7.87 us (1%)
    ppermute x25, waiting for transfers between devices, by_pair(): return lax.ppermute(value, 'tp', PAIR)  98.2 us
    pallas_call x13, Pallas kernels, run(): pl.pallas_call(body, name=name, in_specs=specs, out_specs=out_specs or [V...  93.4 us
    ppermute x15, waiting for transfers between devices, by_side(): return lax.ppermute(value, 'ctx', SIDE)  72.7 us
    ppermute x23, starting transfers between devices, by_core(): return lax.ppermute(value, 'tp', CORE)  56.2 us
    unnamed x216, local copies, waits for them, and re-layouts  40.1 us
    pallas_call x1, Pallas kernels, attend_back(): pl.pallas_call(bwd_kernel, grid_spec=pltpu.PrefetchScalarGridSpec(num_sca...  33.3 us
    ppermute x25, starting transfers between devices, by_pair(): return lax.ppermute(value, 'tp', PAIR)  31 us
    ppermute x15, starting transfers between devices, by_side(): return lax.ppermute(value, 'ctx', SIDE)  17 us
  transfers between devices with their start and end apart: 79, of which 39 were waited for; matrix products, arithmetic and copies ran while one was open for 5% of the time, Pallas kernels for 22%

profile of v1, /device:TPU:1, one launch (start us, length us, event | category | flops | bytes accessed | tf_op | source)
XLA Modules:
  0.0 563.1 jit_solution(6463897386930349491)
XLA Ops:
  12.3 7.9 %all-reduce = s32[8]{0:T(128)S(1)} all-reduce(s32[8]{0:T(128)S(1)} %dynamic-update-slice), channel_id=1, replica_groups=mesh['shard'=4,'ctx'=2,'tp'=4] {'shard'}, use_global_device_ids=true, to_apply=%add | all-reduce | flops 8 | bytes 64
  25.3 9.2 %collective-permute-done.1 = bf16[512,512]{1,0:T(8,128)(2,1)S(1)} collective-permute-done((bf16[512,512]{1,0:T(8,128)(2,1)S(1)}, bf16[512,512]{1,0:T(8,128)(2,1)S(1)}, u32[]{:S(2)}, u32[]{:S(2)}) %collective-permute-start.1) | collective-permute-done | bytes 524320 | tf_op jit(solution)/shard_map/ppermute | solution.py:37
  48.1 7.1 %collective-permute-done.12 = bf16[256,512]{1,0:T(8,128)(2,1)S(1)} collective-permute-done((bf16[256,512]{1,0:T(8,128)(2,1)S(1)}, bf16[256,512]{1,0:T(8,128)(2,1)S(1)}, u32[]{:S(2)}, u32[]{:S(2)}) %collective-permute-start.12) | collective-permute-done | bytes 262176 | tf_op jit(solution)/shard_map/ppermute | solution.py:37
  56.1 12.5 %collective-permute-done.3.refs_5_.refs_10_ = bf16[1024,512]{1,0:T(8,128)(2,1)} collective-permute-done((bf16[1024,512]{1,0:T(8,128)(2,1)}, bf16[1024,512]{1,0:T(8,128)(2,1)}, u32[]{:S(2)}, u32[]{:S(2)}) %collective-permute-start.3) | collective-permute-done | bytes 1048608 | tf_op jit(solution)/shard_map/ppermute | solution.py:41
  75.0 20.5 %collective-permute-done.6.refs_9_.refs_14_ = bf16[1024,512]{1,0:T(8,128)(2,1)} collective-permute-done((bf16[1024,512]{1,0:T(8,128)(2,1)}, bf16[1024,512]{1,0:T(8,128)(2,1)}, u32[]{:S(2)}, u32[]{:S(2)}) %collective-permute-start.6) | collective-permute-done | bytes 1048608 | tf_op jit(solution)/shard_map/ppermute | solution.py:41
  95.5 4.0 all-gather.12.cloned.1.call-done.refs_0_.refs_15_
  108.3 11.2 %hidden_forward.2 = (f32[256,1024]{1,0:T(8,128)S(1)}, bf16[256,1024]{1,0:T(8,128)(2,1)S(1)}, f32[4,512,512]{2,1,0:T(8,128)}, bf16[512,128]{1,0:T(8,128)(2,1)S(1)}, bf16[512,128]{1,0:T(8,128)(2,1)S(1)}) custom-call(s32[4]{0:T(128)S(1)} %pad_add_fusion.where.refs_0_, bf16[256,1024]{1,0:T(8,128)(2,1)S(1)} %get-tuple-element.98.refs_1_.refs_3_, ...), custom_call_target="tpu_custom_call" | custom-call | flops 4294967296 | bytes 16777216 | tf_op jit(solution)/shard_map/hidden_forward/pallas_call | solution.py:320
  122.0 3.1 collective-permute-done.14.refs_2_.refs_17_
  126.0 2.9 all-gather.14.cloned.1.call-done
  131.3 21.9 %collective-permute-done.18.refs_6_.refs_21_ = bf16[1024,512]{1,0:T(8,128)(2,1)S(1)} collective-permute-done((bf16[1024,512]{1,0:T(8,128)(2,1)}, bf16[1024,512]{1,0:T(8,128)(2,1)S(1)}, u32[]{:S(2)}, u32[]{:S(2)}) %collective-permute-start.18) | collective-permute-done | bytes 1048608 | tf_op jit(solution)/shard_map/ppermute | solution.py:41
  158.5 10.1 %collective-permute-done.8.other = bf16[256,1024]{1,0:T(8,128)(2,1)S(1)} collective-permute-done((bf16[256,1024]{1,0:T(8,128)(2,1)}, bf16[256,1024]{1,0:T(8,128)(2,1)S(1)}, u32[]{:S(2)}, u32[]{:S(2)}) %collective-permute-start.8) | collective-permute-done | bytes 524320 | tf_op jit(solution)/shard_map/ppermute | solution.py:37
  171.2 6.3 %heads_forward.1 = (f32[256,1024]{1,0:T(8,128)S(1)}, bf16[256,768]{1,0:T(8,128)(2,1)S(1)}, bf16[256,768]{1,0:T(8,128)(2,1)S(1)}, bf16[256,768]{1,0:T(8,128)(2,1)...) custom-call(s32[4]{0:T(128)S(1)} %pad_add_fusion.where.refs_0_, f32[256,1024]{1,0:T(8,128)S(1)} %copy-done.18, ...), custom_call_target="tpu_custom_call" | custom-call | flops 1610612736 | bytes 16777216 | tf_op jit(solution)/shard_map/heads_forward/pallas_call | solution.py:320
  182.6 7.2 %collective-permute-done.20.s1 = bf16[256,768]{1,0:T(8,128)(2,1)S(1)} collective-permute-done((bf16[256,768]{1,0:T(8,128)(2,1)S(1)}, bf16[256,768]{1,0:T(8,128)(2,1)S(1)}, u32[]{:S(2)}, u32[]{:S(2)}) %collective-permute-start.20) | collective-permute-done | bytes 393248 | tf_op jit(solution)/shard_map/ppermute | solution.py:37
  191.5 7.7 %collective-permute-done.22.s3 = bf16[256,768]{1,0:T(8,128)(2,1)S(1)} collective-permute-done((bf16[256,768]{1,0:T(8,128)(2,1)S(1)}, bf16[256,768]{1,0:T(8,128)(2,1)S(1)}, u32[]{:S(2)}, u32[]{:S(2)}) %collective-permute-start.22) | collective-permute-done | bytes 393248 | tf_op jit(solution)/shard_map/ppermute | solution.py:45
  207.5 14.8 %attend.1 = (bf16[4,256,256]{2,1,0:T(8,128)(2,1)S(1)}, f32[4,1024,1]{2,1,0:T(8,128)S(1)}) custom-call(s32[1]{0:T(128)} %bitcast.14.b_ref, bf16[256,768]{1,0:T(8,128)(2,1)S(1)} %copy-done.81, bf16[256,768]{1,0:T(8,128)(2,1)S(1)} %copy-done.83, bf16[256,768]{1,0:T(8,128)(2,1)S(1)} %copy-done.85, bf16[256,768]{1,0:T(8,128)(2,1)S(1)} %copy-done.87, ...), custom_call_target="tpu_custom_call" | custom-call | flops 1073741824 | bytes 2097152 | tf_op jit(solution)/shard_map/attend/pallas_call | solution.py:112
  226.4 8.5 %collective-permute-done.31.refs_14_.refs_12_.refs_13_.refs_29_ = bf16[1024,384]{1,0:T(8,128)(2,1)} collective-permute-done((bf16[1024,384]{1,0:T(8,128)(2,1)}, bf16[1024,384]{1,0:T(8,128)(2,1)}, u32[]{:S(2)}, u32[]{:S(2)}) %collective-permute-start.31) | collective-permute-done | bytes 786464 | tf_op jit(solution)/shard_map/ppermute | solution.py:37
  234.9 4.6 collective-permute-start.26
  240.7 7.4 %collective-permute-done.24.m2.refs_12_ = bf16[256,256]{1,0:T(8,128)(2,1)S(1)} collective-permute-done((bf16[256,256]{1,0:T(8,128)(2,1)S(1)}, bf16[256,256]{1,0:T(8,128)(2,1)S(1)}, u32[]{:S(2)}, u32[]{:S(2)}) %collective-permute-start.24) | collective-permute-done | bytes 131104 | tf_op jit(solution)/shard_map/ppermute | solution.py:41
  248.1 4.3 collective-permute-start.30
  257.0 6.8 %pair_forward.1 = (f32[256,1024]{1,0:T(8,128)S(1)}, f32[256,1024]{1,0:T(8,128)S(1)}, f32[256,1024]{1,0:T(8,128)S(1)}, f32[2,2,32,256]{3,2,1,0:T(8,128)S(1)}, bf1...) custom-call(s32[4]{0:T(128)S(1)} %pad_add_fusion.where.refs_0_, f32[256,1024]{1,0:T(8,128)} %copy-done.16, ...), custom_call_target="tpu_custom_call" | custom-call | flops 1610612736 | bytes 16777216 | tf_op jit(solution)/shard_map/pair_forward/pallas_call | solution.py:320
  268.8 2.5 collective-permute-done.33.refs_4_
  271.3 6.8 %conv_forward.1 = (f32[256,1024]{1,0:T(8,128)S(1)}, f32[256,1024]{1,0:T(8,128)S(1)}, bf16[256,1024]{1,0:T(8,128)(2,1)S(1)}, bf16[256,128]{1,0:T(8,128)(2,1)S(1)}) custom-call(s32[4]{0:T(128)S(1)} %pad_add_fusion.where.refs_0_, f32[256,1024]{1,0:T(8,128)S(1)} %get-tuple-element.122.refs_1_.refs_7_, f32[256,1024]{1,0:T(8,128)} %copy-done.22, ...), custom_call_target="tpu_custom_call" | custom-call | flops 536870912 | bytes 16777216 | tf_op jit(solution)/shard_map/conv_forward/pallas_call | solution.py:320
  282.4 11.3 %collective-permute-done.34.refs_2_.refs_4_ = bf16[256,1024]{1,0:T(8,128)(2,1)S(1)} collective-permute-done((bf16[256,1024]{1,0:T(8,128)(2,1)S(1)}, bf16[256,1024]{1,0:T(8,128)(2,1)S(1)}, u32[]{:S(2)}, u32[]{:S(2)}) %collective-permute-start.34) | collective-permute-done | bytes 524320 | tf_op jit(solution)/shard_map/ppermute | solution.py:37
  293.7 11.1 %hidden_forward.3 = (f32[256,1024]{1,0:T(8,128)S(1)}, bf16[256,1024]{1,0:T(8,128)(2,1)S(1)}, f32[4,512,512]{2,1,0:T(8,128)}, bf16[512,128]{1,0:T(8,128)(2,1)S(1)}, bf16[512,128]{1,0:T(8,128)(2,1)S(1)}) custom-call(s32[4]{0:T(128)S(1)} %pad_add_fusion.where.refs_0_, bf16[256,1024]{1,0:T(8,128)(2,1)S(1)} %get-tuple-element.127.refs_1_.refs_3_, ...), custom_call_target="tpu_custom_call" | custom-call | flops 4294967296 | bytes 16777216 | tf_op jit(solution)/shard_map/hidden_forward/pallas_call | solution.py:320
  306.1 10.7 %collective-permute-done.38.other = bf16[256,1024]{1,0:T(8,128)(2,1)S(1)} collective-permute-done((bf16[256,1024]{1,0:T(8,128)(2,1)S(1)}, bf16[256,1024]{1,0:T(8,128)(2,1)S(1)}, u32[]{:S(2)}, u32[]{:S(2)}) %collective-permute-start.38) | collective-permute-done | bytes 524320 | tf_op jit(solution)/shard_map/ppermute | solution.py:37
  319.8 10.1 %collective-permute-done.41.refs_2_ = bf16[256,1024]{1,0:T(8,128)(2,1)S(1)} collective-permute-done((bf16[256,1024]{1,0:T(8,128)(2,1)S(1)}, bf16[256,1024]{1,0:T(8,128)(2,1)S(1)}, u32[]{:S(2)}, u32[]{:S(2)}) %collective-permute-start.41) | collective-permute-done | bytes 524320 | tf_op jit(solution)/shard_map/ppermute | solution.py:37
  329.9 12.2 %hidden_backward.2 = (f32[256,1024]{1,0:T(8,128)S(1)}, bf16[256,1024]{1,0:T(8,128)(2,1)S(1)}, f32[2,12,32,128]{3,2,1,0:T(8,128)S(1)}) custom-call(s32[4]{0:T(128)S(1)} %pad_add_fusion.where.refs_0_, bf16[256,1024]{1,0:T(8,128)(2,1)S(1)} %get-tuple-element.137.refs_1_, bf16[256,1024]{1,0:T(8,128)(2,1)S(1)} %collective-permute-done.41.refs_2_, ...), custom_call_target="tpu_custom_call" | custom-call | flops 4294967296 | bytes 16777216 | tf_op jit(solution)/shard_map/hidden_backward/pallas_call | solution.py:320
  343.6 2.8 collective-permute-start.44
  346.4 6.6 %collective-permute-done.42.refs_3_ = bf16[256,1024]{1,0:T(8,128)(2,1)S(1)} collective-permute-done((bf16[256,1024]{1,0:T(8,128)(2,1)S(1)}, bf16[256,1024]{1,0:T(8,128)(2,1)S(1)}, u32[]{:S(2)}, u32[]{:S(2)}) %collective-permute-start.42) | collective-permute-done | bytes 524320 | tf_op jit(solution)/shard_map/ppermute | solution.py:37
  353.2 5.1 conv_backward.1
  366.0 11.1 %pair_backward.1 = (f32[256,1024]{1,0:T(8,128)}, bf16[256,256]{1,0:T(8,128)(2,1)S(1)}, bf16[256,256]{1,0:T(8,128)(2,1)S(1)}, bf16[256,256]{1,0:T(8,128)(2,1)S(1)...) custom-call(s32[4]{0:T(128)S(1)} %pad_add_fusion.where.refs_0_, ...), custom_call_target="tpu_custom_call" | custom-call | flops 1610612736 | bytes 16777216 | tf_op jit(solution)/shard_map/pair_backward/pallas_call | solution.py:320
  380.9 2.7 collective-permute-done.46
  392.0 4.3 collective-permute-done.39
  397.3 33.3 %attend_back.1 = bf16[4,256,768]{2,1,0:T(8,128)(2,1)} custom-call(s32[1]{0:T(128)} %bitcast.14.b_ref, bf16[256,768]{1,0:T(8,128)(2,1)} %copy-done.80, bf16[256,768]{1,0:T(8,128)(2,1)} %copy-done.82, bf16[256,768]{1,0:T(8,128)(2,1)} %copy-done.84, bf16[256,768]{1,0:T(8,128)(2,1)} %copy-done.86, bf16[256,256]{1,0:T(8,128)(2,1)} %copy-done.88, ...), custom_call_target="tpu_custom_call" | custom-call | flops 2684354560 | bytes 3670016 | tf_op jit(solution)/shard_map/attend_back/pallas_call | solution.py:184
  435.1 10.7 %collective-permute-start.40 = (bf16[1,512,256]{2,1,0:T(8,128)(2,1)S(1)}, bf16[1,512,256]{2,1,0:T(8,128)(2,1)S(1)}, u32[]{:S(2)}, u32[]{:S(2)}) collective-permute-start(bf16[1,512,256]{2,1,0:T(8,128)(2,1)S(1)} %get-tuple-element.202), channel_id=1, source_target_pairs={{0,1},{1,0},{2,3},{3,2},{4,5},{5,4},{6,7},{7,6},{8,9},{9,8},{10,11... | collective-permute-start | bytes 786440 | tf_op jit(solution)/shard_map/ppermute | solution.py:33
  449.1 6.7 %heads_backward.1 = (f32[256,1024]{1,0:T(8,128)S(1)}, bf16[256,1024]{1,0:T(8,128)(2,1)S(1)}, f32[2,2,2,128,128]{4,3,2,1,0:T(8,128)S(1)}) custom-call(s32[4]{0:T(128)S(1)} %pad_add_fusion.where.refs_0_, f32[256,1024]{1,0:T(8,128)S(1)} %copy-done.45, f32[256,1024]{1,0:T(8,128)S(1)} %copy-done.17, bf16[256,384]{1,0:T(8,128)(2,1)S(1)} %copy-done.69, ...), custom_call_target="tpu_custom_call" | custom-call | flops 1610612736 | bytes 16777216 | tf_op jit(solution)/shard_map/heads_backward/pallas_call | solution.py:320
  463.0 2.7 collective-permute-start.71
  465.7 3.3 collective-permute-done.71
  474.9 12.2 %hidden_backward.3 = (f32[256,1024]{1,0:T(8,128)S(1)}, bf16[256,1024]{1,0:T(8,128)(2,1)S(1)}, f32[2,12,32,128]{3,2,1,0:T(8,128)S(1)}) custom-call(s32[4]{0:T(128)S(1)} %pad_add_fusion.where.refs_0_, bf16[256,1024]{1,0:T(8,128)(2,1)S(1)} %copy-done.62, bf16[256,1024]{1,0:T(8,128)(2,1)S(1)} %copy-done.64, bf16[256,1024]{1,0:T(8,128)(2,1)S(1)} %copy-done.39, ...), custom_call_target="tpu_custom_call" | custom-call | flops 4294967296 | bytes 16777216 | tf_op jit(solution)/shard_map/hidden_backward/pallas_call | solution.py:320
  487.9 2.7 collective-permute-done.58
  496.9 3.1 collective-permute-done.61
  509.2 2.7 collective-permute-done.56
  512.9 18.8 %collective-permute-start.57 = (bf16[1,512,256]{2,1,0:T(8,128)(2,1)}, bf16[1,512,256]{2,1,0:T(8,128)(2,1)}, u32[]{:S(2)}, u32[]{:S(2)}) collective-permute-start(bf16[1,512,256]{2,1,0:T(8,128)(2,1)} %get-tuple-element.198), channel_id=1, source_target_pairs={{0,1},{1,0},{2,3},{3,2},{4,5},{5,4},{6,7},{7,6},{8,9},{9,8},{10,11... | collective-permute-start | bytes 786440 | tf_op jit(solution)/shard_map/ppermute | solution.py:33
  532.2 3.5 collective-permute-start.65
  535.7 3.5 collective-permute-start.69
  543.6 4.3 expand.2
  549.5 2.6 expand.3
  552.2 3.6 expand_near.1
  (436 shorter events, 157.1 us)
Async XLA Ops:
  7.3 32.8 %all-gather.8.cloned.1.call-start = ((), (), s32[]{:S(2)}) async-start(), calls=%async_computation | async-start | bytes 1310720 | tf_op jit(solution)/shard_map/all_gather | solution.py:1228
  8.5 14.3 %collective-permute-start = (bf16[512,256]{1,0:T(8,128)(2,1)S(1)}, bf16[512,256]{1,0:T(8,128)(2,1)S(1)}, u32[]{:S(2)}, u32[]{:S(2)}) collective-permute-start(bf16[512,256]{1,0:T(8,128)(2,1)S(1)} %get-tuple-element.214), channel_id=1, source_target_pairs={{0,1},{1,0},{2,3},{3,2},{4,5},{5,4},{6,7},{7,6},{8,9},{9,8},{10,11... | collective-permute-start | bytes 786440 | tf_op jit(solution)/shard_map/ppermute | solution.py:33
  9.4 60.4 %all-gather.10.cloned.1.call-start = ((), (), s32[]{:S(2)}) async-start(), calls=%async_computation.1 | async-start | bytes 1310720 | tf_op jit(solution)/shard_map/all_gather | solution.py:1228
  9.5 31.0 %collective-permute-start.9 = (bf16[31,256]{1,0:T(8,128)(2,1)}, bf16[31,256]{1,0:T(8,128)(2,1)}, u32[]{:S(2)}, u32[]{:S(2)}) collective-permute-start(bf16[31,256]{1,0:T(8,128)(2,1)} %param.29), channel_id=1, source_target_pairs={{0,1},{1,0},{2,3},{3,2},{4,5},{5,4},{6,7},{7,6},{8,9},{9,8},{10,11... | collective-permute-start | bytes 47624 | tf_op jit(solution)/shard_map/ppermute | solution.py:33
  10.7 36.5 %collective-permute-start.11 = (bf16[512,256]{1,0:T(8,128)(2,1)}, bf16[512,256]{1,0:T(8,128)(2,1)S(1)}, u32[]{:S(2)}, u32[]{:S(2)}) collective-permute-start(bf16[512,256]{1,0:T(8,128)(2,1)} %get-tuple-element.212), channel_id=1, source_target_pairs={{0,1},{1,0},{2,3},{3,2},{4,5},{5,4},{6,7},{7,6},{8,9},{9,8},{10,11... | collective-permute-start | bytes 786440 | tf_op jit(solution)/shard_map/ppermute | solution.py:33
  40.1 59.3 %all-gather.12.cloned.1.call-start = ((), (), s32[]{:S(2)}) async-start(), calls=%async_computation.2 | async-start | bytes 1310720 | tf_op jit(solution)/shard_map/all_gather | solution.py:1228
  42.5 13.6 %collective-permute-start.2 = (bf16[1024,512]{1,0:T(8,128)(2,1)}, bf16[1024,512]{1,0:T(8,128)(2,1)S(1)}, u32[]{:S(2)}, u32[]{:S(2)}) collective-permute-start(bf16[1024,512]{1,0:T(8,128)(2,1)} %all-gather.8.cloned.1.call-done.refs_3_.refs_8_), channel_id=1, source_target_pairs={{0,1},{1,0},{2,3},{3,2},{4,5},{5,4},{6,7},{7,6},{8,9},{9,8},{10,11... | collective-permute-start | bytes 3145736 | tf_op jit(solution)/shard_map/ppermute | solution.py:33
  43.5 25.1 %collective-permute-start.3 = (bf16[1024,512]{1,0:T(8,128)(2,1)}, bf16[1024,512]{1,0:T(8,128)(2,1)}, u32[]{:S(2)}, u32[]{:S(2)}) collective-permute-start(bf16[1024,512]{1,0:T(8,128)(2,1)} %all-gather.8.cloned.1.call-done.refs_3_.refs_8_), channel_id=1, source_target_pairs={{0,4},{4,0},{1,5},{5,1},{2,6},{6,2},{3,7},{7,3},{8,12},{12,8},{9,1... | collective-permute-start | bytes 3145736 | tf_op jit(solution)/shard_map/ppermute | solution.py:41
  69.9 59.0 %all-gather.14.cloned.1.call-start = ((), (), s32[]{:S(2)}) async-start(), calls=%async_computation.3 | async-start | bytes 1310720 | tf_op jit(solution)/shard_map/all_gather | solution.py:1228
  70.9 24.6 %collective-permute-start.6 = (bf16[1024,512]{1,0:T(8,128)(2,1)}, bf16[1024,512]{1,0:T(8,128)(2,1)}, u32[]{:S(2)}, u32[]{:S(2)}) collective-permute-start(bf16[1024,512]{1,0:T(8,128)(2,1)} %all-gather.10.cloned.1.call-done.refs_7_.refs_12_), channel_id=1, source_target_pairs={{0,4},{4,0},{1,5},{5,1},{2,6},{6,2},{3,7},{7,3},{8,12},{12,8},{9,1... | collective-permute-start | bytes 3145736 | tf_op jit(solution)/shard_map/ppermute | solution.py:41
  99.5 100.5 %all-gather.16.cloned.1.call-start = ((), (), s32[]{:S(2)}) async-start(), calls=%async_computation.4 | async-start | bytes 2621440 | tf_op jit(solution)/shard_map/all_gather | solution.py:1228
  100.4 21.6 %collective-permute-start.13 = (bf16[1024,512]{1,0:T(8,128)(2,1)}, bf16[1024,512]{1,0:T(8,128)(2,1)S(1)}, u32[]{:S(2)}, u32[]{:S(2)}) collective-permute-start(bf16[1024,512]{1,0:T(8,128)(2,1)} %all-gather.12.cloned.1.call-done.refs_0_.refs_15_), channel_id=1, source_target_pairs={{0,1},{1,0},{2,3},{3,2},{4,5},{5,4},{6,7},{7,6},{8,9},{9,8},{10,11... | collective-permute-start | bytes 3145736 | tf_op jit(solution)/shard_map/ppermute | solution.py:33
  100.5 24.6 %collective-permute-start.14 = (bf16[1024,512]{1,0:T(8,128)(2,1)}, bf16[1024,512]{1,0:T(8,128)(2,1)}, u32[]{:S(2)}, u32[]{:S(2)}) collective-permute-start(bf16[1024,512]{1,0:T(8,128)(2,1)} %all-gather.12.cloned.1.call-done.refs_0_.refs_15_), channel_id=1, source_target_pairs={{0,2},{2,0},{1,3},{3,1},{4,6},{6,4},{5,7},{7,5},{8,10},{10,8},{9,1... | collective-permute-start | bytes 3145736 | tf_op jit(solution)/shard_map/ppermute | solution.py:37
  101.7 24.3 %collective-permute-start.16 = (bf16[1024,512]{1,0:T(8,128)(2,1)}, bf16[1024,512]{1,0:T(8,128)(2,1)}, u32[]{:S(2)}, u32[]{:S(2)}) collective-permute-start(bf16[1024,512]{1,0:T(8,128)(2,1)} %all-gather.12.cloned.1.call-done.refs_0_.refs_15_), channel_id=1, source_target_pairs={{0,4},{4,0},{1,5},{5,1},{2,6},{6,2},{3,7},{7,3},{8,12},{12,8},{9,1... | collective-permute-start | bytes 3145736 | tf_op jit(solution)/shard_map/ppermute | solution.py:41
  128.9 412.6 %all-gather.20.cloned.1.call-start = ((), (), s32[]{:S(2)}) async-start(), calls=%async_computation.6 | async-start | bytes 4055040 | tf_op jit(solution)/shard_map/all_gather | solution.py:1268
  129.0 24.2 %collective-permute-start.18 = (bf16[1024,512]{1,0:T(8,128)(2,1)}, bf16[1024,512]{1,0:T(8,128)(2,1)S(1)}, u32[]{:S(2)}, u32[]{:S(2)}) collective-permute-start(bf16[1024,512]{1,0:T(8,128)(2,1)} %collective-permute-done.14.refs_2_.refs_17_), channel_id=1, source_target_pairs={{0,4},{4,0},{1,5},{5,1},{2,6},{6,2},{3,7},{7,3},{8,12},{12,8},{9,1... | collective-permute-start | bytes 3145736 | tf_op jit(solution)/shard_map/ppermute | solution.py:41
  130.2 38.4 %collective-permute-start.15 = (bf16[1024,512]{1,0:T(8,128)(2,1)}, bf16[1024,512]{1,0:T(8,128)(2,1)S(1)}, u32[]{:S(2)}, u32[]{:S(2)}) collective-permute-start(bf16[1024,512]{1,0:T(8,128)(2,1)} %collective-permute-done.14.refs_2_.refs_17_), channel_id=1, source_target_pairs={{0,1},{1,0},{2,3},{3,2},{4,5},{5,4},{6,7},{7,6},{8,9},{9,8},{10,11... | collective-permute-start | bytes 3145736 | tf_op jit(solution)/shard_map/ppermute | solution.py:33
  131.3 37.3 %collective-permute-start.17 = (bf16[1024,512]{1,0:T(8,128)(2,1)}, bf16[1024,512]{1,0:T(8,128)(2,1)S(1)}, u32[]{:S(2)}, u32[]{:S(2)}) collective-permute-start(bf16[1024,512]{1,0:T(8,128)(2,1)} %collective-permute-done.16.refs_4_.refs_19_), channel_id=1, source_target_pairs={{0,1},{1,0},{2,3},{3,2},{4,5},{5,4},{6,7},{7,6},{8,9},{9,8},{10,11... | collective-permute-start | bytes 3145736 | tf_op jit(solution)/shard_map/ppermute | solution.py:33
  153.2 15.4 %collective-permute-start.19 = (bf16[1024,512]{1,0:T(8,128)(2,1)S(1)}, bf16[1024,512]{1,0:T(8,128)(2,1)S(1)}, u32[]{:S(2)}, u32[]{:S(2)}) collective-permute-start(bf16[1024,512]{1,0:T(8,128)(2,1)S(1)} %collective-permute-done.18.refs_6_.refs_21_), channel_id=1, source_target_pairs={{0,1},{1,0},{2,3},{3,2},{4,5},{5,4},{6,7},{7,6},{8,9},{9,8},{10,11... | collective-permute-start | bytes 3145736 | tf_op jit(solution)/shard_map/ppermute | solution.py:33
  154.8 13.8 %collective-permute-start.8 = (bf16[256,1024]{1,0:T(8,128)(2,1)}, bf16[256,1024]{1,0:T(8,128)(2,1)S(1)}, u32[]{:S(2)}, u32[]{:S(2)}) collective-permute-start(bf16[256,1024]{1,0:T(8,128)(2,1)} %copy-done.79), channel_id=1, source_target_pairs={{0,2},{2,0},{1,3},{3,1},{4,6},{6,4},{5,7},{7,5},{8,10},{10,8},{9,1... | collective-permute-start | bytes 1572872 | tf_op jit(solution)/shard_map/ppermute | solution.py:37
  157.2 45.0 %collective-permute-start.29 = (bf16[1024,384]{1,0:T(8,128)(2,1)S(1)}, bf16[1024,384]{1,0:T(8,128)(2,1)}, u32[]{:S(2)}, u32[]{:S(2)}) collective-permute-start(bf16[1024,384]{1,0:T(8,128)(2,1)S(1)} %slice.138.refs_8_.refs_6_.refs_7_.refs_23_), channel_id=1, source_target_pairs={{0,4},{4,0},{1,5},{5,1},{2,6},{6,2},{3,7},{7,3},{8,12},{12,8},{9,1... | collective-permute-start | bytes 2359304 | tf_op jit(solution)/shard_map/ppermute | solution.py:41
  182.4 16.8 %collective-permute-start.22 = (bf16[256,768]{1,0:T(8,128)(2,1)S(1)}, bf16[256,768]{1,0:T(8,128)(2,1)S(1)}, u32[]{:S(2)}, u32[]{:S(2)}) collective-permute-start(bf16[256,768]{1,0:T(8,128)(2,1)S(1)} %get-tuple-element.111), channel_id=1, source_target_pairs={{0,6},{1,7},{2,4},{3,5},{4,2},{5,3},{6,0},{7,1},{8,14},{9,15},{10,... | collective-permute-start | bytes 1179656 | tf_op jit(solution)/shard_map/ppermute | solution.py:45
  199.9 66.0 %collective-permute-start.36 = (bf16[1024,1024]{1,0:T(8,128)(2,1)}, bf16[1024,1024]{1,0:T(8,128)(2,1)S(1)}, u32[]{:S(2)}, u32[]{:S(2)}) collective-permute-start(bf16[1024,1024]{1,0:T(8,128)(2,1)} %all-gather.16.cloned.1.call-done.refs_3_.refs_7_.refs_8_.refs_12_), channel_id=1, source_target_pairs={{0,4},{4,0},{1,5},{5,1},{2,6},{6,2},{3,7},{7,3},{8,12},{12,8},{9,1... | collective-permute-start | bytes 6291464 | tf_op jit(solution)/shard_map/ppermute | solution.py:41
  201.1 24.1 %collective-permute-start.27 = (bf16[1024,384]{1,0:T(8,128)(2,1)S(1)}, bf16[1024,384]{1,0:T(8,128)(2,1)}, u32[]{:S(2)}, u32[]{:S(2)}) collective-permute-start(bf16[1024,384]{1,0:T(8,128)(2,1)S(1)} %slice.138.refs_8_.refs_6_.refs_7_.refs_23_), channel_id=1, source_target_pairs={{0,2},{2,0},{1,3},{3,1},{4,6},{6,4},{5,7},{7,5},{8,10},{10,8},{9,1... | collective-permute-start | bytes 2359304 | tf_op jit(solution)/shard_map/ppermute | solution.py:37
  202.3 32.6 %collective-permute-start.31 = (bf16[1024,384]{1,0:T(8,128)(2,1)}, bf16[1024,384]{1,0:T(8,128)(2,1)}, u32[]{:S(2)}, u32[]{:S(2)}) collective-permute-start(bf16[1024,384]{1,0:T(8,128)(2,1)} %collective-permute-done.29.refs_12_.refs_10_.refs_11_.refs_27_), channel_id=1, source_target_pairs={{0,2},{2,0},{1,3},{3,1},{4,6},{6,4},{5,7},{7,5},{8,10},{10,8},{9,1... | collective-permute-start | bytes 2359304 | tf_op jit(solution)/shard_map/ppermute | solution.py:37
  223.7 15.8 %collective-permute-start.23 = (bf16[256,256]{1,0:T(8,128)(2,1)S(1)}, bf16[256,256]{1,0:T(8,128)(2,1)S(1)}, u32[]{:S(2)}, u32[]{:S(2)}) collective-permute-start(bf16[256,256]{1,0:T(8,128)(2,1)S(1)} %get-tuple-element.207), channel_id=1, source_target_pairs={{0,2},{2,0},{1,3},{3,1},{4,6},{6,4},{5,7},{7,5},{8,10},{10,8},{9,1... | collective-permute-start | bytes 393224 | tf_op jit(solution)/shard_map/ppermute | solution.py:37
  224.9 23.2 %collective-permute-start.24 = (bf16[256,256]{1,0:T(8,128)(2,1)S(1)}, bf16[256,256]{1,0:T(8,128)(2,1)S(1)}, u32[]{:S(2)}, u32[]{:S(2)}) collective-permute-start(bf16[256,256]{1,0:T(8,128)(2,1)S(1)} %get-tuple-element.206), channel_id=1, source_target_pairs={{0,4},{4,0},{1,5},{5,1},{2,6},{6,2},{3,7},{7,3},{8,12},{12,8},{9,1... | collective-permute-start | bytes 393224 | tf_op jit(solution)/shard_map/ppermute | solution.py:41
  225.2 27.2 %collective-permute-start.25 = (bf16[256,256]{1,0:T(8,128)(2,1)S(1)}, bf16[256,256]{1,0:T(8,128)(2,1)S(1)}, u32[]{:S(2)}, u32[]{:S(2)}) collective-permute-start(bf16[256,256]{1,0:T(8,128)(2,1)S(1)} %get-tuple-element.205), channel_id=1, source_target_pairs={{0,6},{1,7},{2,4},{3,5},{4,2},{5,3},{6,0},{7,1},{8,14},{9,15},{10,... | collective-permute-start | bytes 393224 | tf_op jit(solution)/shard_map/ppermute | solution.py:45
  234.9 19.8 %collective-permute-start.26 = (bf16[1024,384]{1,0:T(8,128)(2,1)S(1)}, bf16[1024,384]{1,0:T(8,128)(2,1)S(1)}, u32[]{:S(2)}, u32[]{:S(2)}) collective-permute-start(bf16[1024,384]{1,0:T(8,128)(2,1)S(1)} %slice.138.refs_8_.refs_6_.refs_7_.refs_23_), channel_id=1, source_target_pairs={{0,1},{1,0},{2,3},{3,2},{4,5},{5,4},{6,7},{7,6},{8,9},{9,8},{10,11... | collective-permute-start | bytes 2359304 | tf_op jit(solution)/shard_map/ppermute | solution.py:33
  239.4 15.4 %collective-permute-start.28 = (bf16[1024,384]{1,0:T(8,128)(2,1)}, bf16[1024,384]{1,0:T(8,128)(2,1)S(1)}, u32[]{:S(2)}, u32[]{:S(2)}) collective-permute-start(bf16[1024,384]{1,0:T(8,128)(2,1)} %collective-permute-done.27.refs_10_.refs_8_.refs_9_.refs_25_), channel_id=1, source_target_pairs={{0,1},{1,0},{2,3},{3,2},{4,5},{5,4},{6,7},{7,6},{8,9},{9,8},{10,11... | collective-permute-start | bytes 2359304 | tf_op jit(solution)/shard_map/ppermute | solution.py:33
  254.7 39.0 %collective-permute-start.35 = (bf16[1024,1024]{1,0:T(8,128)(2,1)S(1)}, bf16[1024,1024]{1,0:T(8,128)(2,1)S(1)}, u32[]{:S(2)}, u32[]{:S(2)}) collective-permute-start(bf16[1024,1024]{1,0:T(8,128)(2,1)S(1)} %copy-done.2), channel_id=1, source_target_pairs={{0,1},{1,0},{2,3},{3,2},{4,5},{5,4},{6,7},{7,6},{8,9},{9,8},{10,11... | collective-permute-start | bytes 6291464 | tf_op jit(solution)/shard_map/ppermute | solution.py:33
  266.0 27.7 %collective-permute-start.37 = (bf16[1024,1024]{1,0:T(8,128)(2,1)S(1)}, bf16[1024,1024]{1,0:T(8,128)(2,1)}, u32[]{:S(2)}, u32[]{:S(2)}) collective-permute-start(bf16[1024,1024]{1,0:T(8,128)(2,1)S(1)} %collective-permute-done.36.refs_5_.refs_9_.refs_10_.refs_14_), channel_id=1, source_target_pairs={{0,1},{1,0},{2,3},{3,2},{4,5},{5,4},{6,7},{7,6},{8,9},{9,8},{10,11... | collective-permute-start | bytes 6291464 | tf_op jit(solution)/shard_map/ppermute | solution.py:33
  280.2 13.5 %collective-permute-start.34 = (bf16[256,1024]{1,0:T(8,128)(2,1)S(1)}, bf16[256,1024]{1,0:T(8,128)(2,1)S(1)}, u32[]{:S(2)}, u32[]{:S(2)}) collective-permute-start(bf16[256,1024]{1,0:T(8,128)(2,1)S(1)} %get-tuple-element.127.refs_1_.refs_3_), channel_id=1, source_target_pairs={{0,2},{2,0},{1,3},{3,1},{4,6},{6,4},{5,7},{7,5},{8,10},{10,8},{9,1... | collective-permute-start | bytes 1572872 | tf_op jit(solution)/shard_map/ppermute | solution.py:37
  304.9 11.9 %collective-permute-start.38 = (bf16[256,1024]{1,0:T(8,128)(2,1)S(1)}, bf16[256,1024]{1,0:T(8,128)(2,1)S(1)}, u32[]{:S(2)}, u32[]{:S(2)}) collective-permute-start(bf16[256,1024]{1,0:T(8,128)(2,1)S(1)} %get-tuple-element.133), channel_id=1, source_target_pairs={{0,2},{2,0},{1,3},{3,1},{4,6},{6,4},{5,7},{7,5},{8,10},{10,8},{9,1... | collective-permute-start | bytes 1572872 | tf_op jit(solution)/shard_map/ppermute | solution.py:37
  343.6 18.1 %collective-permute-start.44 = (f32[12,32,128]{2,1,0:T(8,128)S(1)}, f32[12,32,128]{2,1,0:T(8,128)S(1)}, u32[]{:S(2)}, u32[]{:S(2)}) collective-permute-start(f32[12,32,128]{2,1,0:T(8,128)S(1)} %slice_bitcast_fusion.5), channel_id=1, source_target_pairs={{0,4},{4,0},{1,5},{5,1},{2,6},{6,2},{3,7},{7,3},{8,12},{12,8},{9,1... | collective-permute-start | bytes 589832 | tf_op jit(solution)/shard_map/ppermute | solution.py:41
  361.8 19.1 %collective-permute-start.45 = (f32[2,32,128]{2,1,0:T(8,128)S(1)}, f32[2,32,128]{2,1,0:T(8,128)S(1)}, u32[]{:S(2)}, u32[]{:S(2)}) collective-permute-start(f32[2,32,128]{2,1,0:T(8,128)S(1)} %slice.140), channel_id=1, source_target_pairs={{0,2},{2,0},{1,3},{3,1},{4,6},{6,4},{5,7},{7,5},{8,10},{10,8},{9,1... | collective-permute-start | bytes 98312 | tf_op jit(solution)/shard_map/ppermute | solution.py:37
  389.0 158.9 %all-gather.18.cloned.1.call-start = ((), (), s32[]{:S(2)}) async-start(), calls=%async_computation.5 | async-start | bytes 2162688 | tf_op jit(solution)/shard_map/all_gather | solution.py:1268
  432.3 15.6 %collective-permute-start.51 = (bf16[256,768]{1,0:T(8,128)(2,1)S(1)}, bf16[256,768]{1,0:T(8,128)(2,1)S(1)}, u32[]{:S(2)}, u32[]{:S(2)}) collective-permute-start(bf16[256,768]{1,0:T(8,128)(2,1)S(1)} %get-tuple-element.194), channel_id=1, source_target_pairs={{0,2},{2,0},{1,3},{3,1},{4,6},{6,4},{5,7},{7,5},{8,10},{10,8},{9,1... | collective-permute-start | bytes 1179656 | tf_op jit(solution)/shard_map/ppermute | solution.py:37
  433.8 14.0 %collective-permute-start.52 = (bf16[256,768]{1,0:T(8,128)(2,1)S(1)}, bf16[256,768]{1,0:T(8,128)(2,1)S(1)}, u32[]{:S(2)}, u32[]{:S(2)}) collective-permute-start(bf16[256,768]{1,0:T(8,128)(2,1)S(1)} %get-tuple-element.193), channel_id=1, source_target_pairs={{0,4},{4,0},{1,5},{5,1},{2,6},{6,2},{3,7},{7,3},{8,12},{12,8},{9,1... | collective-permute-start | bytes 1179656 | tf_op jit(solution)/shard_map/ppermute | solution.py:41
  433.8 15.2 %collective-permute-start.53 = (bf16[256,768]{1,0:T(8,128)(2,1)S(1)}, bf16[256,768]{1,0:T(8,128)(2,1)S(1)}, u32[]{:S(2)}, u32[]{:S(2)}) collective-permute-start(bf16[256,768]{1,0:T(8,128)(2,1)S(1)} %get-tuple-element.192), channel_id=1, source_target_pairs={{0,6},{1,7},{2,4},{3,5},{4,2},{5,3},{6,0},{7,1},{8,14},{9,15},{10,... | collective-permute-start | bytes 1179656 | tf_op jit(solution)/shard_map/ppermute | solution.py:45
  435.1 11.9 %collective-permute-start.40 = (bf16[1,512,256]{2,1,0:T(8,128)(2,1)S(1)}, bf16[1,512,256]{2,1,0:T(8,128)(2,1)S(1)}, u32[]{:S(2)}, u32[]{:S(2)}) collective-permute-start(bf16[1,512,256]{2,1,0:T(8,128)(2,1)S(1)} %get-tuple-element.202), channel_id=1, source_target_pairs={{0,1},{1,0},{2,3},{3,2},{4,5},{5,4},{6,7},{7,6},{8,9},{9,8},{10,11... | collective-permute-start | bytes 786440 | tf_op jit(solution)/shard_map/ppermute | solution.py:33
  504.9 27.2 %collective-permute-start.64 = (bf16[4,10,32,128]{3,2,1,0:T(8,128)(2,1)S(1)}, bf16[4,10,32,128]{3,2,1,0:T(8,128)(2,1)S(1)}, u32[]{:S(2)}, u32[]{:S(2)}) collective-permute-start(bf16[4,10,32,128]{3,2,1,0:T(8,128)(2,1)S(1)} %pad_maximum_fusion.1.refs_3_), channel_id=1, source_target_pairs={{0,2},{2,0},{1,3},{3,1},{4,6},{6,4},{5,7},{7,5},{8,10},{10,8},{9,1... | collective-permute-start | bytes 983048 | tf_op jit(solution)/shard_map/ppermute | solution.py:37
  507.2 28.5 %collective-permute-start.68 = (bf16[4,10,32,128]{3,2,1,0:T(8,128)(2,1)S(1)}, bf16[4,10,32,128]{3,2,1,0:T(8,128)(2,1)S(1)}, u32[]{:S(2)}, u32[]{:S(2)}) collective-permute-start(bf16[4,10,32,128]{3,2,1,0:T(8,128)(2,1)S(1)} %collective-permute-done.66.refs_7_), channel_id=1, source_target_pairs={{0,2},{2,0},{1,3},{3,1},{4,6},{6,4},{5,7},{7,5},{8,10},{10,8},{9,1... | collective-permute-start | bytes 983048 | tf_op jit(solution)/shard_map/ppermute | solution.py:37
  512.9 26.5 %collective-permute-start.57 = (bf16[1,512,256]{2,1,0:T(8,128)(2,1)}, bf16[1,512,256]{2,1,0:T(8,128)(2,1)}, u32[]{:S(2)}, u32[]{:S(2)}) collective-permute-start(bf16[1,512,256]{2,1,0:T(8,128)(2,1)} %get-tuple-element.198), channel_id=1, source_target_pairs={{0,1},{1,0},{2,3},{3,2},{4,5},{5,4},{6,7},{7,6},{8,9},{9,8},{10,11... | collective-permute-start | bytes 786440 | tf_op jit(solution)/shard_map/ppermute | solution.py:33
  531.7 20.5 %collective-permute-start.63 = (bf16[4,10,32,128]{3,2,1,0:T(8,128)(2,1)S(1)}, bf16[4,10,32,128]{3,2,1,0:T(8,128)(2,1)S(1)}, u32[]{:S(2)}, u32[]{:S(2)}) collective-permute-start(bf16[4,10,32,128]{3,2,1,0:T(8,128)(2,1)S(1)} %pad_maximum_fusion.1.refs_3_), channel_id=1, source_target_pairs={{0,1},{1,0},{2,3},{3,2},{4,5},{5,4},{6,7},{7,6},{8,9},{9,8},{10,11... | collective-permute-start | bytes 983048 | tf_op jit(solution)/shard_map/ppermute | solution.py:33
  531.7 20.5 %collective-permute-start.67 = (bf16[4,10,32,128]{3,2,1,0:T(8,128)(2,1)S(1)}, bf16[4,10,32,128]{3,2,1,0:T(8,128)(2,1)S(1)}, u32[]{:S(2)}, u32[]{:S(2)}) collective-permute-start(bf16[4,10,32,128]{3,2,1,0:T(8,128)(2,1)S(1)} %collective-permute-done.66.refs_7_), channel_id=1, source_target_pairs={{0,1},{1,0},{2,3},{3,2},{4,5},{5,4},{6,7},{7,6},{8,9},{9,8},{10,11... | collective-permute-start | bytes 983048 | tf_op jit(solution)/shard_map/ppermute | solution.py:33
  532.2 20.0 %collective-permute-start.65 = (bf16[4,10,32,128]{3,2,1,0:T(8,128)(2,1)S(1)}, bf16[4,10,32,128]{3,2,1,0:T(8,128)(2,1)S(1)}, u32[]{:S(2)}, u32[]{:S(2)}) collective-permute-start(bf16[4,10,32,128]{3,2,1,0:T(8,128)(2,1)S(1)} %collective-permute-done.64.refs_5_), channel_id=1, source_target_pairs={{0,1},{1,0},{2,3},{3,2},{4,5},{5,4},{6,7},{7,6},{8,9},{9,8},{10,11... | collective-permute-start | bytes 983048 | tf_op jit(solution)/shard_map/ppermute | solution.py:33
  535.7 16.5 %collective-permute-start.69 = (bf16[4,10,32,128]{3,2,1,0:T(8,128)(2,1)S(1)}, bf16[4,10,32,128]{3,2,1,0:T(8,128)(2,1)S(1)}, u32[]{:S(2)}, u32[]{:S(2)}) collective-permute-start(bf16[4,10,32,128]{3,2,1,0:T(8,128)(2,1)S(1)} %collective-permute-done.68.refs_9_), channel_id=1, source_target_pairs={{0,1},{1,0},{2,3},{3,2},{4,5},{5,4},{6,7},{7,6},{8,9},{9,8},{10,11... | collective-permute-start | bytes 983048 | tf_op jit(solution)/shard_map/ppermute | solution.py:33
  (137 other events, 2024.5 us)
Sparse Core Ops, SparseCore 0:
  10.2 29.7 all-gather.7
  42.2 27.5 all-gather.9
  72.0 27.4 all-gather.11
  101.4 27.4 all-gather.13
  130.9 45.5 all-gather.15
  389.1 74.0 all-gather.19
  470.6 71.6 all-gather.17

commit v2 on v1

--- a/solution.py
+++ b/solution.py
@@ -191,7 +191,7 @@
               pltpu.VMEM((length,LANES),F32),pltpu.VMEM((LANES,length),F32),pltpu.VMEM((LANES,length),F32),
               pltpu.SemaphoreType.DMA((2*n,)),pltpu.SemaphoreType.DMA((2*n,))]),
         out_shape=jax.ShapeDtypeStruct((n,rows,6*LANES),BF),
-        compiler_params=pltpu.CompilerParams(vmem_limit_bytes=56<<20),
+        compiler_params=pltpu.CompilerParams(vmem_limit_bytes=30<<20),
         name="attend_back",
         cost_estimate=pl.CostEstimate(flops=10*4*length*length*64,bytes_accessed=length*14*LANES*2,transcendentals=4*length*length),
     )(b,*slots,*grads,text,lse)
@@ -623,7 +623,7 @@
     return (found[0], found[1:5], found[5])
 
 
-def heads_back_body(where, grad, first, t_in, g0, g1, g2, g3, partial, *refs):
+def heads_back_body(where, grad, first, t_in, g0, g1, g2, g3, partial, convs, *refs):
     pieces = refs[:8]
     down, up = refs[8:10]
     result, half, grads = refs[10:13]
@@ -668,27 +668,30 @@
                 grads[side, pair, piece, 3 * RANK : 4 * RANK, :] = partial[
                     side, pair, piece, :RANK, :
                 ]
-                grads[side, pair, piece, 7 * RANK :, :] = partial[side, pair, piece, RANK:, :]
-
-
-def heads_back(where, grad, first, t_in, slots, partial, pieces, down, up):
+                grads[side, pair, piece, 7 * RANK : 8 * RANK, :] = partial[
+                    side, pair, piece, RANK:, :
+                ]
+                grads[side, pair, piece, 8 * RANK :, :] = convs[side, pair, piece]
+
+
+def heads_back(where, grad, first, t_in, slots, partial, convs, pieces, down, up):
     count, width = grad.shape
     three = 3 * LANES
     return run(
         heads_back_body,
         "heads_backward",
-        "v" * 8 + "a" * 10,
+        "v" * 9 + "a" * 10,
         [
             shape((count, width), F32),
             shape((count, width), BF),
-            shape((2, 2, 2, 8 * RANK, LANES), F32),
+            shape((2, 2, 2, 13 * RANK, LANES), F32),
         ],
         [
             pltpu.VMEM((4, width + three, 2 * three), BF),
             pltpu.VMEM((width, three), BF),
             pltpu.SemaphoreType.DMA((35,)),
         ],
-        [where, grad, first, t_in, *slots, partial, *pieces, down, up],
+        [where, grad, first, t_in, *slots, partial, convs, *pieces, down, up],
         flops=2 * count * width * 3 * width,
     )
 
@@ -1399,22 +1402,18 @@
     )
     came = after(by_pair(sums_two[2:4]), grad)
     sums_two = jnp.concatenate([sums_two[:2] + came, sums_two[4:]], axis=0)
+    found_two = everywhere(sums_two)
     grad_slots = exchanged(grad_slots)
-    conv_sums = conv_sums[0] + by_side(conv_sums[1])
-    conv_sums = conv_sums[0] + by_pair(after(conv_sums[1], grad_slots[1]))
-    payload = jnp.concatenate(
-        [sums_two.astype(BF).reshape(-1, LANES), conv_sums.astype(BF).reshape(-1, LANES)], axis=0
-    )
-    found = everywhere(payload)
-    back = attend_back(after(block, payload), slots, grad_slots, text, logs)
+    back = attend_back(block, slots, grad_slots, text, logs)
     output = feature_parts(output, place)
     back = exchanged([back[n] for n in range(4)])
     grad, half, head_sums = heads_back(
-        after(where, output), grad, first, t_heads, back, partial, heads, adapt_down, adapt_up
+        after(where, output), grad, first, t_heads, back, partial, conv_sums, heads,
+        adapt_down, adapt_up,
     )
     other_half = by_pair(half)
-    head_sums = head_sums[0] + by_side(head_sums[1])
-    head_sums = head_sums[0] + by_pair(head_sums[1])
+    head_sums = head_sums[0] + by_side(head_sums[1].astype(BF)).astype(F32)
+    head_sums = head_sums[0] + by_pair(head_sums[1].astype(BF)).astype(F32)
     found_heads = everywhere(after(head_sums, other_half))
     part, send, sums_one = ffn_back(
         0, 0, 7, where, half, other_half, *kept_one, w1_in, w1_out, adapters
@@ -1430,19 +1429,14 @@
 
     outs = [shape(v.shape, F32) for v in (adapt_down, adapt_up, adapt_down_ff, adapt_up_ff)]
     ffn_blocks, ffn_rows = sums_two.shape[:2]
-    conv_blocks, conv_rows = conv_sums.shape[:2]
-    base = ffn_blocks * ffn_rows
     plan = [(kind, slot, rows_of(0, 2, ffn_rows, g)) for kind, slot, g in ((0, 5, 0), (1, 8, 1))]
     plan += [
         (kind, 1, rows_of(0, ffn_blocks, ffn_rows, g, 2)) for kind, g in ((2, 0), (3, 1))
     ]
-    plan += [
-        (kind, slot, rows_of(base, conv_blocks, conv_rows, g))
-        for kind, slot, g in ((0, 4, 0), (1, 6, 1), (0, 7, 2), (1, 3, 3), (1, 4, 4))
-    ]
-    outs = expand(plan, spread, turned, after(found, send), outs)
+    outs = expand(plan, spread, turned, after(found_two, send), outs)
     head_blocks, head_rows = head_sums.shape[:2]
     places = ((0, 1), (0, 2), (0, 3), (1, 5), (1, 0), (1, 1), (1, 2), (0, 6))
+    places += ((0, 4), (1, 6), (0, 7), (1, 3), (1, 4))
     plan = [
         (kind, slot, rows_of(0, head_blocks, head_rows, g))
         for g, (kind, slot) in enumerate(places)

time: 573 us -> 560 us (0.977)
  starting transfers between devices: 115 us -> 104 us
    ppermute x25 -> x24, starting transfers between devices: 31 us -> 24.8 us  [by_pair(): return lax.ppermute(value, 'tp', PAIR)]
    ppermute x25 -> x24, waiting for transfers between devices: 98.2 us -> 94 us  [by_pair(): return lax.ppermute(value, 'tp', PAIR)]
    unnamed x216 -> x226, local copies, waits for them, and re-layouts: 40.1 us -> 43 us
    ppermute x15 -> x14, waiting for transfers between devices: 72.7 us -> 74.3 us  [by_side(): return lax.ppermute(value, 'ctx', SIDE)]
    ppermute x15 -> x14, starting transfers between devices: 17 us -> 16.7 us  [by_side(): return lax.ppermute(value, 'ctx', SIDE)]
  transfers between devices with their start and end apart: 79 -> 77, of which waited for: 39 -> 36; matrix products, arithmetic and copies ran while one was open for 5% -> 5% of each run, Pallas kernels for 22% -> 22%
where the time goes in v2:
time: 560 us; the launch traced here: 551 us
  waiting for transfers between devices  204 us (36%)
  Pallas kernels  148 us (26%)
  starting transfers between devices  104 us (19%)
  local copies, waits for them, and re-layouts  56.6 us (10%)
  between operations  16.7 us (3%)
  other arithmetic  13 us (2%)
  blocking collectives  7.87 us (1%)
    ppermute x24, waiting for transfers between devices, by_pair(): return lax.ppermute(value, 'tp', PAIR)  94 us
    pallas_call x13, Pallas kernels, run(): pl.pallas_call(body, name=name, in_specs=specs, out_specs=out_specs or [V...  93.7 us
    ppermute x14, waiting for transfers between devices, by_side(): return lax.ppermute(value, 'ctx', SIDE)  74.3 us
    ppermute x23, starting transfers between devices, by_core(): return lax.ppermute(value, 'tp', CORE)  50.9 us
    unnamed x226, local copies, waits for them, and re-layouts  43 us
    pallas_call x1, Pallas kernels, attend_back(): pl.pallas_call(bwd_kernel, grid_spec=pltpu.PrefetchScalarGridSpec(num_sca...  29.2 us
    ppermute x24, starting transfers between devices, by_pair(): return lax.ppermute(value, 'tp', PAIR)  24.8 us
    ppermute x14, starting transfers between devices, by_side(): return lax.ppermute(value, 'ctx', SIDE)  16.7 us
  transfers between devices with their start and end apart: 77, of which 36 were waited for; matrix products, arithmetic and copies ran while one was open for 5% of the time, Pallas kernels for 22%

profile of v2, /device:TPU:1, one launch (start us, length us, event | category | flops | bytes accessed | tf_op | source)
XLA Modules:
  0.0 550.7 jit_solution(1878253700698765728)
XLA Ops:
  12.3 7.9 %all-reduce = s32[8]{0:T(128)S(1)} all-reduce(s32[8]{0:T(128)S(1)} %dynamic-update-slice), channel_id=1, replica_groups=mesh['shard'=4,'ctx'=2,'tp'=4] {'shard'}, use_global_device_ids=true, to_apply=%add | all-reduce | flops 8 | bytes 64
  25.3 9.2 %collective-permute-done.1 = bf16[512,512]{1,0:T(8,128)(2,1)S(1)} collective-permute-done((bf16[512,512]{1,0:T(8,128)(2,1)S(1)}, bf16[512,512]{1,0:T(8,128)(2,1)S(1)}, u32[]{:S(2)}, u32[]{:S(2)}) %collective-permute-start.1) | collective-permute-done | bytes 524320 | tf_op jit(solution)/shard_map/ppermute | solution.py:37
  48.1 7.1 %collective-permute-done.12 = bf16[256,512]{1,0:T(8,128)(2,1)S(1)} collective-permute-done((bf16[256,512]{1,0:T(8,128)(2,1)S(1)}, bf16[256,512]{1,0:T(8,128)(2,1)S(1)}, u32[]{:S(2)}, u32[]{:S(2)}) %collective-permute-start.12) | collective-permute-done | bytes 262176 | tf_op jit(solution)/shard_map/ppermute | solution.py:37
  56.1 12.5 %collective-permute-done.3.refs_5_.refs_10_ = bf16[1024,512]{1,0:T(8,128)(2,1)} collective-permute-done((bf16[1024,512]{1,0:T(8,128)(2,1)}, bf16[1024,512]{1,0:T(8,128)(2,1)}, u32[]{:S(2)}, u32[]{:S(2)}) %collective-permute-start.3) | collective-permute-done | bytes 1048608 | tf_op jit(solution)/shard_map/ppermute | solution.py:41
  75.0 20.5 %collective-permute-done.6.refs_9_.refs_14_ = bf16[1024,512]{1,0:T(8,128)(2,1)} collective-permute-done((bf16[1024,512]{1,0:T(8,128)(2,1)}, bf16[1024,512]{1,0:T(8,128)(2,1)}, u32[]{:S(2)}, u32[]{:S(2)}) %collective-permute-start.6) | collective-permute-done | bytes 1048608 | tf_op jit(solution)/shard_map/ppermute | solution.py:41
  95.5 4.0 all-gather.12.cloned.1.call-done.refs_0_.refs_15_
  108.3 11.2 %hidden_forward.2 = (f32[256,1024]{1,0:T(8,128)S(1)}, bf16[256,1024]{1,0:T(8,128)(2,1)S(1)}, f32[4,512,512]{2,1,0:T(8,128)}, bf16[512,128]{1,0:T(8,128)(2,1)S(1)}, bf16[512,128]{1,0:T(8,128)(2,1)S(1)}) custom-call(s32[4]{0:T(128)S(1)} %pad_add_fusion.where.refs_0_, bf16[256,1024]{1,0:T(8,128)(2,1)S(1)} %get-tuple-element.96.refs_1_.refs_3_, ...), custom_call_target="tpu_custom_call" | custom-call | flops 4294967296 | bytes 16777216 | tf_op jit(solution)/shard_map/hidden_forward/pallas_call | solution.py:320
  122.0 3.1 collective-permute-done.14.refs_2_.refs_17_
  126.0 2.9 all-gather.14.cloned.1.call-done
  131.3 21.9 %collective-permute-done.18.refs_6_.refs_21_ = bf16[1024,512]{1,0:T(8,128)(2,1)S(1)} collective-permute-done((bf16[1024,512]{1,0:T(8,128)(2,1)}, bf16[1024,512]{1,0:T(8,128)(2,1)S(1)}, u32[]{:S(2)}, u32[]{:S(2)}) %collective-permute-start.18) | collective-permute-done | bytes 1048608 | tf_op jit(solution)/shard_map/ppermute | solution.py:41
  158.5 10.1 %collective-permute-done.8.other = bf16[256,1024]{1,0:T(8,128)(2,1)S(1)} collective-permute-done((bf16[256,1024]{1,0:T(8,128)(2,1)}, bf16[256,1024]{1,0:T(8,128)(2,1)S(1)}, u32[]{:S(2)}, u32[]{:S(2)}) %collective-permute-start.8) | collective-permute-done | bytes 524320 | tf_op jit(solution)/shard_map/ppermute | solution.py:37
  171.2 6.3 %heads_forward.1 = (f32[256,1024]{1,0:T(8,128)S(1)}, bf16[256,768]{1,0:T(8,128)(2,1)S(1)}, bf16[256,768]{1,0:T(8,128)(2,1)S(1)}, bf16[256,768]{1,0:T(8,128)(2,1)...) custom-call(s32[4]{0:T(128)S(1)} %pad_add_fusion.where.refs_0_, f32[256,1024]{1,0:T(8,128)S(1)} %copy-done.17, ...), custom_call_target="tpu_custom_call" | custom-call | flops 1610612736 | bytes 16777216 | tf_op jit(solution)/shard_map/heads_forward/pallas_call | solution.py:320
  182.6 7.2 %collective-permute-done.20.s1 = bf16[256,768]{1,0:T(8,128)(2,1)S(1)} collective-permute-done((bf16[256,768]{1,0:T(8,128)(2,1)S(1)}, bf16[256,768]{1,0:T(8,128)(2,1)S(1)}, u32[]{:S(2)}, u32[]{:S(2)}) %collective-permute-start.20) | collective-permute-done | bytes 393248 | tf_op jit(solution)/shard_map/ppermute | solution.py:37
  191.5 7.6 %collective-permute-done.22.s3 = bf16[256,768]{1,0:T(8,128)(2,1)S(1)} collective-permute-done((bf16[256,768]{1,0:T(8,128)(2,1)S(1)}, bf16[256,768]{1,0:T(8,128)(2,1)S(1)}, u32[]{:S(2)}, u32[]{:S(2)}) %collective-permute-start.22) | collective-permute-done | bytes 393248 | tf_op jit(solution)/shard_map/ppermute | solution.py:45
  207.5 14.8 %attend.1 = (bf16[4,256,256]{2,1,0:T(8,128)(2,1)S(1)}, f32[4,1024,1]{2,1,0:T(8,128)S(1)}) custom-call(s32[1]{0:T(128)} %bitcast.14.b_ref, bf16[256,768]{1,0:T(8,128)(2,1)S(1)} %copy-done.82, bf16[256,768]{1,0:T(8,128)(2,1)S(1)} %copy-done.85, bf16[256,768]{1,0:T(8,128)(2,1)S(1)} %copy-done.88, bf16[256,768]{1,0:T(8,128)(2,1)S(1)} %copy-done.91, ...), custom_call_target="tpu_custom_call" | custom-call | flops 1073741824 | bytes 2097152 | tf_op jit(solution)/shard_map/attend/pallas_call | solution.py:112
  226.4 8.5 %collective-permute-done.31.refs_14_.refs_12_.refs_13_.refs_29_ = bf16[1024,384]{1,0:T(8,128)(2,1)} collective-permute-done((bf16[1024,384]{1,0:T(8,128)(2,1)}, bf16[1024,384]{1,0:T(8,128)(2,1)}, u32[]{:S(2)}, u32[]{:S(2)}) %collective-permute-start.31) | collective-permute-done | bytes 786464 | tf_op jit(solution)/shard_map/ppermute | solution.py:37
  234.8 4.6 collective-permute-start.26
  240.7 7.4 %collective-permute-done.24.m2.refs_12_ = bf16[256,256]{1,0:T(8,128)(2,1)S(1)} collective-permute-done((bf16[256,256]{1,0:T(8,128)(2,1)S(1)}, bf16[256,256]{1,0:T(8,128)(2,1)S(1)}, u32[]{:S(2)}, u32[]{:S(2)}) %collective-permute-start.24) | collective-permute-done | bytes 131104 | tf_op jit(solution)/shard_map/ppermute | solution.py:41
  248.1 4.3 collective-permute-start.30
  257.0 6.8 %pair_forward.1 = (f32[256,1024]{1,0:T(8,128)S(1)}, f32[256,1024]{1,0:T(8,128)S(1)}, f32[256,1024]{1,0:T(8,128)S(1)}, f32[2,2,32,256]{3,2,1,0:T(8,128)S(1)}, bf1...) custom-call(s32[4]{0:T(128)S(1)} %pad_add_fusion.where.refs_0_, f32[256,1024]{1,0:T(8,128)} %copy-done.15, ...), custom_call_target="tpu_custom_call" | custom-call | flops 1610612736 | bytes 16777216 | tf_op jit(solution)/shard_map/pair_forward/pallas_call | solution.py:320
  268.8 2.5 collective-permute-done.33.refs_4_
  271.3 6.8 %conv_forward.1 = (f32[256,1024]{1,0:T(8,128)S(1)}, f32[256,1024]{1,0:T(8,128)S(1)}, bf16[256,1024]{1,0:T(8,128)(2,1)S(1)}, bf16[256,128]{1,0:T(8,128)(2,1)S(1)}) custom-call(s32[4]{0:T(128)S(1)} %pad_add_fusion.where.refs_0_, f32[256,1024]{1,0:T(8,128)S(1)} %get-tuple-element.120.refs_1_.refs_7_, f32[256,1024]{1,0:T(8,128)} %copy-done.21, ...), custom_call_target="tpu_custom_call" | custom-call | flops 536870912 | bytes 16777216 | tf_op jit(solution)/shard_map/conv_forward/pallas_call | solution.py:320
  282.3 11.3 %collective-permute-done.34.refs_2_.refs_4_ = bf16[256,1024]{1,0:T(8,128)(2,1)S(1)} collective-permute-done((bf16[256,1024]{1,0:T(8,128)(2,1)S(1)}, bf16[256,1024]{1,0:T(8,128)(2,1)S(1)}, u32[]{:S(2)}, u32[]{:S(2)}) %collective-permute-start.34) | collective-permute-done | bytes 524320 | tf_op jit(solution)/shard_map/ppermute | solution.py:37
  293.7 11.1 %hidden_forward.3 = (f32[256,1024]{1,0:T(8,128)S(1)}, bf16[256,1024]{1,0:T(8,128)(2,1)S(1)}, f32[4,512,512]{2,1,0:T(8,128)}, bf16[512,128]{1,0:T(8,128)(2,1)S(1)}, bf16[512,128]{1,0:T(8,128)(2,1)S(1)}) custom-call(s32[4]{0:T(128)S(1)} %pad_add_fusion.where.refs_0_, bf16[256,1024]{1,0:T(8,128)(2,1)S(1)} %get-tuple-element.125.refs_1_.refs_3_, ...), custom_call_target="tpu_custom_call" | custom-call | flops 4294967296 | bytes 16777216 | tf_op jit(solution)/shard_map/hidden_forward/pallas_call | solution.py:320
  306.1 10.7 %collective-permute-done.38.other = bf16[256,1024]{1,0:T(8,128)(2,1)S(1)} collective-permute-done((bf16[256,1024]{1,0:T(8,128)(2,1)S(1)}, bf16[256,1024]{1,0:T(8,128)(2,1)S(1)}, u32[]{:S(2)}, u32[]{:S(2)}) %collective-permute-start.38) | collective-permute-done | bytes 524320 | tf_op jit(solution)/shard_map/ppermute | solution.py:37
  319.8 10.1 %collective-permute-done.41.refs_2_ = bf16[256,1024]{1,0:T(8,128)(2,1)S(1)} collective-permute-done((bf16[256,1024]{1,0:T(8,128)(2,1)S(1)}, bf16[256,1024]{1,0:T(8,128)(2,1)S(1)}, u32[]{:S(2)}, u32[]{:S(2)}) %collective-permute-start.41) | collective-permute-done | bytes 524320 | tf_op jit(solution)/shard_map/ppermute | solution.py:37
  329.9 12.2 %hidden_backward.2 = (f32[256,1024]{1,0:T(8,128)S(1)}, bf16[256,1024]{1,0:T(8,128)(2,1)S(1)}, f32[2,12,32,128]{3,2,1,0:T(8,128)S(1)}) custom-call(s32[4]{0:T(128)S(1)} %pad_add_fusion.where.refs_0_, bf16[256,1024]{1,0:T(8,128)(2,1)S(1)} %get-tuple-element.135.refs_1_, bf16[256,1024]{1,0:T(8,128)(2,1)S(1)} %collective-permute-done.41.refs_2_, ...), custom_call_target="tpu_custom_call" | custom-call | flops 4294967296 | bytes 16777216 | tf_op jit(solution)/shard_map/hidden_backward/pallas_call | solution.py:320
  343.6 2.8 collective-permute-start.68
  346.4 6.7 %collective-permute-done.42.refs_3_ = bf16[256,1024]{1,0:T(8,128)(2,1)S(1)} collective-permute-done((bf16[256,1024]{1,0:T(8,128)(2,1)S(1)}, bf16[256,1024]{1,0:T(8,128)(2,1)S(1)}, u32[]{:S(2)}, u32[]{:S(2)}) %collective-permute-start.42) | collective-permute-done | bytes 524320 | tf_op jit(solution)/shard_map/ppermute | solution.py:37
  353.2 5.1 conv_backward.1
  366.0 11.2 %pair_backward.1 = (f32[256,1024]{1,0:T(8,128)}, bf16[256,256]{1,0:T(8,128)(2,1)S(1)}, bf16[256,256]{1,0:T(8,128)(2,1)S(1)}, bf16[256,256]{1,0:T(8,128)(2,1)S(1)...) custom-call(s32[4]{0:T(128)S(1)} %pad_add_fusion.where.refs_0_, ...), custom_call_target="tpu_custom_call" | custom-call | flops 1610612736 | bytes 16777216 | tf_op jit(solution)/shard_map/pair_backward/pallas_call | solution.py:320
  391.2 29.2 %attend_back.1 = bf16[4,256,768]{2,1,0:T(8,128)(2,1)S(1)} custom-call(s32[1]{0:T(128)} %bitcast.14.b_ref, bf16[256,768]{1,0:T(8,128)(2,1)S(1)} %copy-done.83, bf16[256,768]{1,0:T(8,128)(2,1)S(1)} %copy-done.86, bf16[256,768]{1,0:T(8,128)(2,1)S(1)} %copy-done.89, bf16[256,768]{1,0:T(8,128)(2,1)S(1)} %copy-done.92, ...), custom_call_target="tpu_custom_call" | custom-call | flops 2684354560 | bytes 3670016 | tf_op jit(solution)/shard_map/attend_back/pallas_call | solution.py:184
  423.6 8.3 %collective-permute-start.40 = (bf16[1,512,256]{2,1,0:T(8,128)(2,1)S(1)}, bf16[1,512,256]{2,1,0:T(8,128)(2,1)S(1)}, u32[]{:S(2)}, u32[]{:S(2)}) collective-permute-start(bf16[1,512,256]{2,1,0:T(8,128)(2,1)S(1)} %get-tuple-element.198), channel_id=1, source_target_pairs={{0,1},{1,0},{2,3},{3,2},{4,5},{5,4},{6,7},{7,6},{8,9},{9,8},{10,11... | collective-permute-start | bytes 786440 | tf_op jit(solution)/shard_map/ppermute | solution.py:33
  433.9 6.0 %collective-permute-done.49.g3 = bf16[256,768]{1,0:T(8,128)(2,1)S(1)} collective-permute-done((bf16[256,768]{1,0:T(8,128)(2,1)S(1)}, bf16[256,768]{1,0:T(8,128)(2,1)S(1)}, u32[]{:S(2)}, u32[]{:S(2)}) %collective-permute-start.49) | collective-permute-done | bytes 393248 | tf_op jit(solution)/shard_map/ppermute | solution.py:45
  439.9 7.0 %heads_backward.1 = (f32[256,1024]{1,0:T(8,128)S(1)}, bf16[256,1024]{1,0:T(8,128)(2,1)S(1)}, f32[2,2,2,208,128]{4,3,2,1,0:T(8,128)S(1)}) custom-call(s32[4]{0:T(128)S(1)} %pad_add_fusion.where.refs_0_, f32[256,1024]{1,0:T(8,128)S(1)} %copy-done.44, f32[256,1024]{1,0:T(8,128)S(1)} %copy-done.16, bf16[256,384]{1,0:T(8,128)(2,1)S(1)} %copy-done.69, ...), custom_call_target="tpu_custom_call" | custom-call | flops 1610612736 | bytes 16777216 | tf_op jit(solution)/shard_map/heads_backward/pallas_call | solution.py:320
  447.9 2.5 collective-permute-start.66
  451.2 2.4 collective-permute-done.66
  454.8 5.1 collective-permute-done.67
  465.8 12.2 %hidden_backward.3 = (f32[256,1024]{1,0:T(8,128)S(1)}, bf16[256,1024]{1,0:T(8,128)(2,1)S(1)}, f32[2,12,32,128]{3,2,1,0:T(8,128)S(1)}) custom-call(s32[4]{0:T(128)S(1)} %pad_add_fusion.where.refs_0_, bf16[256,1024]{1,0:T(8,128)(2,1)S(1)} %copy-done.61, bf16[256,1024]{1,0:T(8,128)(2,1)S(1)} %copy-done.63, bf16[256,1024]{1,0:T(8,128)(2,1)S(1)} %copy-done.38, ...), custom_call_target="tpu_custom_call" | custom-call | flops 4294967296 | bytes 16777216 | tf_op jit(solution)/shard_map/hidden_backward/pallas_call | solution.py:320
  478.2 3.3 collective-permute-done.54
  488.0 3.0 collective-permute-done.57
  495.3 5.3 collective-permute-done.62.refs_7_
  503.3 12.6 %collective-permute-start.53 = (bf16[1,512,256]{2,1,0:T(8,128)(2,1)}, bf16[1,512,256]{2,1,0:T(8,128)(2,1)}, u32[]{:S(2)}, u32[]{:S(2)}) collective-permute-start(bf16[1,512,256]{2,1,0:T(8,128)(2,1)} %get-tuple-element.194), channel_id=1, source_target_pairs={{0,1},{1,0},{2,3},{3,2},{4,5},{5,4},{6,7},{7,6},{8,9},{9,8},{10,11... | collective-permute-start | bytes 786440 | tf_op jit(solution)/shard_map/ppermute | solution.py:33
  516.4 6.7 %collective-permute-start.61 = (bf16[4,10,32,128]{3,2,1,0:T(8,128)(2,1)S(1)}, bf16[4,10,32,128]{3,2,1,0:T(8,128)(2,1)S(1)}, u32[]{:S(2)}, u32[]{:S(2)}) collective-permute-start(bf16[4,10,32,128]{3,2,1,0:T(8,128)(2,1)S(1)} %collective-permute-done.60.refs_5_), channel_id=1, source_target_pairs={{0,1},{1,0},{2,3},{3,2},{4,5},{5,4},{6,7},{7,6},{8,9},{9,8},{10,11... | collective-permute-start | bytes 983048 | tf_op jit(solution)/shard_map/ppermute | solution.py:33
  523.1 3.5 collective-permute-start.65
  530.7 3.1 expand.2
  535.8 3.8 expand.3
  539.7 3.6 expand_near.1
  (437 shorter events, 147.6 us)
Async XLA Ops:
  7.3 32.8 %all-gather.8.cloned.1.call-start = ((), (), s32[]{:S(2)}) async-start(), calls=%async_computation | async-start | bytes 1310720 | tf_op jit(solution)/shard_map/all_gather | solution.py:1231
  8.5 14.3 %collective-permute-start = (bf16[512,256]{1,0:T(8,128)(2,1)S(1)}, bf16[512,256]{1,0:T(8,128)(2,1)S(1)}, u32[]{:S(2)}, u32[]{:S(2)}) collective-permute-start(bf16[512,256]{1,0:T(8,128)(2,1)S(1)} %get-tuple-element.210), channel_id=1, source_target_pairs={{0,1},{1,0},{2,3},{3,2},{4,5},{5,4},{6,7},{7,6},{8,9},{9,8},{10,11... | collective-permute-start | bytes 786440 | tf_op jit(solution)/shard_map/ppermute | solution.py:33
  9.4 60.4 %all-gather.10.cloned.1.call-start = ((), (), s32[]{:S(2)}) async-start(), calls=%async_computation.1 | async-start | bytes 1310720 | tf_op jit(solution)/shard_map/all_gather | solution.py:1231
  9.5 31.0 %collective-permute-start.9 = (bf16[31,256]{1,0:T(8,128)(2,1)}, bf16[31,256]{1,0:T(8,128)(2,1)}, u32[]{:S(2)}, u32[]{:S(2)}) collective-permute-start(bf16[31,256]{1,0:T(8,128)(2,1)} %param.29), channel_id=1, source_target_pairs={{0,1},{1,0},{2,3},{3,2},{4,5},{5,4},{6,7},{7,6},{8,9},{9,8},{10,11... | collective-permute-start | bytes 47624 | tf_op jit(solution)/shard_map/ppermute | solution.py:33
  10.7 36.5 %collective-permute-start.11 = (bf16[512,256]{1,0:T(8,128)(2,1)}, bf16[512,256]{1,0:T(8,128)(2,1)S(1)}, u32[]{:S(2)}, u32[]{:S(2)}) collective-permute-start(bf16[512,256]{1,0:T(8,128)(2,1)} %get-tuple-element.208), channel_id=1, source_target_pairs={{0,1},{1,0},{2,3},{3,2},{4,5},{5,4},{6,7},{7,6},{8,9},{9,8},{10,11... | collective-permute-start | bytes 786440 | tf_op jit(solution)/shard_map/ppermute | solution.py:33
  23.0 11.5 %collective-permute-start.1 = (bf16[512,512]{1,0:T(8,128)(2,1)S(1)}, bf16[512,512]{1,0:T(8,128)(2,1)S(1)}, u32[]{:S(2)}, u32[]{:S(2)}) collective-permute-start(bf16[512,512]{1,0:T(8,128)(2,1)S(1)} %maximum_select_fusion.1), channel_id=1, source_target_pairs={{0,2},{2,0},{1,3},{3,1},{4,6},{6,4},{5,7},{7,5},{8,10},{10,8},{9,1... | collective-permute-start | bytes 1572872 | tf_op jit(solution)/shard_map/ppermute | solution.py:37
  40.1 59.3 %all-gather.12.cloned.1.call-start = ((), (), s32[]{:S(2)}) async-start(), calls=%async_computation.2 | async-start | bytes 1310720 | tf_op jit(solution)/shard_map/all_gather | solution.py:1231
  42.5 13.6 %collective-permute-start.2 = (bf16[1024,512]{1,0:T(8,128)(2,1)}, bf16[1024,512]{1,0:T(8,128)(2,1)S(1)}, u32[]{:S(2)}, u32[]{:S(2)}) collective-permute-start(bf16[1024,512]{1,0:T(8,128)(2,1)} %all-gather.8.cloned.1.call-done.refs_3_.refs_8_), channel_id=1, source_target_pairs={{0,1},{1,0},{2,3},{3,2},{4,5},{5,4},{6,7},{7,6},{8,9},{9,8},{10,11... | collective-permute-start | bytes 3145736 | tf_op jit(solution)/shard_map/ppermute | solution.py:33
  43.5 25.1 %collective-permute-start.3 = (bf16[1024,512]{1,0:T(8,128)(2,1)}, bf16[1024,512]{1,0:T(8,128)(2,1)}, u32[]{:S(2)}, u32[]{:S(2)}) collective-permute-start(bf16[1024,512]{1,0:T(8,128)(2,1)} %all-gather.8.cloned.1.call-done.refs_3_.refs_8_), channel_id=1, source_target_pairs={{0,4},{4,0},{1,5},{5,1},{2,6},{6,2},{3,7},{7,3},{8,12},{12,8},{9,1... | collective-permute-start | bytes 3145736 | tf_op jit(solution)/shard_map/ppermute | solution.py:41
  69.9 59.0 %all-gather.14.cloned.1.call-start = ((), (), s32[]{:S(2)}) async-start(), calls=%async_computation.3 | async-start | bytes 1310720 | tf_op jit(solution)/shard_map/all_gather | solution.py:1231
  70.9 24.6 %collective-permute-start.6 = (bf16[1024,512]{1,0:T(8,128)(2,1)}, bf16[1024,512]{1,0:T(8,128)(2,1)}, u32[]{:S(2)}, u32[]{:S(2)}) collective-permute-start(bf16[1024,512]{1,0:T(8,128)(2,1)} %all-gather.10.cloned.1.call-done.refs_7_.refs_12_), channel_id=1, source_target_pairs={{0,4},{4,0},{1,5},{5,1},{2,6},{6,2},{3,7},{7,3},{8,12},{12,8},{9,1... | collective-permute-start | bytes 3145736 | tf_op jit(solution)/shard_map/ppermute | solution.py:41
  99.5 100.4 %all-gather.16.cloned.1.call-start = ((), (), s32[]{:S(2)}) async-start(), calls=%async_computation.4 | async-start | bytes 2621440 | tf_op jit(solution)/shard_map/all_gather | solution.py:1231
  100.4 21.6 %collective-permute-start.13 = (bf16[1024,512]{1,0:T(8,128)(2,1)}, bf16[1024,512]{1,0:T(8,128)(2,1)S(1)}, u32[]{:S(2)}, u32[]{:S(2)}) collective-permute-start(bf16[1024,512]{1,0:T(8,128)(2,1)} %all-gather.12.cloned.1.call-done.refs_0_.refs_15_), channel_id=1, source_target_pairs={{0,1},{1,0},{2,3},{3,2},{4,5},{5,4},{6,7},{7,6},{8,9},{9,8},{10,11... | collective-permute-start | bytes 3145736 | tf_op jit(solution)/shard_map/ppermute | solution.py:33
  100.5 24.6 %collective-permute-start.14 = (bf16[1024,512]{1,0:T(8,128)(2,1)}, bf16[1024,512]{1,0:T(8,128)(2,1)}, u32[]{:S(2)}, u32[]{:S(2)}) collective-permute-start(bf16[1024,512]{1,0:T(8,128)(2,1)} %all-gather.12.cloned.1.call-done.refs_0_.refs_15_), channel_id=1, source_target_pairs={{0,2},{2,0},{1,3},{3,1},{4,6},{6,4},{5,7},{7,5},{8,10},{10,8},{9,1... | collective-permute-start | bytes 3145736 | tf_op jit(solution)/shard_map/ppermute | solution.py:37
  101.7 24.3 %collective-permute-start.16 = (bf16[1024,512]{1,0:T(8,128)(2,1)}, bf16[1024,512]{1,0:T(8,128)(2,1)}, u32[]{:S(2)}, u32[]{:S(2)}) collective-permute-start(bf16[1024,512]{1,0:T(8,128)(2,1)} %all-gather.12.cloned.1.call-done.refs_0_.refs_15_), channel_id=1, source_target_pairs={{0,4},{4,0},{1,5},{5,1},{2,6},{6,2},{3,7},{7,3},{8,12},{12,8},{9,1... | collective-permute-start | bytes 3145736 | tf_op jit(solution)/shard_map/ppermute | solution.py:41
  128.9 400.1 %all-gather.20.cloned.1.call-start = ((), (), s32[]{:S(2)}) async-start(), calls=%async_computation.6 | async-start | bytes 2703360 | tf_op jit(solution)/shard_map/all_gather | solution.py:1271
  129.0 24.2 %collective-permute-start.18 = (bf16[1024,512]{1,0:T(8,128)(2,1)}, bf16[1024,512]{1,0:T(8,128)(2,1)S(1)}, u32[]{:S(2)}, u32[]{:S(2)}) collective-permute-start(bf16[1024,512]{1,0:T(8,128)(2,1)} %collective-permute-done.14.refs_2_.refs_17_), channel_id=1, source_target_pairs={{0,4},{4,0},{1,5},{5,1},{2,6},{6,2},{3,7},{7,3},{8,12},{12,8},{9,1... | collective-permute-start | bytes 3145736 | tf_op jit(solution)/shard_map/ppermute | solution.py:41
  130.2 38.4 %collective-permute-start.15 = (bf16[1024,512]{1,0:T(8,128)(2,1)}, bf16[1024,512]{1,0:T(8,128)(2,1)S(1)}, u32[]{:S(2)}, u32[]{:S(2)}) collective-permute-start(bf16[1024,512]{1,0:T(8,128)(2,1)} %collective-permute-done.14.refs_2_.refs_17_), channel_id=1, source_target_pairs={{0,1},{1,0},{2,3},{3,2},{4,5},{5,4},{6,7},{7,6},{8,9},{9,8},{10,11... | collective-permute-start | bytes 3145736 | tf_op jit(solution)/shard_map/ppermute | solution.py:33
  131.3 37.3 %collective-permute-start.17 = (bf16[1024,512]{1,0:T(8,128)(2,1)}, bf16[1024,512]{1,0:T(8,128)(2,1)S(1)}, u32[]{:S(2)}, u32[]{:S(2)}) collective-permute-start(bf16[1024,512]{1,0:T(8,128)(2,1)} %collective-permute-done.16.refs_4_.refs_19_), channel_id=1, source_target_pairs={{0,1},{1,0},{2,3},{3,2},{4,5},{5,4},{6,7},{7,6},{8,9},{9,8},{10,11... | collective-permute-start | bytes 3145736 | tf_op jit(solution)/shard_map/ppermute | solution.py:33
  153.2 15.4 %collective-permute-start.19 = (bf16[1024,512]{1,0:T(8,128)(2,1)S(1)}, bf16[1024,512]{1,0:T(8,128)(2,1)S(1)}, u32[]{:S(2)}, u32[]{:S(2)}) collective-permute-start(bf16[1024,512]{1,0:T(8,128)(2,1)S(1)} %collective-permute-done.18.refs_6_.refs_21_), channel_id=1, source_target_pairs={{0,1},{1,0},{2,3},{3,2},{4,5},{5,4},{6,7},{7,6},{8,9},{9,8},{10,11... | collective-permute-start | bytes 3145736 | tf_op jit(solution)/shard_map/ppermute | solution.py:33
  154.8 13.8 %collective-permute-start.8 = (bf16[256,1024]{1,0:T(8,128)(2,1)}, bf16[256,1024]{1,0:T(8,128)(2,1)S(1)}, u32[]{:S(2)}, u32[]{:S(2)}) collective-permute-start(bf16[256,1024]{1,0:T(8,128)(2,1)} %copy-done.80), channel_id=1, source_target_pairs={{0,2},{2,0},{1,3},{3,1},{4,6},{6,4},{5,7},{7,5},{8,10},{10,8},{9,1... | collective-permute-start | bytes 1572872 | tf_op jit(solution)/shard_map/ppermute | solution.py:37
  157.2 45.0 %collective-permute-start.29 = (bf16[1024,384]{1,0:T(8,128)(2,1)S(1)}, bf16[1024,384]{1,0:T(8,128)(2,1)}, u32[]{:S(2)}, u32[]{:S(2)}) collective-permute-start(bf16[1024,384]{1,0:T(8,128)(2,1)S(1)} %slice.124.refs_8_.refs_6_.refs_7_.refs_23_), channel_id=1, source_target_pairs={{0,4},{4,0},{1,5},{5,1},{2,6},{6,2},{3,7},{7,3},{8,12},{12,8},{9,1... | collective-permute-start | bytes 2359304 | tf_op jit(solution)/shard_map/ppermute | solution.py:41
  182.4 16.8 %collective-permute-start.22 = (bf16[256,768]{1,0:T(8,128)(2,1)S(1)}, bf16[256,768]{1,0:T(8,128)(2,1)S(1)}, u32[]{:S(2)}, u32[]{:S(2)}) collective-permute-start(bf16[256,768]{1,0:T(8,128)(2,1)S(1)} %get-tuple-element.109), channel_id=1, source_target_pairs={{0,6},{1,7},{2,4},{3,5},{4,2},{5,3},{6,0},{7,1},{8,14},{9,15},{10,... | collective-permute-start | bytes 1179656 | tf_op jit(solution)/shard_map/ppermute | solution.py:45
  199.9 66.0 %collective-permute-start.36 = (bf16[1024,1024]{1,0:T(8,128)(2,1)}, bf16[1024,1024]{1,0:T(8,128)(2,1)S(1)}, u32[]{:S(2)}, u32[]{:S(2)}) collective-permute-start(bf16[1024,1024]{1,0:T(8,128)(2,1)} %all-gather.16.cloned.1.call-done.refs_3_.refs_7_.refs_8_.refs_12_), channel_id=1, source_target_pairs={{0,4},{4,0},{1,5},{5,1},{2,6},{6,2},{3,7},{7,3},{8,12},{12,8},{9,1... | collective-permute-start | bytes 6291464 | tf_op jit(solution)/shard_map/ppermute | solution.py:41
  201.1 24.1 %collective-permute-start.27 = (bf16[1024,384]{1,0:T(8,128)(2,1)S(1)}, bf16[1024,384]{1,0:T(8,128)(2,1)}, u32[]{:S(2)}, u32[]{:S(2)}) collective-permute-start(bf16[1024,384]{1,0:T(8,128)(2,1)S(1)} %slice.124.refs_8_.refs_6_.refs_7_.refs_23_), channel_id=1, source_target_pairs={{0,2},{2,0},{1,3},{3,1},{4,6},{6,4},{5,7},{7,5},{8,10},{10,8},{9,1... | collective-permute-start | bytes 2359304 | tf_op jit(solution)/shard_map/ppermute | solution.py:37
  202.3 32.6 %collective-permute-start.31 = (bf16[1024,384]{1,0:T(8,128)(2,1)}, bf16[1024,384]{1,0:T(8,128)(2,1)}, u32[]{:S(2)}, u32[]{:S(2)}) collective-permute-start(bf16[1024,384]{1,0:T(8,128)(2,1)} %collective-permute-done.29.refs_12_.refs_10_.refs_11_.refs_27_), channel_id=1, source_target_pairs={{0,2},{2,0},{1,3},{3,1},{4,6},{6,4},{5,7},{7,5},{8,10},{10,8},{9,1... | collective-permute-start | bytes 2359304 | tf_op jit(solution)/shard_map/ppermute | solution.py:37
  223.7 15.8 %collective-permute-start.23 = (bf16[256,256]{1,0:T(8,128)(2,1)S(1)}, bf16[256,256]{1,0:T(8,128)(2,1)S(1)}, u32[]{:S(2)}, u32[]{:S(2)}) collective-permute-start(bf16[256,256]{1,0:T(8,128)(2,1)S(1)} %get-tuple-element.203), channel_id=1, source_target_pairs={{0,2},{2,0},{1,3},{3,1},{4,6},{6,4},{5,7},{7,5},{8,10},{10,8},{9,1... | collective-permute-start | bytes 393224 | tf_op jit(solution)/shard_map/ppermute | solution.py:37
  224.9 23.2 %collective-permute-start.24 = (bf16[256,256]{1,0:T(8,128)(2,1)S(1)}, bf16[256,256]{1,0:T(8,128)(2,1)S(1)}, u32[]{:S(2)}, u32[]{:S(2)}) collective-permute-start(bf16[256,256]{1,0:T(8,128)(2,1)S(1)} %get-tuple-element.202), channel_id=1, source_target_pairs={{0,4},{4,0},{1,5},{5,1},{2,6},{6,2},{3,7},{7,3},{8,12},{12,8},{9,1... | collective-permute-start | bytes 393224 | tf_op jit(solution)/shard_map/ppermute | solution.py:41
  225.2 27.2 %collective-permute-start.25 = (bf16[256,256]{1,0:T(8,128)(2,1)S(1)}, bf16[256,256]{1,0:T(8,128)(2,1)S(1)}, u32[]{:S(2)}, u32[]{:S(2)}) collective-permute-start(bf16[256,256]{1,0:T(8,128)(2,1)S(1)} %get-tuple-element.201), channel_id=1, source_target_pairs={{0,6},{1,7},{2,4},{3,5},{4,2},{5,3},{6,0},{7,1},{8,14},{9,15},{10,... | collective-permute-start | bytes 393224 | tf_op jit(solution)/shard_map/ppermute | solution.py:45
  234.8 19.8 %collective-permute-start.26 = (bf16[1024,384]{1,0:T(8,128)(2,1)S(1)}, bf16[1024,384]{1,0:T(8,128)(2,1)S(1)}, u32[]{:S(2)}, u32[]{:S(2)}) collective-permute-start(bf16[1024,384]{1,0:T(8,128)(2,1)S(1)} %slice.124.refs_8_.refs_6_.refs_7_.refs_23_), channel_id=1, source_target_pairs={{0,1},{1,0},{2,3},{3,2},{4,5},{5,4},{6,7},{7,6},{8,9},{9,8},{10,11... | collective-permute-start | bytes 2359304 | tf_op jit(solution)/shard_map/ppermute | solution.py:33
  239.4 15.4 %collective-permute-start.28 = (bf16[1024,384]{1,0:T(8,128)(2,1)}, bf16[1024,384]{1,0:T(8,128)(2,1)S(1)}, u32[]{:S(2)}, u32[]{:S(2)}) collective-permute-start(bf16[1024,384]{1,0:T(8,128)(2,1)} %collective-permute-done.27.refs_10_.refs_8_.refs_9_.refs_25_), channel_id=1, source_target_pairs={{0,1},{1,0},{2,3},{3,2},{4,5},{5,4},{6,7},{7,6},{8,9},{9,8},{10,11... | collective-permute-start | bytes 2359304 | tf_op jit(solution)/shard_map/ppermute | solution.py:33
  254.7 39.0 %collective-permute-start.35 = (bf16[1024,1024]{1,0:T(8,128)(2,1)S(1)}, bf16[1024,1024]{1,0:T(8,128)(2,1)S(1)}, u32[]{:S(2)}, u32[]{:S(2)}) collective-permute-start(bf16[1024,1024]{1,0:T(8,128)(2,1)S(1)} %copy-done.2), channel_id=1, source_target_pairs={{0,1},{1,0},{2,3},{3,2},{4,5},{5,4},{6,7},{7,6},{8,9},{9,8},{10,11... | collective-permute-start | bytes 6291464 | tf_op jit(solution)/shard_map/ppermute | solution.py:33
  265.9 27.7 %collective-permute-start.37 = (bf16[1024,1024]{1,0:T(8,128)(2,1)S(1)}, bf16[1024,1024]{1,0:T(8,128)(2,1)}, u32[]{:S(2)}, u32[]{:S(2)}) collective-permute-start(bf16[1024,1024]{1,0:T(8,128)(2,1)S(1)} %collective-permute-done.36.refs_5_.refs_9_.refs_10_.refs_14_), channel_id=1, source_target_pairs={{0,1},{1,0},{2,3},{3,2},{4,5},{5,4},{6,7},{7,6},{8,9},{9,8},{10,11... | collective-permute-start | bytes 6291464 | tf_op jit(solution)/shard_map/ppermute | solution.py:33
  280.1 13.5 %collective-permute-start.34 = (bf16[256,1024]{1,0:T(8,128)(2,1)S(1)}, bf16[256,1024]{1,0:T(8,128)(2,1)S(1)}, u32[]{:S(2)}, u32[]{:S(2)}) collective-permute-start(bf16[256,1024]{1,0:T(8,128)(2,1)S(1)} %get-tuple-element.125.refs_1_.refs_3_), channel_id=1, source_target_pairs={{0,2},{2,0},{1,3},{3,1},{4,6},{6,4},{5,7},{7,5},{8,10},{10,8},{9,1... | collective-permute-start | bytes 1572872 | tf_op jit(solution)/shard_map/ppermute | solution.py:37
  304.9 11.9 %collective-permute-start.38 = (bf16[256,1024]{1,0:T(8,128)(2,1)S(1)}, bf16[256,1024]{1,0:T(8,128)(2,1)S(1)}, u32[]{:S(2)}, u32[]{:S(2)}) collective-permute-start(bf16[256,1024]{1,0:T(8,128)(2,1)S(1)} %get-tuple-element.131), channel_id=1, source_target_pairs={{0,2},{2,0},{1,3},{3,1},{4,6},{6,4},{5,7},{7,5},{8,10},{10,8},{9,1... | collective-permute-start | bytes 1572872 | tf_op jit(solution)/shard_map/ppermute | solution.py:37
  343.6 18.1 %collective-permute-start.68 = (f32[12,32,128]{2,1,0:T(8,128)S(1)}, f32[12,32,128]{2,1,0:T(8,128)S(1)}, u32[]{:S(2)}, u32[]{:S(2)}) collective-permute-start(f32[12,32,128]{2,1,0:T(8,128)S(1)} %slice_bitcast_fusion.5), channel_id=1, source_target_pairs={{0,4},{4,0},{1,5},{5,1},{2,6},{6,2},{3,7},{7,3},{8,12},{12,8},{9,1... | collective-permute-start | bytes 589832 | tf_op jit(solution)/shard_map/ppermute | solution.py:41
  361.8 17.4 %collective-permute-start.69 = (f32[2,32,128]{2,1,0:T(8,128)S(1)}, f32[2,32,128]{2,1,0:T(8,128)S(1)}, u32[]{:S(2)}, u32[]{:S(2)}) collective-permute-start(f32[2,32,128]{2,1,0:T(8,128)S(1)} %slice.137), channel_id=1, source_target_pairs={{0,2},{2,0},{1,3},{3,1},{4,6},{6,4},{5,7},{7,5},{8,10},{10,8},{9,1... | collective-permute-start | bytes 98312 | tf_op jit(solution)/shard_map/ppermute | solution.py:37
  379.9 154.0 %all-gather.18.cloned.1.call-start = ((), (), s32[]{:S(2)}) async-start(), calls=%async_computation.5 | async-start | bytes 3514368 | tf_op jit(solution)/shard_map/all_gather | solution.py:1271
  420.6 13.3 %collective-permute-start.47 = (bf16[256,768]{1,0:T(8,128)(2,1)S(1)}, bf16[256,768]{1,0:T(8,128)(2,1)S(1)}, u32[]{:S(2)}, u32[]{:S(2)}) collective-permute-start(bf16[256,768]{1,0:T(8,128)(2,1)S(1)} %get-tuple-element.190), channel_id=1, source_target_pairs={{0,2},{2,0},{1,3},{3,1},{4,6},{6,4},{5,7},{7,5},{8,10},{10,8},{9,1... | collective-permute-start | bytes 1179656 | tf_op jit(solution)/shard_map/ppermute | solution.py:37
  422.1 11.8 %collective-permute-start.48 = (bf16[256,768]{1,0:T(8,128)(2,1)S(1)}, bf16[256,768]{1,0:T(8,128)(2,1)S(1)}, u32[]{:S(2)}, u32[]{:S(2)}) collective-permute-start(bf16[256,768]{1,0:T(8,128)(2,1)S(1)} %get-tuple-element.189), channel_id=1, source_target_pairs={{0,4},{4,0},{1,5},{5,1},{2,6},{6,2},{3,7},{7,3},{8,12},{12,8},{9,1... | collective-permute-start | bytes 1179656 | tf_op jit(solution)/shard_map/ppermute | solution.py:41
  422.4 17.4 %collective-permute-start.49 = (bf16[256,768]{1,0:T(8,128)(2,1)S(1)}, bf16[256,768]{1,0:T(8,128)(2,1)S(1)}, u32[]{:S(2)}, u32[]{:S(2)}) collective-permute-start(bf16[256,768]{1,0:T(8,128)(2,1)S(1)} %get-tuple-element.188), channel_id=1, source_target_pairs={{0,6},{1,7},{2,4},{3,5},{4,2},{5,3},{6,0},{7,1},{8,14},{9,15},{10,... | collective-permute-start | bytes 1179656 | tf_op jit(solution)/shard_map/ppermute | solution.py:45
  494.8 21.7 %collective-permute-start.60 = (bf16[4,10,32,128]{3,2,1,0:T(8,128)(2,1)S(1)}, bf16[4,10,32,128]{3,2,1,0:T(8,128)(2,1)S(1)}, u32[]{:S(2)}, u32[]{:S(2)}) collective-permute-start(bf16[4,10,32,128]{3,2,1,0:T(8,128)(2,1)S(1)} %pad_maximum_fusion.1.refs_3_), channel_id=1, source_target_pairs={{0,2},{2,0},{1,3},{3,1},{4,6},{6,4},{5,7},{7,5},{8,10},{10,8},{9,1... | collective-permute-start | bytes 983048 | tf_op jit(solution)/shard_map/ppermute | solution.py:37
  500.6 22.5 %collective-permute-start.64 = (bf16[4,10,32,128]{3,2,1,0:T(8,128)(2,1)S(1)}, bf16[4,10,32,128]{3,2,1,0:T(8,128)(2,1)S(1)}, u32[]{:S(2)}, u32[]{:S(2)}) collective-permute-start(bf16[4,10,32,128]{3,2,1,0:T(8,128)(2,1)S(1)} %collective-permute-done.62.refs_7_), channel_id=1, source_target_pairs={{0,2},{2,0},{1,3},{3,1},{4,6},{6,4},{5,7},{7,5},{8,10},{10,8},{9,1... | collective-permute-start | bytes 983048 | tf_op jit(solution)/shard_map/ppermute | solution.py:37
  503.3 23.6 %collective-permute-start.53 = (bf16[1,512,256]{2,1,0:T(8,128)(2,1)}, bf16[1,512,256]{2,1,0:T(8,128)(2,1)}, u32[]{:S(2)}, u32[]{:S(2)}) collective-permute-start(bf16[1,512,256]{2,1,0:T(8,128)(2,1)} %get-tuple-element.194), channel_id=1, source_target_pairs={{0,1},{1,0},{2,3},{3,2},{4,5},{5,4},{6,7},{7,6},{8,9},{9,8},{10,11... | collective-permute-start | bytes 786440 | tf_op jit(solution)/shard_map/ppermute | solution.py:33
  515.9 23.8 %collective-permute-start.59 = (bf16[4,10,32,128]{3,2,1,0:T(8,128)(2,1)S(1)}, bf16[4,10,32,128]{3,2,1,0:T(8,128)(2,1)S(1)}, u32[]{:S(2)}, u32[]{:S(2)}) collective-permute-start(bf16[4,10,32,128]{3,2,1,0:T(8,128)(2,1)S(1)} %pad_maximum_fusion.1.refs_3_), channel_id=1, source_target_pairs={{0,1},{1,0},{2,3},{3,2},{4,5},{5,4},{6,7},{7,6},{8,9},{9,8},{10,11... | collective-permute-start | bytes 983048 | tf_op jit(solution)/shard_map/ppermute | solution.py:33
  515.9 23.8 %collective-permute-start.63 = (bf16[4,10,32,128]{3,2,1,0:T(8,128)(2,1)S(1)}, bf16[4,10,32,128]{3,2,1,0:T(8,128)(2,1)S(1)}, u32[]{:S(2)}, u32[]{:S(2)}) collective-permute-start(bf16[4,10,32,128]{3,2,1,0:T(8,128)(2,1)S(1)} %collective-permute-done.62.refs_7_), channel_id=1, source_target_pairs={{0,1},{1,0},{2,3},{3,2},{4,5},{5,4},{6,7},{7,6},{8,9},{9,8},{10,11... | collective-permute-start | bytes 983048 | tf_op jit(solution)/shard_map/ppermute | solution.py:33
  516.4 23.3 %collective-permute-start.61 = (bf16[4,10,32,128]{3,2,1,0:T(8,128)(2,1)S(1)}, bf16[4,10,32,128]{3,2,1,0:T(8,128)(2,1)S(1)}, u32[]{:S(2)}, u32[]{:S(2)}) collective-permute-start(bf16[4,10,32,128]{3,2,1,0:T(8,128)(2,1)S(1)} %collective-permute-done.60.refs_5_), channel_id=1, source_target_pairs={{0,1},{1,0},{2,3},{3,2},{4,5},{5,4},{6,7},{7,6},{8,9},{9,8},{10,11... | collective-permute-start | bytes 983048 | tf_op jit(solution)/shard_map/ppermute | solution.py:33
  523.1 16.6 %collective-permute-start.65 = (bf16[4,10,32,128]{3,2,1,0:T(8,128)(2,1)S(1)}, bf16[4,10,32,128]{3,2,1,0:T(8,128)(2,1)S(1)}, u32[]{:S(2)}, u32[]{:S(2)}) collective-permute-start(bf16[4,10,32,128]{3,2,1,0:T(8,128)(2,1)S(1)} %collective-permute-done.64.refs_9_), channel_id=1, source_target_pairs={{0,1},{1,0},{2,3},{3,2},{4,5},{5,4},{6,7},{7,6},{8,9},{9,8},{10,11... | collective-permute-start | bytes 983048 | tf_op jit(solution)/shard_map/ppermute | solution.py:33
  (140 other events, 2018.9 us)
Sparse Core Ops, SparseCore 0:
  10.2 29.7 all-gather.7
  42.2 27.5 all-gather.9
  72.0 27.4 all-gather.11
  101.4 27.4 all-gather.13
  130.9 45.5 all-gather.15
  380.0 67.3 all-gather.19
  461.5 68.4 all-gather.17

commit v3 on v2

--- a/solution.py
+++ b/solution.py
@@ -1357,15 +1357,16 @@
     )
     kept_one = (rows_own, rows_next, (pre, t_in, t_out))
     base_two = gathered(after(local, (base_convs, heads_side, heads_pair, heads_core, send)))
+    other = by_pair(send)
     heads_far = by_side(heads_pair)
     heads = [base_heads, heads_core, heads_pair, by_core(heads_pair)]
-    heads += [heads_side, by_core(heads_side), heads_far, by_core(heads_far)]
+    heads += [heads_side, by_core(heads_side), heads_far, by_core(after(heads_far, other))]
     base_convs = base_convs[:, :step]
     convs_pair = by_pair(after(base_convs, heads_pair))
     convs_side = by_side(after(base_convs, heads_far))
 
     first, slots, t_heads = heads_forward(
-        where, own.astype(F32), part, by_pair(send), heads, adapt_down, adapt_up
+        where, own.astype(F32), part, other, heads, adapt_down, adapt_up
     )
     slots = exchanged(slots)
     convs_far = by_pair(after(convs_side, tuple(slots)))

time: 560 us -> 553 us (0.988)
    ppermute x14, waiting for transfers between devices: 74.3 us -> 67.4 us  [by_side(): return lax.ppermute(value, 'ctx', SIDE)]
  transfers between devices with their start and end apart: 77 -> 77, of which waited for: 36 -> 38; matrix products, arithmetic and copies ran while one was open for 5% -> 5% of each run, Pallas kernels for 22% -> 22%
where the time goes in v3:
time: 553 us; the launch traced here: 543 us
  waiting for transfers between devices  201 us (36%)
  Pallas kernels  148 us (27%)
  starting transfers between devices  99.1 us (18%)
  local copies, waits for them, and re-layouts  56.6 us (10%)
  between operations  16.7 us (3%)
  other arithmetic  13 us (2%)
  blocking collectives  7.87 us (1%)
    ppermute x24, waiting for transfers between devices, by_pair(): return lax.ppermute(value, 'tp', PAIR)  96.3 us
    pallas_call x13, Pallas kernels, run(): pl.pallas_call(body, name=name, in_specs=specs, out_specs=out_specs or [V...  93.7 us
    ppermute x14, waiting for transfers between devices, by_side(): return lax.ppermute(value, 'ctx', SIDE)  67.4 us
    ppermute x23, starting transfers between devices, by_core(): return lax.ppermute(value, 'tp', CORE)  48.1 us
    unnamed x226, local copies, waits for them, and re-layouts  43 us
    pallas_call x1, Pallas kernels, attend_back(): pl.pallas_call(bwd_kernel, grid_spec=pltpu.PrefetchScalarGridSpec(num_sca...  29.2 us
    ppermute x24, starting transfers between devices, by_pair(): return lax.ppermute(value, 'tp', PAIR)  23.6 us
    ppermute x4, waiting for transfers between devices, across(): return lax.ppermute(value, ('ctx', 'tp'), ACROSS)  15 us
  transfers between devices with their start and end apart: 77, of which 38 were waited for; matrix products, arithmetic and copies ran while one was open for 5% of the time, Pallas kernels for 22%

profile of v3, /device:TPU:1, one launch (start us, length us, event | category | flops | bytes accessed | tf_op | source)
XLA Modules:
  0.0 543.2 jit_solution(12929595021833393747)
XLA Ops:
  12.3 7.9 %all-reduce = s32[8]{0:T(128)S(1)} all-reduce(s32[8]{0:T(128)S(1)} %dynamic-update-slice), channel_id=1, replica_groups=mesh['shard'=4,'ctx'=2,'tp'=4] {'shard'}, use_global_device_ids=true, to_apply=%add | all-reduce | flops 8 | bytes 64
  25.3 9.2 %collective-permute-done.1 = bf16[512,512]{1,0:T(8,128)(2,1)S(1)} collective-permute-done((bf16[512,512]{1,0:T(8,128)(2,1)S(1)}, bf16[512,512]{1,0:T(8,128)(2,1)S(1)}, u32[]{:S(2)}, u32[]{:S(2)}) %collective-permute-start.1) | collective-permute-done | bytes 524320 | tf_op jit(solution)/shard_map/ppermute | solution.py:37
  48.1 7.1 %collective-permute-done.12 = bf16[256,512]{1,0:T(8,128)(2,1)S(1)} collective-permute-done((bf16[256,512]{1,0:T(8,128)(2,1)S(1)}, bf16[256,512]{1,0:T(8,128)(2,1)S(1)}, u32[]{:S(2)}, u32[]{:S(2)}) %collective-permute-start.12) | collective-permute-done | bytes 262176 | tf_op jit(solution)/shard_map/ppermute | solution.py:37
  56.1 12.5 %collective-permute-done.3.refs_5_.refs_10_ = bf16[1024,512]{1,0:T(8,128)(2,1)} collective-permute-done((bf16[1024,512]{1,0:T(8,128)(2,1)}, bf16[1024,512]{1,0:T(8,128)(2,1)}, u32[]{:S(2)}, u32[]{:S(2)}) %collective-permute-start.3) | collective-permute-done | bytes 1048608 | tf_op jit(solution)/shard_map/ppermute | solution.py:41
  75.0 20.5 %collective-permute-done.6.refs_9_.refs_14_ = bf16[1024,512]{1,0:T(8,128)(2,1)} collective-permute-done((bf16[1024,512]{1,0:T(8,128)(2,1)}, bf16[1024,512]{1,0:T(8,128)(2,1)}, u32[]{:S(2)}, u32[]{:S(2)}) %collective-permute-start.6) | collective-permute-done | bytes 1048608 | tf_op jit(solution)/shard_map/ppermute | solution.py:41
  95.5 4.0 all-gather.12.cloned.1.call-done.refs_0_.refs_15_
  108.3 11.2 %hidden_forward.2 = (f32[256,1024]{1,0:T(8,128)S(1)}, bf16[256,1024]{1,0:T(8,128)(2,1)S(1)}, f32[4,512,512]{2,1,0:T(8,128)}, bf16[512,128]{1,0:T(8,128)(2,1)S(1)}, bf16[512,128]{1,0:T(8,128)(2,1)S(1)}) custom-call(s32[4]{0:T(128)S(1)} %pad_add_fusion.where.refs_0_, bf16[256,1024]{1,0:T(8,128)(2,1)S(1)} %get-tuple-element.97.refs_1_.refs_3_, ...), custom_call_target="tpu_custom_call" | custom-call | flops 4294967296 | bytes 16777216 | tf_op jit(solution)/shard_map/hidden_forward/pallas_call | solution.py:320
  122.0 3.1 collective-permute-done.14.refs_2_.refs_17_
  126.0 2.9 all-gather.14.cloned.1.call-done
  132.8 10.1 %collective-permute-done.8.other = bf16[256,1024]{1,0:T(8,128)(2,1)S(1)} collective-permute-done((bf16[256,1024]{1,0:T(8,128)(2,1)}, bf16[256,1024]{1,0:T(8,128)(2,1)S(1)}, u32[]{:S(2)}, u32[]{:S(2)}) %collective-permute-start.8) | collective-permute-done | bytes 524320 | tf_op jit(solution)/shard_map/ppermute | solution.py:37
  142.9 10.3 %collective-permute-done.18.refs_6_.refs_21_ = bf16[1024,512]{1,0:T(8,128)(2,1)S(1)} collective-permute-done((bf16[1024,512]{1,0:T(8,128)(2,1)}, bf16[1024,512]{1,0:T(8,128)(2,1)S(1)}, u32[]{:S(2)}, u32[]{:S(2)}) %collective-permute-start.18) | collective-permute-done | bytes 1048608 | tf_op jit(solution)/shard_map/ppermute | solution.py:41
  159.9 6.3 %heads_forward.1 = (f32[256,1024]{1,0:T(8,128)S(1)}, bf16[256,768]{1,0:T(8,128)(2,1)S(1)}, bf16[256,768]{1,0:T(8,128)(2,1)S(1)}, bf16[256,768]{1,0:T(8,128)(2,1)...) custom-call(s32[4]{0:T(128)S(1)} %pad_add_fusion.where.refs_0_, f32[256,1024]{1,0:T(8,128)S(1)} %copy-done.17, ...), custom_call_target="tpu_custom_call" | custom-call | flops 1610612736 | bytes 16777216 | tf_op jit(solution)/shard_map/heads_forward/pallas_call | solution.py:320
  171.3 7.3 %collective-permute-done.20.s1 = bf16[256,768]{1,0:T(8,128)(2,1)S(1)} collective-permute-done((bf16[256,768]{1,0:T(8,128)(2,1)S(1)}, bf16[256,768]{1,0:T(8,128)(2,1)S(1)}, u32[]{:S(2)}, u32[]{:S(2)}) %collective-permute-start.20) | collective-permute-done | bytes 393248 | tf_op jit(solution)/shard_map/ppermute | solution.py:37
  179.4 3.9 collective-permute-done.21.s2
  184.0 8.6 %collective-permute-done.22.s3 = bf16[256,768]{1,0:T(8,128)(2,1)S(1)} collective-permute-done((bf16[256,768]{1,0:T(8,128)(2,1)S(1)}, bf16[256,768]{1,0:T(8,128)(2,1)S(1)}, u32[]{:S(2)}, u32[]{:S(2)}) %collective-permute-start.22) | collective-permute-done | bytes 393248 | tf_op jit(solution)/shard_map/ppermute | solution.py:45
  200.9 14.8 %attend.1 = (bf16[4,256,256]{2,1,0:T(8,128)(2,1)S(1)}, f32[4,1024,1]{2,1,0:T(8,128)S(1)}) custom-call(s32[1]{0:T(128)} %bitcast.14.b_ref, bf16[256,768]{1,0:T(8,128)(2,1)S(1)} %copy-done.82, bf16[256,768]{1,0:T(8,128)(2,1)S(1)} %copy-done.85, bf16[256,768]{1,0:T(8,128)(2,1)S(1)} %copy-done.88, bf16[256,768]{1,0:T(8,128)(2,1)S(1)} %copy-done.91, ...), custom_call_target="tpu_custom_call" | custom-call | flops 1073741824 | bytes 2097152 | tf_op jit(solution)/shard_map/attend/pallas_call | solution.py:112
  219.8 9.2 %collective-permute-done.31.refs_14_.refs_12_.refs_13_.refs_29_ = bf16[1024,384]{1,0:T(8,128)(2,1)} collective-permute-done((bf16[1024,384]{1,0:T(8,128)(2,1)}, bf16[1024,384]{1,0:T(8,128)(2,1)}, u32[]{:S(2)}, u32[]{:S(2)}) %collective-permute-start.31) | collective-permute-done | bytes 786464 | tf_op jit(solution)/shard_map/ppermute | solution.py:37
  229.0 3.8 collective-permute-start.26
  234.2 8.1 %collective-permute-done.24.m2.refs_12_ = bf16[256,256]{1,0:T(8,128)(2,1)S(1)} collective-permute-done((bf16[256,256]{1,0:T(8,128)(2,1)S(1)}, bf16[256,256]{1,0:T(8,128)(2,1)S(1)}, u32[]{:S(2)}, u32[]{:S(2)}) %collective-permute-start.24) | collective-permute-done | bytes 131104 | tf_op jit(solution)/shard_map/ppermute | solution.py:41
  242.3 3.6 collective-permute-start.30
  249.5 6.8 %pair_forward.1 = (f32[256,1024]{1,0:T(8,128)S(1)}, f32[256,1024]{1,0:T(8,128)S(1)}, f32[256,1024]{1,0:T(8,128)S(1)}, f32[2,2,32,256]{3,2,1,0:T(8,128)S(1)}, bf1...) custom-call(s32[4]{0:T(128)S(1)} %pad_add_fusion.where.refs_0_, f32[256,1024]{1,0:T(8,128)} %copy-done.15, ...), custom_call_target="tpu_custom_call" | custom-call | flops 1610612736 | bytes 16777216 | tf_op jit(solution)/shard_map/pair_forward/pallas_call | solution.py:320
  258.9 3.3 collective-permute-start.33
  262.2 2.5 collective-permute-done.33.refs_4_
  264.8 6.8 %conv_forward.1 = (f32[256,1024]{1,0:T(8,128)S(1)}, f32[256,1024]{1,0:T(8,128)S(1)}, bf16[256,1024]{1,0:T(8,128)(2,1)S(1)}, bf16[256,128]{1,0:T(8,128)(2,1)S(1)}) custom-call(s32[4]{0:T(128)S(1)} %pad_add_fusion.where.refs_0_, f32[256,1024]{1,0:T(8,128)S(1)} %get-tuple-element.122.refs_1_.refs_7_, f32[256,1024]{1,0:T(8,128)} %copy-done.21, ...), custom_call_target="tpu_custom_call" | custom-call | flops 536870912 | bytes 16777216 | tf_op jit(solution)/shard_map/conv_forward/pallas_call | solution.py:320
  275.8 11.3 %collective-permute-done.34.refs_2_.refs_4_ = bf16[256,1024]{1,0:T(8,128)(2,1)S(1)} collective-permute-done((bf16[256,1024]{1,0:T(8,128)(2,1)S(1)}, bf16[256,1024]{1,0:T(8,128)(2,1)S(1)}, u32[]{:S(2)}, u32[]{:S(2)}) %collective-permute-start.34) | collective-permute-done | bytes 524320 | tf_op jit(solution)/shard_map/ppermute | solution.py:37
  287.2 11.1 %hidden_forward.3 = (f32[256,1024]{1,0:T(8,128)S(1)}, bf16[256,1024]{1,0:T(8,128)(2,1)S(1)}, f32[4,512,512]{2,1,0:T(8,128)}, bf16[512,128]{1,0:T(8,128)(2,1)S(1)}, bf16[512,128]{1,0:T(8,128)(2,1)S(1)}) custom-call(s32[4]{0:T(128)S(1)} %pad_add_fusion.where.refs_0_, bf16[256,1024]{1,0:T(8,128)(2,1)S(1)} %get-tuple-element.127.refs_1_.refs_3_, ...), custom_call_target="tpu_custom_call" | custom-call | flops 4294967296 | bytes 16777216 | tf_op jit(solution)/shard_map/hidden_forward/pallas_call | solution.py:320
  299.6 10.7 %collective-permute-done.38.other = bf16[256,1024]{1,0:T(8,128)(2,1)S(1)} collective-permute-done((bf16[256,1024]{1,0:T(8,128)(2,1)S(1)}, bf16[256,1024]{1,0:T(8,128)(2,1)S(1)}, u32[]{:S(2)}, u32[]{:S(2)}) %collective-permute-start.38) | collective-permute-done | bytes 524320 | tf_op jit(solution)/shard_map/ppermute | solution.py:37
  313.2 10.1 %collective-permute-done.41.refs_2_ = bf16[256,1024]{1,0:T(8,128)(2,1)S(1)} collective-permute-done((bf16[256,1024]{1,0:T(8,128)(2,1)S(1)}, bf16[256,1024]{1,0:T(8,128)(2,1)S(1)}, u32[]{:S(2)}, u32[]{:S(2)}) %collective-permute-start.41) | collective-permute-done | bytes 524320 | tf_op jit(solution)/shard_map/ppermute | solution.py:37
  323.3 12.2 %hidden_backward.2 = (f32[256,1024]{1,0:T(8,128)S(1)}, bf16[256,1024]{1,0:T(8,128)(2,1)S(1)}, f32[2,12,32,128]{3,2,1,0:T(8,128)S(1)}) custom-call(s32[4]{0:T(128)S(1)} %pad_add_fusion.where.refs_0_, bf16[256,1024]{1,0:T(8,128)(2,1)S(1)} %get-tuple-element.137.refs_1_, bf16[256,1024]{1,0:T(8,128)(2,1)S(1)} %collective-permute-done.41.refs_2_, ...), custom_call_target="tpu_custom_call" | custom-call | flops 4294967296 | bytes 16777216 | tf_op jit(solution)/shard_map/hidden_backward/pallas_call | solution.py:320
  338.3 8.2 %collective-permute-done.42.refs_3_ = bf16[256,1024]{1,0:T(8,128)(2,1)S(1)} collective-permute-done((bf16[256,1024]{1,0:T(8,128)(2,1)S(1)}, bf16[256,1024]{1,0:T(8,128)(2,1)S(1)}, u32[]{:S(2)}, u32[]{:S(2)}) %collective-permute-start.42) | collective-permute-done | bytes 524320 | tf_op jit(solution)/shard_map/ppermute | solution.py:37
  346.6 5.1 conv_backward.1
  359.5 11.2 %pair_backward.1 = (f32[256,1024]{1,0:T(8,128)}, bf16[256,256]{1,0:T(8,128)(2,1)S(1)}, bf16[256,256]{1,0:T(8,128)(2,1)S(1)}, bf16[256,256]{1,0:T(8,128)(2,1)S(1)...) custom-call(s32[4]{0:T(128)S(1)} %pad_add_fusion.where.refs_0_, ...), custom_call_target="tpu_custom_call" | custom-call | flops 1610612736 | bytes 16777216 | tf_op jit(solution)/shard_map/pair_backward/pallas_call | solution.py:320
  384.3 29.2 %attend_back.1 = bf16[4,256,768]{2,1,0:T(8,128)(2,1)S(1)} custom-call(s32[1]{0:T(128)} %bitcast.14.b_ref, bf16[256,768]{1,0:T(8,128)(2,1)S(1)} %copy-done.83, bf16[256,768]{1,0:T(8,128)(2,1)S(1)} %copy-done.86, bf16[256,768]{1,0:T(8,128)(2,1)S(1)} %copy-done.89, bf16[256,768]{1,0:T(8,128)(2,1)S(1)} %copy-done.92, ...), custom_call_target="tpu_custom_call" | custom-call | flops 2684354560 | bytes 3670016 | tf_op jit(solution)/shard_map/attend_back/pallas_call | solution.py:184
  416.4 8.0 %collective-permute-start.40 = (bf16[1,512,256]{2,1,0:T(8,128)(2,1)S(1)}, bf16[1,512,256]{2,1,0:T(8,128)(2,1)S(1)}, u32[]{:S(2)}, u32[]{:S(2)}) collective-permute-start(bf16[1,512,256]{2,1,0:T(8,128)(2,1)S(1)} %get-tuple-element.200), channel_id=1, source_target_pairs={{0,1},{1,0},{2,3},{3,2},{4,5},{5,4},{6,7},{7,6},{8,9},{9,8},{10,11... | collective-permute-start | bytes 786440 | tf_op jit(solution)/shard_map/ppermute | solution.py:33
  426.4 6.4 %collective-permute-done.49.g3 = bf16[256,768]{1,0:T(8,128)(2,1)S(1)} collective-permute-done((bf16[256,768]{1,0:T(8,128)(2,1)S(1)}, bf16[256,768]{1,0:T(8,128)(2,1)S(1)}, u32[]{:S(2)}, u32[]{:S(2)}) %collective-permute-start.49) | collective-permute-done | bytes 393248 | tf_op jit(solution)/shard_map/ppermute | solution.py:45
  432.9 7.0 %heads_backward.1 = (f32[256,1024]{1,0:T(8,128)S(1)}, bf16[256,1024]{1,0:T(8,128)(2,1)S(1)}, f32[2,2,2,208,128]{4,3,2,1,0:T(8,128)S(1)}) custom-call(s32[4]{0:T(128)S(1)} %pad_add_fusion.where.refs_0_, f32[256,1024]{1,0:T(8,128)S(1)} %copy-done.44, f32[256,1024]{1,0:T(8,128)S(1)} %copy-done.16, bf16[256,384]{1,0:T(8,128)(2,1)S(1)} %copy-done.69, ...), custom_call_target="tpu_custom_call" | custom-call | flops 1610612736 | bytes 16777216 | tf_op jit(solution)/shard_map/heads_backward/pallas_call | solution.py:320
  443.6 2.3 collective-permute-done.66
  447.5 4.7 collective-permute-done.67
  458.1 12.2 %hidden_backward.3 = (f32[256,1024]{1,0:T(8,128)S(1)}, bf16[256,1024]{1,0:T(8,128)(2,1)S(1)}, f32[2,12,32,128]{3,2,1,0:T(8,128)S(1)}) custom-call(s32[4]{0:T(128)S(1)} %pad_add_fusion.where.refs_0_, bf16[256,1024]{1,0:T(8,128)(2,1)S(1)} %copy-done.61, bf16[256,1024]{1,0:T(8,128)(2,1)S(1)} %copy-done.63, bf16[256,1024]{1,0:T(8,128)(2,1)S(1)} %copy-done.38, ...), custom_call_target="tpu_custom_call" | custom-call | flops 4294967296 | bytes 16777216 | tf_op jit(solution)/shard_map/hidden_backward/pallas_call | solution.py:320
  470.5 3.4 collective-permute-done.54
  480.3 2.8 collective-permute-done.57
  488.2 5.4 collective-permute-done.62.refs_7_
  496.2 12.3 %collective-permute-start.53 = (bf16[1,512,256]{2,1,0:T(8,128)(2,1)}, bf16[1,512,256]{2,1,0:T(8,128)(2,1)}, u32[]{:S(2)}, u32[]{:S(2)}) collective-permute-start(bf16[1,512,256]{2,1,0:T(8,128)(2,1)} %get-tuple-element.196), channel_id=1, source_target_pairs={{0,1},{1,0},{2,3},{3,2},{4,5},{5,4},{6,7},{7,6},{8,9},{9,8},{10,11... | collective-permute-start | bytes 786440 | tf_op jit(solution)/shard_map/ppermute | solution.py:33
  509.0 6.6 %collective-permute-start.61 = (bf16[4,10,32,128]{3,2,1,0:T(8,128)(2,1)S(1)}, bf16[4,10,32,128]{3,2,1,0:T(8,128)(2,1)S(1)}, u32[]{:S(2)}, u32[]{:S(2)}) collective-permute-start(bf16[4,10,32,128]{3,2,1,0:T(8,128)(2,1)S(1)} %collective-permute-done.60.refs_5_), channel_id=1, source_target_pairs={{0,1},{1,0},{2,3},{3,2},{4,5},{5,4},{6,7},{7,6},{8,9},{9,8},{10,11... | collective-permute-start | bytes 983048 | tf_op jit(solution)/shard_map/ppermute | solution.py:33
  515.6 3.5 collective-permute-start.65
  523.3 3.1 expand.2
  528.4 3.8 expand.3
  532.3 3.6 expand_near.1
  (437 shorter events, 148.1 us)
Async XLA Ops:
  7.3 32.8 %all-gather.8.cloned.1.call-start = ((), (), s32[]{:S(2)}) async-start(), calls=%async_computation | async-start | bytes 1310720 | tf_op jit(solution)/shard_map/all_gather | solution.py:1231
  8.5 14.3 %collective-permute-start = (bf16[512,256]{1,0:T(8,128)(2,1)S(1)}, bf16[512,256]{1,0:T(8,128)(2,1)S(1)}, u32[]{:S(2)}, u32[]{:S(2)}) collective-permute-start(bf16[512,256]{1,0:T(8,128)(2,1)S(1)} %get-tuple-element.212), channel_id=1, source_target_pairs={{0,1},{1,0},{2,3},{3,2},{4,5},{5,4},{6,7},{7,6},{8,9},{9,8},{10,11... | collective-permute-start | bytes 786440 | tf_op jit(solution)/shard_map/ppermute | solution.py:33
  9.4 60.4 %all-gather.10.cloned.1.call-start = ((), (), s32[]{:S(2)}) async-start(), calls=%async_computation.1 | async-start | bytes 1310720 | tf_op jit(solution)/shard_map/all_gather | solution.py:1231
  9.5 31.0 %collective-permute-start.9 = (bf16[31,256]{1,0:T(8,128)(2,1)}, bf16[31,256]{1,0:T(8,128)(2,1)}, u32[]{:S(2)}, u32[]{:S(2)}) collective-permute-start(bf16[31,256]{1,0:T(8,128)(2,1)} %param.29), channel_id=1, source_target_pairs={{0,1},{1,0},{2,3},{3,2},{4,5},{5,4},{6,7},{7,6},{8,9},{9,8},{10,11... | collective-permute-start | bytes 47624 | tf_op jit(solution)/shard_map/ppermute | solution.py:33
  10.7 36.5 %collective-permute-start.11 = (bf16[512,256]{1,0:T(8,128)(2,1)}, bf16[512,256]{1,0:T(8,128)(2,1)S(1)}, u32[]{:S(2)}, u32[]{:S(2)}) collective-permute-start(bf16[512,256]{1,0:T(8,128)(2,1)} %get-tuple-element.210), channel_id=1, source_target_pairs={{0,1},{1,0},{2,3},{3,2},{4,5},{5,4},{6,7},{7,6},{8,9},{9,8},{10,11... | collective-permute-start | bytes 786440 | tf_op jit(solution)/shard_map/ppermute | solution.py:33
  23.0 11.5 %collective-permute-start.1 = (bf16[512,512]{1,0:T(8,128)(2,1)S(1)}, bf16[512,512]{1,0:T(8,128)(2,1)S(1)}, u32[]{:S(2)}, u32[]{:S(2)}) collective-permute-start(bf16[512,512]{1,0:T(8,128)(2,1)S(1)} %maximum_select_fusion.1), channel_id=1, source_target_pairs={{0,2},{2,0},{1,3},{3,1},{4,6},{6,4},{5,7},{7,5},{8,10},{10,8},{9,1... | collective-permute-start | bytes 1572872 | tf_op jit(solution)/shard_map/ppermute | solution.py:37
  40.1 59.3 %all-gather.12.cloned.1.call-start = ((), (), s32[]{:S(2)}) async-start(), calls=%async_computation.2 | async-start | bytes 1310720 | tf_op jit(solution)/shard_map/all_gather | solution.py:1231
  42.5 13.6 %collective-permute-start.2 = (bf16[1024,512]{1,0:T(8,128)(2,1)}, bf16[1024,512]{1,0:T(8,128)(2,1)S(1)}, u32[]{:S(2)}, u32[]{:S(2)}) collective-permute-start(bf16[1024,512]{1,0:T(8,128)(2,1)} %all-gather.8.cloned.1.call-done.refs_3_.refs_8_), channel_id=1, source_target_pairs={{0,1},{1,0},{2,3},{3,2},{4,5},{5,4},{6,7},{7,6},{8,9},{9,8},{10,11... | collective-permute-start | bytes 3145736 | tf_op jit(solution)/shard_map/ppermute | solution.py:33
  43.5 25.1 %collective-permute-start.3 = (bf16[1024,512]{1,0:T(8,128)(2,1)}, bf16[1024,512]{1,0:T(8,128)(2,1)}, u32[]{:S(2)}, u32[]{:S(2)}) collective-permute-start(bf16[1024,512]{1,0:T(8,128)(2,1)} %all-gather.8.cloned.1.call-done.refs_3_.refs_8_), channel_id=1, source_target_pairs={{0,4},{4,0},{1,5},{5,1},{2,6},{6,2},{3,7},{7,3},{8,12},{12,8},{9,1... | collective-permute-start | bytes 3145736 | tf_op jit(solution)/shard_map/ppermute | solution.py:41
  69.9 59.0 %all-gather.14.cloned.1.call-start = ((), (), s32[]{:S(2)}) async-start(), calls=%async_computation.3 | async-start | bytes 1310720 | tf_op jit(solution)/shard_map/all_gather | solution.py:1231
  70.9 24.6 %collective-permute-start.6 = (bf16[1024,512]{1,0:T(8,128)(2,1)}, bf16[1024,512]{1,0:T(8,128)(2,1)}, u32[]{:S(2)}, u32[]{:S(2)}) collective-permute-start(bf16[1024,512]{1,0:T(8,128)(2,1)} %all-gather.10.cloned.1.call-done.refs_7_.refs_12_), channel_id=1, source_target_pairs={{0,4},{4,0},{1,5},{5,1},{2,6},{6,2},{3,7},{7,3},{8,12},{12,8},{9,1... | collective-permute-start | bytes 3145736 | tf_op jit(solution)/shard_map/ppermute | solution.py:41
  99.5 93.9 %all-gather.16.cloned.1.call-start = ((), (), s32[]{:S(2)}) async-start(), calls=%async_computation.4 | async-start | bytes 2621440 | tf_op jit(solution)/shard_map/all_gather | solution.py:1231
  100.4 21.6 %collective-permute-start.13 = (bf16[1024,512]{1,0:T(8,128)(2,1)}, bf16[1024,512]{1,0:T(8,128)(2,1)S(1)}, u32[]{:S(2)}, u32[]{:S(2)}) collective-permute-start(bf16[1024,512]{1,0:T(8,128)(2,1)} %all-gather.12.cloned.1.call-done.refs_0_.refs_15_), channel_id=1, source_target_pairs={{0,1},{1,0},{2,3},{3,2},{4,5},{5,4},{6,7},{7,6},{8,9},{9,8},{10,11... | collective-permute-start | bytes 3145736 | tf_op jit(solution)/shard_map/ppermute | solution.py:33
  100.5 24.6 %collective-permute-start.14 = (bf16[1024,512]{1,0:T(8,128)(2,1)}, bf16[1024,512]{1,0:T(8,128)(2,1)}, u32[]{:S(2)}, u32[]{:S(2)}) collective-permute-start(bf16[1024,512]{1,0:T(8,128)(2,1)} %all-gather.12.cloned.1.call-done.refs_0_.refs_15_), channel_id=1, source_target_pairs={{0,2},{2,0},{1,3},{3,1},{4,6},{6,4},{5,7},{7,5},{8,10},{10,8},{9,1... | collective-permute-start | bytes 3145736 | tf_op jit(solution)/shard_map/ppermute | solution.py:37
  101.7 24.3 %collective-permute-start.16 = (bf16[1024,512]{1,0:T(8,128)(2,1)}, bf16[1024,512]{1,0:T(8,128)(2,1)}, u32[]{:S(2)}, u32[]{:S(2)}) collective-permute-start(bf16[1024,512]{1,0:T(8,128)(2,1)} %all-gather.12.cloned.1.call-done.refs_0_.refs_15_), channel_id=1, source_target_pairs={{0,4},{4,0},{1,5},{5,1},{2,6},{6,2},{3,7},{7,3},{8,12},{12,8},{9,1... | collective-permute-start | bytes 3145736 | tf_op jit(solution)/shard_map/ppermute | solution.py:41
  128.9 392.6 %all-gather.20.cloned.1.call-start = ((), (), s32[]{:S(2)}) async-start(), calls=%async_computation.6 | async-start | bytes 2703360 | tf_op jit(solution)/shard_map/all_gather | solution.py:1271
  129.0 24.2 %collective-permute-start.18 = (bf16[1024,512]{1,0:T(8,128)(2,1)}, bf16[1024,512]{1,0:T(8,128)(2,1)S(1)}, u32[]{:S(2)}, u32[]{:S(2)}) collective-permute-start(bf16[1024,512]{1,0:T(8,128)(2,1)} %collective-permute-done.14.refs_2_.refs_17_), channel_id=1, source_target_pairs={{0,4},{4,0},{1,5},{5,1},{2,6},{6,2},{3,7},{7,3},{8,12},{12,8},{9,1... | collective-permute-start | bytes 3145736 | tf_op jit(solution)/shard_map/ppermute | solution.py:41
  130.2 12.6 %collective-permute-start.8 = (bf16[256,1024]{1,0:T(8,128)(2,1)}, bf16[256,1024]{1,0:T(8,128)(2,1)S(1)}, u32[]{:S(2)}, u32[]{:S(2)}) collective-permute-start(bf16[256,1024]{1,0:T(8,128)(2,1)} %copy-done.80), channel_id=1, source_target_pairs={{0,2},{2,0},{1,3},{3,1},{4,6},{6,4},{5,7},{7,5},{8,10},{10,8},{9,1... | collective-permute-start | bytes 1572872 | tf_op jit(solution)/shard_map/ppermute | solution.py:37
  131.4 25.9 %collective-permute-start.15 = (bf16[1024,512]{1,0:T(8,128)(2,1)}, bf16[1024,512]{1,0:T(8,128)(2,1)S(1)}, u32[]{:S(2)}, u32[]{:S(2)}) collective-permute-start(bf16[1024,512]{1,0:T(8,128)(2,1)} %collective-permute-done.14.refs_2_.refs_17_), channel_id=1, source_target_pairs={{0,1},{1,0},{2,3},{3,2},{4,5},{5,4},{6,7},{7,6},{8,9},{9,8},{10,11... | collective-permute-start | bytes 3145736 | tf_op jit(solution)/shard_map/ppermute | solution.py:33
  132.8 24.5 %collective-permute-start.17 = (bf16[1024,512]{1,0:T(8,128)(2,1)}, bf16[1024,512]{1,0:T(8,128)(2,1)S(1)}, u32[]{:S(2)}, u32[]{:S(2)}) collective-permute-start(bf16[1024,512]{1,0:T(8,128)(2,1)} %collective-permute-done.16.refs_4_.refs_19_), channel_id=1, source_target_pairs={{0,1},{1,0},{2,3},{3,2},{4,5},{5,4},{6,7},{7,6},{8,9},{9,8},{10,11... | collective-permute-start | bytes 3145736 | tf_op jit(solution)/shard_map/ppermute | solution.py:33
  156.1 38.8 %collective-permute-start.29 = (bf16[1024,384]{1,0:T(8,128)(2,1)S(1)}, bf16[1024,384]{1,0:T(8,128)(2,1)}, u32[]{:S(2)}, u32[]{:S(2)}) collective-permute-start(bf16[1024,384]{1,0:T(8,128)(2,1)S(1)} %slice.124.refs_8_.refs_6_.refs_7_.refs_23_), channel_id=1, source_target_pairs={{0,4},{4,0},{1,5},{5,1},{2,6},{6,2},{3,7},{7,3},{8,12},{12,8},{9,1... | collective-permute-start | bytes 2359304 | tf_op jit(solution)/shard_map/ppermute | solution.py:41
  169.8 13.4 %collective-permute-start.21 = (bf16[256,768]{1,0:T(8,128)(2,1)S(1)}, bf16[256,768]{1,0:T(8,128)(2,1)S(1)}, u32[]{:S(2)}, u32[]{:S(2)}) collective-permute-start(bf16[256,768]{1,0:T(8,128)(2,1)S(1)} %get-tuple-element.110), channel_id=1, source_target_pairs={{0,4},{4,0},{1,5},{5,1},{2,6},{6,2},{3,7},{7,3},{8,12},{12,8},{9,1... | collective-permute-start | bytes 1179656 | tf_op jit(solution)/shard_map/ppermute | solution.py:41
  170.5 22.1 %collective-permute-start.22 = (bf16[256,768]{1,0:T(8,128)(2,1)S(1)}, bf16[256,768]{1,0:T(8,128)(2,1)S(1)}, u32[]{:S(2)}, u32[]{:S(2)}) collective-permute-start(bf16[256,768]{1,0:T(8,128)(2,1)S(1)} %get-tuple-element.111), channel_id=1, source_target_pairs={{0,6},{1,7},{2,4},{3,5},{4,2},{5,3},{6,0},{7,1},{8,14},{9,15},{10,... | collective-permute-start | bytes 1179656 | tf_op jit(solution)/shard_map/ppermute | solution.py:45
  193.4 65.1 %collective-permute-start.36 = (bf16[1024,1024]{1,0:T(8,128)(2,1)}, bf16[1024,1024]{1,0:T(8,128)(2,1)S(1)}, u32[]{:S(2)}, u32[]{:S(2)}) collective-permute-start(bf16[1024,1024]{1,0:T(8,128)(2,1)} %all-gather.16.cloned.1.call-done.refs_3_.refs_7_.refs_8_.refs_12_), channel_id=1, source_target_pairs={{0,4},{4,0},{1,5},{5,1},{2,6},{6,2},{3,7},{7,3},{8,12},{12,8},{9,1... | collective-permute-start | bytes 6291464 | tf_op jit(solution)/shard_map/ppermute | solution.py:41
  194.6 23.2 %collective-permute-start.27 = (bf16[1024,384]{1,0:T(8,128)(2,1)S(1)}, bf16[1024,384]{1,0:T(8,128)(2,1)}, u32[]{:S(2)}, u32[]{:S(2)}) collective-permute-start(bf16[1024,384]{1,0:T(8,128)(2,1)S(1)} %slice.124.refs_8_.refs_6_.refs_7_.refs_23_), channel_id=1, source_target_pairs={{0,2},{2,0},{1,3},{3,1},{4,6},{6,4},{5,7},{7,5},{8,10},{10,8},{9,1... | collective-permute-start | bytes 2359304 | tf_op jit(solution)/shard_map/ppermute | solution.py:37
  194.8 34.2 %collective-permute-start.31 = (bf16[1024,384]{1,0:T(8,128)(2,1)}, bf16[1024,384]{1,0:T(8,128)(2,1)}, u32[]{:S(2)}, u32[]{:S(2)}) collective-permute-start(bf16[1024,384]{1,0:T(8,128)(2,1)} %collective-permute-done.29.refs_12_.refs_10_.refs_11_.refs_27_), channel_id=1, source_target_pairs={{0,2},{2,0},{1,3},{3,1},{4,6},{6,4},{5,7},{7,5},{8,10},{10,8},{9,1... | collective-permute-start | bytes 2359304 | tf_op jit(solution)/shard_map/ppermute | solution.py:37
  217.1 15.8 %collective-permute-start.23 = (bf16[256,256]{1,0:T(8,128)(2,1)S(1)}, bf16[256,256]{1,0:T(8,128)(2,1)S(1)}, u32[]{:S(2)}, u32[]{:S(2)}) collective-permute-start(bf16[256,256]{1,0:T(8,128)(2,1)S(1)} %get-tuple-element.205), channel_id=1, source_target_pairs={{0,2},{2,0},{1,3},{3,1},{4,6},{6,4},{5,7},{7,5},{8,10},{10,8},{9,1... | collective-permute-start | bytes 393224 | tf_op jit(solution)/shard_map/ppermute | solution.py:37
  217.5 24.8 %collective-permute-start.24 = (bf16[256,256]{1,0:T(8,128)(2,1)S(1)}, bf16[256,256]{1,0:T(8,128)(2,1)S(1)}, u32[]{:S(2)}, u32[]{:S(2)}) collective-permute-start(bf16[256,256]{1,0:T(8,128)(2,1)S(1)} %get-tuple-element.204), channel_id=1, source_target_pairs={{0,4},{4,0},{1,5},{5,1},{2,6},{6,2},{3,7},{7,3},{8,12},{12,8},{9,1... | collective-permute-start | bytes 393224 | tf_op jit(solution)/shard_map/ppermute | solution.py:41
  217.7 28.1 %collective-permute-start.25 = (bf16[256,256]{1,0:T(8,128)(2,1)S(1)}, bf16[256,256]{1,0:T(8,128)(2,1)S(1)}, u32[]{:S(2)}, u32[]{:S(2)}) collective-permute-start(bf16[256,256]{1,0:T(8,128)(2,1)S(1)} %get-tuple-element.203), channel_id=1, source_target_pairs={{0,6},{1,7},{2,4},{3,5},{4,2},{5,3},{6,0},{7,1},{8,14},{9,15},{10,... | collective-permute-start | bytes 393224 | tf_op jit(solution)/shard_map/ppermute | solution.py:45
  229.0 18.2 %collective-permute-start.26 = (bf16[1024,384]{1,0:T(8,128)(2,1)S(1)}, bf16[1024,384]{1,0:T(8,128)(2,1)S(1)}, u32[]{:S(2)}, u32[]{:S(2)}) collective-permute-start(bf16[1024,384]{1,0:T(8,128)(2,1)S(1)} %slice.124.refs_8_.refs_6_.refs_7_.refs_23_), channel_id=1, source_target_pairs={{0,1},{1,0},{2,3},{3,2},{4,5},{5,4},{6,7},{7,6},{8,9},{9,8},{10,11... | collective-permute-start | bytes 2359304 | tf_op jit(solution)/shard_map/ppermute | solution.py:33
  232.9 14.4 %collective-permute-start.28 = (bf16[1024,384]{1,0:T(8,128)(2,1)}, bf16[1024,384]{1,0:T(8,128)(2,1)S(1)}, u32[]{:S(2)}, u32[]{:S(2)}) collective-permute-start(bf16[1024,384]{1,0:T(8,128)(2,1)} %collective-permute-done.27.refs_10_.refs_8_.refs_9_.refs_25_), channel_id=1, source_target_pairs={{0,1},{1,0},{2,3},{3,2},{4,5},{5,4},{6,7},{7,6},{8,9},{9,8},{10,11... | collective-permute-start | bytes 2359304 | tf_op jit(solution)/shard_map/ppermute | solution.py:33
  247.2 39.9 %collective-permute-start.35 = (bf16[1024,1024]{1,0:T(8,128)(2,1)S(1)}, bf16[1024,1024]{1,0:T(8,128)(2,1)S(1)}, u32[]{:S(2)}, u32[]{:S(2)}) collective-permute-start(bf16[1024,1024]{1,0:T(8,128)(2,1)S(1)} %copy-done.2), channel_id=1, source_target_pairs={{0,1},{1,0},{2,3},{3,2},{4,5},{5,4},{6,7},{7,6},{8,9},{9,8},{10,11... | collective-permute-start | bytes 6291464 | tf_op jit(solution)/shard_map/ppermute | solution.py:33
  258.5 28.7 %collective-permute-start.37 = (bf16[1024,1024]{1,0:T(8,128)(2,1)S(1)}, bf16[1024,1024]{1,0:T(8,128)(2,1)}, u32[]{:S(2)}, u32[]{:S(2)}) collective-permute-start(bf16[1024,1024]{1,0:T(8,128)(2,1)S(1)} %collective-permute-done.36.refs_5_.refs_9_.refs_10_.refs_14_), channel_id=1, source_target_pairs={{0,1},{1,0},{2,3},{3,2},{4,5},{5,4},{6,7},{7,6},{8,9},{9,8},{10,11... | collective-permute-start | bytes 6291464 | tf_op jit(solution)/shard_map/ppermute | solution.py:33
  273.6 13.5 %collective-permute-start.34 = (bf16[256,1024]{1,0:T(8,128)(2,1)S(1)}, bf16[256,1024]{1,0:T(8,128)(2,1)S(1)}, u32[]{:S(2)}, u32[]{:S(2)}) collective-permute-start(bf16[256,1024]{1,0:T(8,128)(2,1)S(1)} %get-tuple-element.127.refs_1_.refs_3_), channel_id=1, source_target_pairs={{0,2},{2,0},{1,3},{3,1},{4,6},{6,4},{5,7},{7,5},{8,10},{10,8},{9,1... | collective-permute-start | bytes 1572872 | tf_op jit(solution)/shard_map/ppermute | solution.py:37
  298.4 11.9 %collective-permute-start.38 = (bf16[256,1024]{1,0:T(8,128)(2,1)S(1)}, bf16[256,1024]{1,0:T(8,128)(2,1)S(1)}, u32[]{:S(2)}, u32[]{:S(2)}) collective-permute-start(bf16[256,1024]{1,0:T(8,128)(2,1)S(1)} %get-tuple-element.133), channel_id=1, source_target_pairs={{0,2},{2,0},{1,3},{3,1},{4,6},{6,4},{5,7},{7,5},{8,10},{10,8},{9,1... | collective-permute-start | bytes 1572872 | tf_op jit(solution)/shard_map/ppermute | solution.py:37
  337.0 18.1 %collective-permute-start.68 = (f32[12,32,128]{2,1,0:T(8,128)S(1)}, f32[12,32,128]{2,1,0:T(8,128)S(1)}, u32[]{:S(2)}, u32[]{:S(2)}) collective-permute-start(f32[12,32,128]{2,1,0:T(8,128)S(1)} %slice_bitcast_fusion.5), channel_id=1, source_target_pairs={{0,4},{4,0},{1,5},{5,1},{2,6},{6,2},{3,7},{7,3},{8,12},{12,8},{9,1... | collective-permute-start | bytes 589832 | tf_op jit(solution)/shard_map/ppermute | solution.py:41
  355.2 17.4 %collective-permute-start.69 = (f32[2,32,128]{2,1,0:T(8,128)S(1)}, f32[2,32,128]{2,1,0:T(8,128)S(1)}, u32[]{:S(2)}, u32[]{:S(2)}) collective-permute-start(f32[2,32,128]{2,1,0:T(8,128)S(1)} %slice.137), channel_id=1, source_target_pairs={{0,2},{2,0},{1,3},{3,1},{4,6},{6,4},{5,7},{7,5},{8,10},{10,8},{9,1... | collective-permute-start | bytes 98312 | tf_op jit(solution)/shard_map/ppermute | solution.py:37
  373.3 153.1 %all-gather.18.cloned.1.call-start = ((), (), s32[]{:S(2)}) async-start(), calls=%async_computation.5 | async-start | bytes 3514368 | tf_op jit(solution)/shard_map/all_gather | solution.py:1271
  413.7 12.8 %collective-permute-start.47 = (bf16[256,768]{1,0:T(8,128)(2,1)S(1)}, bf16[256,768]{1,0:T(8,128)(2,1)S(1)}, u32[]{:S(2)}, u32[]{:S(2)}) collective-permute-start(bf16[256,768]{1,0:T(8,128)(2,1)S(1)} %get-tuple-element.192), channel_id=1, source_target_pairs={{0,2},{2,0},{1,3},{3,1},{4,6},{6,4},{5,7},{7,5},{8,10},{10,8},{9,1... | collective-permute-start | bytes 1179656 | tf_op jit(solution)/shard_map/ppermute | solution.py:37
  414.9 11.5 %collective-permute-start.48 = (bf16[256,768]{1,0:T(8,128)(2,1)S(1)}, bf16[256,768]{1,0:T(8,128)(2,1)S(1)}, u32[]{:S(2)}, u32[]{:S(2)}) collective-permute-start(bf16[256,768]{1,0:T(8,128)(2,1)S(1)} %get-tuple-element.191), channel_id=1, source_target_pairs={{0,4},{4,0},{1,5},{5,1},{2,6},{6,2},{3,7},{7,3},{8,12},{12,8},{9,1... | collective-permute-start | bytes 1179656 | tf_op jit(solution)/shard_map/ppermute | solution.py:41
  414.9 18.0 %collective-permute-start.49 = (bf16[256,768]{1,0:T(8,128)(2,1)S(1)}, bf16[256,768]{1,0:T(8,128)(2,1)S(1)}, u32[]{:S(2)}, u32[]{:S(2)}) collective-permute-start(bf16[256,768]{1,0:T(8,128)(2,1)S(1)} %get-tuple-element.190), channel_id=1, source_target_pairs={{0,6},{1,7},{2,4},{3,5},{4,2},{5,3},{6,0},{7,1},{8,14},{9,15},{10,... | collective-permute-start | bytes 1179656 | tf_op jit(solution)/shard_map/ppermute | solution.py:45
  487.6 21.4 %collective-permute-start.60 = (bf16[4,10,32,128]{3,2,1,0:T(8,128)(2,1)S(1)}, bf16[4,10,32,128]{3,2,1,0:T(8,128)(2,1)S(1)}, u32[]{:S(2)}, u32[]{:S(2)}) collective-permute-start(bf16[4,10,32,128]{3,2,1,0:T(8,128)(2,1)S(1)} %pad_maximum_fusion.1.refs_3_), channel_id=1, source_target_pairs={{0,2},{2,0},{1,3},{3,1},{4,6},{6,4},{5,7},{7,5},{8,10},{10,8},{9,1... | collective-permute-start | bytes 983048 | tf_op jit(solution)/shard_map/ppermute | solution.py:37
  493.6 22.1 %collective-permute-start.64 = (bf16[4,10,32,128]{3,2,1,0:T(8,128)(2,1)S(1)}, bf16[4,10,32,128]{3,2,1,0:T(8,128)(2,1)S(1)}, u32[]{:S(2)}, u32[]{:S(2)}) collective-permute-start(bf16[4,10,32,128]{3,2,1,0:T(8,128)(2,1)S(1)} %collective-permute-done.62.refs_7_), channel_id=1, source_target_pairs={{0,2},{2,0},{1,3},{3,1},{4,6},{6,4},{5,7},{7,5},{8,10},{10,8},{9,1... | collective-permute-start | bytes 983048 | tf_op jit(solution)/shard_map/ppermute | solution.py:37
  496.2 23.2 %collective-permute-start.53 = (bf16[1,512,256]{2,1,0:T(8,128)(2,1)}, bf16[1,512,256]{2,1,0:T(8,128)(2,1)}, u32[]{:S(2)}, u32[]{:S(2)}) collective-permute-start(bf16[1,512,256]{2,1,0:T(8,128)(2,1)} %get-tuple-element.196), channel_id=1, source_target_pairs={{0,1},{1,0},{2,3},{3,2},{4,5},{5,4},{6,7},{7,6},{8,9},{9,8},{10,11... | collective-permute-start | bytes 786440 | tf_op jit(solution)/shard_map/ppermute | solution.py:33
  508.5 23.7 %collective-permute-start.59 = (bf16[4,10,32,128]{3,2,1,0:T(8,128)(2,1)S(1)}, bf16[4,10,32,128]{3,2,1,0:T(8,128)(2,1)S(1)}, u32[]{:S(2)}, u32[]{:S(2)}) collective-permute-start(bf16[4,10,32,128]{3,2,1,0:T(8,128)(2,1)S(1)} %pad_maximum_fusion.1.refs_3_), channel_id=1, source_target_pairs={{0,1},{1,0},{2,3},{3,2},{4,5},{5,4},{6,7},{7,6},{8,9},{9,8},{10,11... | collective-permute-start | bytes 983048 | tf_op jit(solution)/shard_map/ppermute | solution.py:33
  508.5 23.8 %collective-permute-start.63 = (bf16[4,10,32,128]{3,2,1,0:T(8,128)(2,1)S(1)}, bf16[4,10,32,128]{3,2,1,0:T(8,128)(2,1)S(1)}, u32[]{:S(2)}, u32[]{:S(2)}) collective-permute-start(bf16[4,10,32,128]{3,2,1,0:T(8,128)(2,1)S(1)} %collective-permute-done.62.refs_7_), channel_id=1, source_target_pairs={{0,1},{1,0},{2,3},{3,2},{4,5},{5,4},{6,7},{7,6},{8,9},{9,8},{10,11... | collective-permute-start | bytes 983048 | tf_op jit(solution)/shard_map/ppermute | solution.py:33
  509.0 23.2 %collective-permute-start.61 = (bf16[4,10,32,128]{3,2,1,0:T(8,128)(2,1)S(1)}, bf16[4,10,32,128]{3,2,1,0:T(8,128)(2,1)S(1)}, u32[]{:S(2)}, u32[]{:S(2)}) collective-permute-start(bf16[4,10,32,128]{3,2,1,0:T(8,128)(2,1)S(1)} %collective-permute-done.60.refs_5_), channel_id=1, source_target_pairs={{0,1},{1,0},{2,3},{3,2},{4,5},{5,4},{6,7},{7,6},{8,9},{9,8},{10,11... | collective-permute-start | bytes 983048 | tf_op jit(solution)/shard_map/ppermute | solution.py:33
  515.6 16.6 %collective-permute-start.65 = (bf16[4,10,32,128]{3,2,1,0:T(8,128)(2,1)S(1)}, bf16[4,10,32,128]{3,2,1,0:T(8,128)(2,1)S(1)}, u32[]{:S(2)}, u32[]{:S(2)}) collective-permute-start(bf16[4,10,32,128]{3,2,1,0:T(8,128)(2,1)S(1)} %collective-permute-done.64.refs_9_), channel_id=1, source_target_pairs={{0,1},{1,0},{2,3},{3,2},{4,5},{5,4},{6,7},{7,6},{8,9},{9,8},{10,11... | collective-permute-start | bytes 983048 | tf_op jit(solution)/shard_map/ppermute | solution.py:33
  (140 other events, 1955.0 us)
Sparse Core Ops, SparseCore 0:
  10.2 29.7 all-gather.7
  42.2 27.5 all-gather.9
  72.0 27.4 all-gather.11
  101.4 27.4 all-gather.13
  130.9 45.5 all-gather.15
  373.4 66.5 all-gather.19
  453.8 68.8 all-gather.17

commit v4 on v3

--- a/solution.py
+++ b/solution.py
@@ -1060,18 +1060,24 @@
     copies = []
     for item, (kind, slot, starts) in enumerate(plan):
         column = len(starts) * LANES
+        times = len(starts[0])
         for pair in range(2):
             for side in range(2):
-                parts = [
-                    found[:, side, pair, :, row : row + RANK, :].reshape(-1, LANES)
-                    for row in starts
-                ]
+                parts = []
+                for rows in starts:
+                    terms = [
+                        found[:, side, pair ^ far, :, row : row + RANK, :].reshape(-1, LANES)
+                        for far, row in enumerate(rows)
+                    ]
+                    parts.append(jnp.concatenate(terms, axis=0))
                 value = jnp.concatenate(parts, axis=1)
                 start = (2 * pair + side) * column
                 if kind % 2 == 0:
-                    held[item][start : start + column, :] = tn(value, spread[...])
+                    whole = jnp.concatenate([spread[...]] * times, axis=0)
+                    held[item][start : start + column, :] = tn(value, whole)
                 else:
-                    held[item][:, start : start + column] = nn(turned[...], value)
+                    whole = jnp.concatenate([turned[...]] * times, axis=1)
+                    held[item][:, start : start + column] = nn(whole, value)
         copy = pltpu.make_async_copy(held[item], outs[kinds.index(kind)].at[slot], sems.at[item])
         copy.start()
         copies.append(copy)
@@ -1139,7 +1145,7 @@
 
 
 def rows_of(base, blocks, rows, group, first=0):
-    return [base + n * rows + group * RANK for n in range(first, blocks)]
+    return [(base + n * rows + group * RANK,) for n in range(first, blocks)]
 
 
 def expand(plan, spread, turned, found, outs):
@@ -1401,8 +1407,6 @@
         taps, where, grad, grad_conv, edge, value, gate, kernel, second, t_pair, t_mix, mixed,
         partial, heads, convs, adapt_down, adapt_up,
     )
-    came = after(by_pair(sums_two[2:4]), grad)
-    sums_two = jnp.concatenate([sums_two[:2] + came, sums_two[4:]], axis=0)
     found_two = everywhere(sums_two)
     grad_slots = exchanged(grad_slots)
     back = attend_back(block, slots, grad_slots, text, logs)
@@ -1416,8 +1420,18 @@
     head_sums = head_sums[0] + by_side(head_sums[1].astype(BF)).astype(F32)
     head_sums = head_sums[0] + by_pair(head_sums[1].astype(BF)).astype(F32)
     found_heads = everywhere(after(head_sums, other_half))
+    outs = [shape(v.shape, F32) for v in (adapt_down, adapt_up, adapt_down_ff, adapt_up_ff)]
+    ffn_blocks, ffn_rows = sums_two.shape[:2]
+    plan = [
+        (kind, slot, [(n * ffn_rows + g * RANK, (n + 2) * ffn_rows + g * RANK) for n in range(2)])
+        for kind, slot, g in ((0, 5, 0), (1, 8, 1))
+    ]
+    plan += [
+        (kind, 1, rows_of(0, ffn_blocks, ffn_rows, g, 4)) for kind, g in ((2, 0), (3, 1))
+    ]
+    outs = expand(plan, spread, turned, after(found_two, half), outs)
     part, send, sums_one = ffn_back(
-        0, 0, 7, where, half, other_half, *kept_one, w1_in, w1_out, adapters
+        0, 0, 7, after(where, outs[0]), half, other_half, *kept_one, w1_in, w1_out, adapters
     )
     sums_one = sums_one[0] + by_side(sums_one[1].astype(BF)).astype(F32)
     sums_one = jnp.concatenate([sums_one[:2] + by_pair(sums_one[2:4]), sums_one[4:]], axis=0)
@@ -1428,13 +1442,6 @@
     input_grad = finish(where, grad, part, by_pair(send), own)
     input_grad = feature_parts(input_grad, place).astype(F32)
 
-    outs = [shape(v.shape, F32) for v in (adapt_down, adapt_up, adapt_down_ff, adapt_up_ff)]
-    ffn_blocks, ffn_rows = sums_two.shape[:2]
-    plan = [(kind, slot, rows_of(0, 2, ffn_rows, g)) for kind, slot, g in ((0, 5, 0), (1, 8, 1))]
-    plan += [
-        (kind, 1, rows_of(0, ffn_blocks, ffn_rows, g, 2)) for kind, g in ((2, 0), (3, 1))
-    ]
-    outs = expand(plan, spread, turned, after(found_two, send), outs)
     head_blocks, head_rows = head_sums.shape[:2]
     places = ((0, 1), (0, 2), (0, 3), (1, 5), (1, 0), (1, 1), (1, 2), (0, 6))
     places += ((0, 4), (1, 6), (0, 7), (1, 3), (1, 4))

time: 553 us -> 549 us (level)
  waiting for transfers between devices: 201 us -> 192 us
    unnamed x226 -> x228, local copies, waits for them, and re-layouts: 43 us -> 45.3 us
    ppermute x24 -> x23, waiting for transfers between devices: 96.3 us -> 94.8 us  [by_pair(): return lax.ppermute(value, 'tp', PAIR)]
    ppermute x24 -> x23, starting transfers between devices: 23.6 us -> 22.3 us  [by_pair(): return lax.ppermute(value, 'tp', PAIR)]
  transfers between devices with their start and end apart: 77 -> 76, of which waited for: 38 -> 37; matrix products, arithmetic and copies ran while one was open for 5% -> 5% of each run, Pallas kernels for 22% -> 22%
where the time goes in v4:
time: 549 us; the launch traced here: 539 us
  waiting for transfers between devices  192 us (35%)
  Pallas kernels  149 us (27%)
  starting transfers between devices  100 us (18%)
  local copies, waits for them, and re-layouts  60 us (11%)
  between operations  16.6 us (3%)
  other arithmetic  13.1 us (2%)
  blocking collectives  7.87 us (1%)
    ppermute x23, waiting for transfers between devices, by_pair(): return lax.ppermute(value, 'tp', PAIR)  94.8 us
    pallas_call x13, Pallas kernels, run(): pl.pallas_call(body, name=name, in_specs=specs, out_specs=out_specs or [V...  93.8 us
    ppermute x14, waiting for transfers between devices, by_side(): return lax.ppermute(value, 'ctx', SIDE)  65.9 us
    ppermute x23, starting transfers between devices, by_core(): return lax.ppermute(value, 'tp', CORE)  50.6 us
    unnamed x228, local copies, waits for them, and re-layouts  45.3 us
    pallas_call x1, Pallas kernels, attend_back(): pl.pallas_call(bwd_kernel, grid_spec=pltpu.PrefetchScalarGridSpec(num_sca...  29.4 us
    ppermute x23, starting transfers between devices, by_pair(): return lax.ppermute(value, 'tp', PAIR)  22.3 us
    pallas_call x1, Pallas kernels, attend(): pl.pallas_call(fwd_kernel, grid_spec=pltpu.PrefetchScalarGridSpec(num_sca...  14.8 us
  transfers between devices with their start and end apart: 76, of which 37 were waited for; matrix products, arithmetic and copies ran while one was open for 5% of the time, Pallas kernels for 22%

profile of v4, /device:TPU:1, one launch (start us, length us, event | category | flops | bytes accessed | tf_op | source)
XLA Modules:
  0.0 539.0 jit_solution(9704692928335391430)
XLA Ops:
  12.3 7.9 %all-reduce = s32[8]{0:T(128)S(1)} all-reduce(s32[8]{0:T(128)S(1)} %dynamic-update-slice), channel_id=1, replica_groups=mesh['shard'=4,'ctx'=2,'tp'=4] {'shard'}, use_global_device_ids=true, to_apply=%add | all-reduce | flops 8 | bytes 64
  25.3 9.2 %collective-permute-done.1 = bf16[512,512]{1,0:T(8,128)(2,1)S(1)} collective-permute-done((bf16[512,512]{1,0:T(8,128)(2,1)S(1)}, bf16[512,512]{1,0:T(8,128)(2,1)S(1)}, u32[]{:S(2)}, u32[]{:S(2)}) %collective-permute-start.1) | collective-permute-done | bytes 524320 | tf_op jit(solution)/shard_map/ppermute | solution.py:37
  48.1 7.1 %collective-permute-done.12 = bf16[256,512]{1,0:T(8,128)(2,1)S(1)} collective-permute-done((bf16[256,512]{1,0:T(8,128)(2,1)S(1)}, bf16[256,512]{1,0:T(8,128)(2,1)S(1)}, u32[]{:S(2)}, u32[]{:S(2)}) %collective-permute-start.12) | collective-permute-done | bytes 262176 | tf_op jit(solution)/shard_map/ppermute | solution.py:37
  56.1 12.5 %collective-permute-done.3.refs_5_.refs_10_ = bf16[1024,512]{1,0:T(8,128)(2,1)} collective-permute-done((bf16[1024,512]{1,0:T(8,128)(2,1)}, bf16[1024,512]{1,0:T(8,128)(2,1)}, u32[]{:S(2)}, u32[]{:S(2)}) %collective-permute-start.3) | collective-permute-done | bytes 1048608 | tf_op jit(solution)/shard_map/ppermute | solution.py:41
  75.0 20.5 %collective-permute-done.6.refs_9_.refs_14_ = bf16[1024,512]{1,0:T(8,128)(2,1)} collective-permute-done((bf16[1024,512]{1,0:T(8,128)(2,1)}, bf16[1024,512]{1,0:T(8,128)(2,1)}, u32[]{:S(2)}, u32[]{:S(2)}) %collective-permute-start.6) | collective-permute-done | bytes 1048608 | tf_op jit(solution)/shard_map/ppermute | solution.py:41
  95.5 4.0 all-gather.12.cloned.1.call-done.refs_0_.refs_15_
  108.3 11.2 %hidden_forward.2 = (f32[256,1024]{1,0:T(8,128)S(1)}, bf16[256,1024]{1,0:T(8,128)(2,1)S(1)}, f32[4,512,512]{2,1,0:T(8,128)}, bf16[512,128]{1,0:T(8,128)(2,1)S(1)}, bf16[512,128]{1,0:T(8,128)(2,1)S(1)}) custom-call(s32[4]{0:T(128)S(1)} %pad_add_fusion.where.refs_0_, bf16[256,1024]{1,0:T(8,128)(2,1)S(1)} %get-tuple-element.97.refs_1_.refs_3_, ...), custom_call_target="tpu_custom_call" | custom-call | flops 4294967296 | bytes 16777216 | tf_op jit(solution)/shard_map/hidden_forward/pallas_call | solution.py:320
  122.0 3.1 collective-permute-done.14.refs_2_.refs_17_
  126.0 2.9 all-gather.14.cloned.1.call-done
  132.8 10.1 %collective-permute-done.8.other = bf16[256,1024]{1,0:T(8,128)(2,1)S(1)} collective-permute-done((bf16[256,1024]{1,0:T(8,128)(2,1)}, bf16[256,1024]{1,0:T(8,128)(2,1)S(1)}, u32[]{:S(2)}, u32[]{:S(2)}) %collective-permute-start.8) | collective-permute-done | bytes 524320 | tf_op jit(solution)/shard_map/ppermute | solution.py:37
  142.9 10.3 %collective-permute-done.18.refs_6_.refs_21_ = bf16[1024,512]{1,0:T(8,128)(2,1)S(1)} collective-permute-done((bf16[1024,512]{1,0:T(8,128)(2,1)}, bf16[1024,512]{1,0:T(8,128)(2,1)S(1)}, u32[]{:S(2)}, u32[]{:S(2)}) %collective-permute-start.18) | collective-permute-done | bytes 1048608 | tf_op jit(solution)/shard_map/ppermute | solution.py:41
  159.9 6.3 %heads_forward.1 = (f32[256,1024]{1,0:T(8,128)S(1)}, bf16[256,768]{1,0:T(8,128)(2,1)S(1)}, bf16[256,768]{1,0:T(8,128)(2,1)S(1)}, bf16[256,768]{1,0:T(8,128)(2,1)...) custom-call(s32[4]{0:T(128)S(1)} %pad_add_fusion.where.refs_0_, f32[256,1024]{1,0:T(8,128)S(1)} %copy-done.17, ...), custom_call_target="tpu_custom_call" | custom-call | flops 1610612736 | bytes 16777216 | tf_op jit(solution)/shard_map/heads_forward/pallas_call | solution.py:320
  171.4 7.3 %collective-permute-done.20.s1 = bf16[256,768]{1,0:T(8,128)(2,1)S(1)} collective-permute-done((bf16[256,768]{1,0:T(8,128)(2,1)S(1)}, bf16[256,768]{1,0:T(8,128)(2,1)S(1)}, u32[]{:S(2)}, u32[]{:S(2)}) %collective-permute-start.20) | collective-permute-done | bytes 393248 | tf_op jit(solution)/shard_map/ppermute | solution.py:37
  179.5 3.8 collective-permute-done.21.s2
  184.0 8.6 %collective-permute-done.22.s3 = bf16[256,768]{1,0:T(8,128)(2,1)S(1)} collective-permute-done((bf16[256,768]{1,0:T(8,128)(2,1)S(1)}, bf16[256,768]{1,0:T(8,128)(2,1)S(1)}, u32[]{:S(2)}, u32[]{:S(2)}) %collective-permute-start.22) | collective-permute-done | bytes 393248 | tf_op jit(solution)/shard_map/ppermute | solution.py:45
  200.9 14.8 %attend.1 = (bf16[4,256,256]{2,1,0:T(8,128)(2,1)S(1)}, f32[4,1024,1]{2,1,0:T(8,128)S(1)}) custom-call(s32[1]{0:T(128)} %bitcast.14.b_ref, bf16[256,768]{1,0:T(8,128)(2,1)S(1)} %copy-done.85, bf16[256,768]{1,0:T(8,128)(2,1)S(1)} %copy-done.88, bf16[256,768]{1,0:T(8,128)(2,1)S(1)} %copy-done.91, bf16[256,768]{1,0:T(8,128)(2,1)S(1)} %copy-done.94, ...), custom_call_target="tpu_custom_call" | custom-call | flops 1073741824 | bytes 2097152 | tf_op jit(solution)/shard_map/attend/pallas_call | solution.py:112
  219.9 9.2 %collective-permute-done.31.refs_14_.refs_12_.refs_13_.refs_29_ = bf16[1024,384]{1,0:T(8,128)(2,1)} collective-permute-done((bf16[1024,384]{1,0:T(8,128)(2,1)}, bf16[1024,384]{1,0:T(8,128)(2,1)}, u32[]{:S(2)}, u32[]{:S(2)}) %collective-permute-start.31) | collective-permute-done | bytes 786464 | tf_op jit(solution)/shard_map/ppermute | solution.py:37
  229.1 3.8 collective-permute-start.26
  234.2 8.1 %collective-permute-done.24.m2.refs_12_ = bf16[256,256]{1,0:T(8,128)(2,1)S(1)} collective-permute-done((bf16[256,256]{1,0:T(8,128)(2,1)S(1)}, bf16[256,256]{1,0:T(8,128)(2,1)S(1)}, u32[]{:S(2)}, u32[]{:S(2)}) %collective-permute-start.24) | collective-permute-done | bytes 131104 | tf_op jit(solution)/shard_map/ppermute | solution.py:41
  242.3 3.6 collective-permute-start.30
  249.6 6.8 %pair_forward.1 = (f32[256,1024]{1,0:T(8,128)S(1)}, f32[256,1024]{1,0:T(8,128)S(1)}, f32[256,1024]{1,0:T(8,128)S(1)}, f32[2,2,32,256]{3,2,1,0:T(8,128)S(1)}, bf1...) custom-call(s32[4]{0:T(128)S(1)} %pad_add_fusion.where.refs_0_, f32[256,1024]{1,0:T(8,128)} %copy-done.15, ...), custom_call_target="tpu_custom_call" | custom-call | flops 1610612736 | bytes 16777216 | tf_op jit(solution)/shard_map/pair_forward/pallas_call | solution.py:320
  258.8 3.3 collective-permute-start.33
  262.2 2.5 collective-permute-done.33.refs_4_
  264.7 6.8 %conv_forward.1 = (f32[256,1024]{1,0:T(8,128)S(1)}, f32[256,1024]{1,0:T(8,128)S(1)}, bf16[256,1024]{1,0:T(8,128)(2,1)S(1)}, bf16[256,128]{1,0:T(8,128)(2,1)S(1)}) custom-call(s32[4]{0:T(128)S(1)} %pad_add_fusion.where.refs_0_, f32[256,1024]{1,0:T(8,128)S(1)} %get-tuple-element.122.refs_1_.refs_7_, f32[256,1024]{1,0:T(8,128)} %copy-done.21, ...), custom_call_target="tpu_custom_call" | custom-call | flops 536870912 | bytes 16777216 | tf_op jit(solution)/shard_map/conv_forward/pallas_call | solution.py:320
  275.8 11.3 %collective-permute-done.34.refs_2_.refs_4_ = bf16[256,1024]{1,0:T(8,128)(2,1)S(1)} collective-permute-done((bf16[256,1024]{1,0:T(8,128)(2,1)S(1)}, bf16[256,1024]{1,0:T(8,128)(2,1)S(1)}, u32[]{:S(2)}, u32[]{:S(2)}) %collective-permute-start.34) | collective-permute-done | bytes 524320 | tf_op jit(solution)/shard_map/ppermute | solution.py:37
  287.1 11.2 %hidden_forward.3 = (f32[256,1024]{1,0:T(8,128)S(1)}, bf16[256,1024]{1,0:T(8,128)(2,1)S(1)}, f32[4,512,512]{2,1,0:T(8,128)}, bf16[512,128]{1,0:T(8,128)(2,1)S(1)}, bf16[512,128]{1,0:T(8,128)(2,1)S(1)}) custom-call(s32[4]{0:T(128)S(1)} %pad_add_fusion.where.refs_0_, bf16[256,1024]{1,0:T(8,128)(2,1)S(1)} %get-tuple-element.127.refs_1_.refs_3_, ...), custom_call_target="tpu_custom_call" | custom-call | flops 4294967296 | bytes 16777216 | tf_op jit(solution)/shard_map/hidden_forward/pallas_call | solution.py:320
  299.5 10.7 %collective-permute-done.38.other = bf16[256,1024]{1,0:T(8,128)(2,1)S(1)} collective-permute-done((bf16[256,1024]{1,0:T(8,128)(2,1)S(1)}, bf16[256,1024]{1,0:T(8,128)(2,1)S(1)}, u32[]{:S(2)}, u32[]{:S(2)}) %collective-permute-start.38) | collective-permute-done | bytes 524320 | tf_op jit(solution)/shard_map/ppermute | solution.py:37
  312.5 10.1 %collective-permute-done.41.refs_2_ = bf16[256,1024]{1,0:T(8,128)(2,1)S(1)} collective-permute-done((bf16[256,1024]{1,0:T(8,128)(2,1)S(1)}, bf16[256,1024]{1,0:T(8,128)(2,1)S(1)}, u32[]{:S(2)}, u32[]{:S(2)}) %collective-permute-start.41) | collective-permute-done | bytes 524320 | tf_op jit(solution)/shard_map/ppermute | solution.py:37
  322.6 12.2 %hidden_backward.2 = (f32[256,1024]{1,0:T(8,128)S(1)}, bf16[256,1024]{1,0:T(8,128)(2,1)S(1)}, f32[2,12,32,128]{3,2,1,0:T(8,128)S(1)}) custom-call(s32[4]{0:T(128)S(1)} %pad_add_fusion.where.refs_0_, bf16[256,1024]{1,0:T(8,128)(2,1)S(1)} %get-tuple-element.137.refs_1_, bf16[256,1024]{1,0:T(8,128)(2,1)S(1)} %collective-permute-done.41.refs_2_, ...), custom_call_target="tpu_custom_call" | custom-call | flops 4294967296 | bytes 16777216 | tf_op jit(solution)/shard_map/hidden_backward/pallas_call | solution.py:320
  337.5 8.3 %collective-permute-done.42.refs_3_ = bf16[256,1024]{1,0:T(8,128)(2,1)S(1)} collective-permute-done((bf16[256,1024]{1,0:T(8,128)(2,1)S(1)}, bf16[256,1024]{1,0:T(8,128)(2,1)S(1)}, u32[]{:S(2)}, u32[]{:S(2)}) %collective-permute-start.42) | collective-permute-done | bytes 524320 | tf_op jit(solution)/shard_map/ppermute | solution.py:37
  345.9 5.1 conv_backward.1
  364.1 11.3 %pair_backward.1 = (f32[256,1024]{1,0:T(8,128)}, bf16[256,256]{1,0:T(8,128)(2,1)S(1)}, bf16[256,256]{1,0:T(8,128)(2,1)S(1)}, bf16[256,256]{1,0:T(8,128)(2,1)S(1)...) custom-call(s32[4]{0:T(128)S(1)} %pad_add_fusion.where.refs_0_, ...), custom_call_target="tpu_custom_call" | custom-call | flops 1610612736 | bytes 16777216 | tf_op jit(solution)/shard_map/pair_backward/pallas_call | solution.py:320
  383.6 29.4 %attend_back.1 = bf16[4,256,768]{2,1,0:T(8,128)(2,1)S(1)} custom-call(s32[1]{0:T(128)} %bitcast.14.b_ref, bf16[256,768]{1,0:T(8,128)(2,1)S(1)} %copy-done.86, bf16[256,768]{1,0:T(8,128)(2,1)S(1)} %copy-done.89, bf16[256,768]{1,0:T(8,128)(2,1)S(1)} %copy-done.92, bf16[256,768]{1,0:T(8,128)(2,1)S(1)} %copy-done.95, ...), custom_call_target="tpu_custom_call" | custom-call | flops 2684354560 | bytes 3670016 | tf_op jit(solution)/shard_map/attend_back/pallas_call | solution.py:184
  415.9 9.9 %collective-permute-start.40 = (bf16[1,512,256]{2,1,0:T(8,128)(2,1)S(1)}, bf16[1,512,256]{2,1,0:T(8,128)(2,1)S(1)}, u32[]{:S(2)}, u32[]{:S(2)}) collective-permute-start(bf16[1,512,256]{2,1,0:T(8,128)(2,1)S(1)} %get-tuple-element.200), channel_id=1, source_target_pairs={{0,1},{1,0},{2,3},{3,2},{4,5},{5,4},{6,7},{7,6},{8,9},{9,8},{10,11... | collective-permute-start | bytes 786440 | tf_op jit(solution)/shard_map/ppermute | solution.py:33
  427.9 7.0 %heads_backward.1 = (f32[256,1024]{1,0:T(8,128)S(1)}, bf16[256,1024]{1,0:T(8,128)(2,1)S(1)}, f32[2,2,2,208,128]{4,3,2,1,0:T(8,128)S(1)}) custom-call(s32[4]{0:T(128)S(1)} %pad_add_fusion.where.refs_0_, f32[256,1024]{1,0:T(8,128)S(1)} %copy-done.44, f32[256,1024]{1,0:T(8,128)S(1)} %copy-done.16, bf16[256,384]{1,0:T(8,128)(2,1)S(1)} %copy-done.70, ...), custom_call_target="tpu_custom_call" | custom-call | flops 1610612736 | bytes 16777216 | tf_op jit(solution)/shard_map/heads_backward/pallas_call | solution.py:320
  437.2 3.5 collective-permute-done.67
  441.1 4.3 collective-permute-done.68
  449.1 3.2 expand.2
  455.4 12.2 %hidden_backward.3 = (f32[256,1024]{1,0:T(8,128)S(1)}, bf16[256,1024]{1,0:T(8,128)(2,1)S(1)}, f32[2,12,32,128]{3,2,1,0:T(8,128)S(1)}) custom-call(s32[4]{0:T(128)S(1)} %pad_add_fusion.where.refs_0_, bf16[256,1024]{1,0:T(8,128)(2,1)S(1)} %copy-done.61, bf16[256,1024]{1,0:T(8,128)(2,1)S(1)} %copy-done.63, bf16[256,1024]{1,0:T(8,128)(2,1)S(1)} %copy-done.38, ...), custom_call_target="tpu_custom_call" | custom-call | flops 4294967296 | bytes 16777216 | tf_op jit(solution)/shard_map/hidden_backward/pallas_call | solution.py:320
  474.0 3.9 collective-permute-start.59
  479.4 2.7 collective-permute-done.58
  486.8 3.0 collective-permute-done.63.refs_7_
  491.1 2.6 collective-permute-done.53
  494.7 17.2 %collective-permute-start.54 = (bf16[1,512,256]{2,1,0:T(8,128)(2,1)}, bf16[1,512,256]{2,1,0:T(8,128)(2,1)S(1)}, u32[]{:S(2)}, u32[]{:S(2)}) collective-permute-start(bf16[1,512,256]{2,1,0:T(8,128)(2,1)} %get-tuple-element.196), channel_id=1, source_target_pairs={{0,1},{1,0},{2,3},{3,2},{4,5},{5,4},{6,7},{7,6},{8,9},{9,8},{10,11... | collective-permute-start | bytes 786440 | tf_op jit(solution)/shard_map/ppermute | solution.py:33
  512.4 2.3 collective-permute-start.62
  514.8 3.5 collective-permute-start.66
  522.5 3.8 expand.3
  528.1 3.6 expand_near.1
  (433 shorter events, 146.0 us)
Async XLA Ops:
  7.3 32.8 %all-gather.8.cloned.1.call-start = ((), (), s32[]{:S(2)}) async-start(), calls=%async_computation | async-start | bytes 1310720 | tf_op jit(solution)/shard_map/all_gather | solution.py:1237
  8.5 14.3 %collective-permute-start = (bf16[512,256]{1,0:T(8,128)(2,1)S(1)}, bf16[512,256]{1,0:T(8,128)(2,1)S(1)}, u32[]{:S(2)}, u32[]{:S(2)}) collective-permute-start(bf16[512,256]{1,0:T(8,128)(2,1)S(1)} %get-tuple-element.212), channel_id=1, source_target_pairs={{0,1},{1,0},{2,3},{3,2},{4,5},{5,4},{6,7},{7,6},{8,9},{9,8},{10,11... | collective-permute-start | bytes 786440 | tf_op jit(solution)/shard_map/ppermute | solution.py:33
  9.4 60.4 %all-gather.10.cloned.1.call-start = ((), (), s32[]{:S(2)}) async-start(), calls=%async_computation.1 | async-start | bytes 1310720 | tf_op jit(solution)/shard_map/all_gather | solution.py:1237
  9.5 31.0 %collective-permute-start.9 = (bf16[31,256]{1,0:T(8,128)(2,1)}, bf16[31,256]{1,0:T(8,128)(2,1)}, u32[]{:S(2)}, u32[]{:S(2)}) collective-permute-start(bf16[31,256]{1,0:T(8,128)(2,1)} %param.29), channel_id=1, source_target_pairs={{0,1},{1,0},{2,3},{3,2},{4,5},{5,4},{6,7},{7,6},{8,9},{9,8},{10,11... | collective-permute-start | bytes 47624 | tf_op jit(solution)/shard_map/ppermute | solution.py:33
  10.7 36.5 %collective-permute-start.11 = (bf16[512,256]{1,0:T(8,128)(2,1)}, bf16[512,256]{1,0:T(8,128)(2,1)S(1)}, u32[]{:S(2)}, u32[]{:S(2)}) collective-permute-start(bf16[512,256]{1,0:T(8,128)(2,1)} %get-tuple-element.210), channel_id=1, source_target_pairs={{0,1},{1,0},{2,3},{3,2},{4,5},{5,4},{6,7},{7,6},{8,9},{9,8},{10,11... | collective-permute-start | bytes 786440 | tf_op jit(solution)/shard_map/ppermute | solution.py:33
  40.1 59.3 %all-gather.12.cloned.1.call-start = ((), (), s32[]{:S(2)}) async-start(), calls=%async_computation.2 | async-start | bytes 1310720 | tf_op jit(solution)/shard_map/all_gather | solution.py:1237
  42.5 13.6 %collective-permute-start.2 = (bf16[1024,512]{1,0:T(8,128)(2,1)}, bf16[1024,512]{1,0:T(8,128)(2,1)S(1)}, u32[]{:S(2)}, u32[]{:S(2)}) collective-permute-start(bf16[1024,512]{1,0:T(8,128)(2,1)} %all-gather.8.cloned.1.call-done.refs_3_.refs_8_), channel_id=1, source_target_pairs={{0,1},{1,0},{2,3},{3,2},{4,5},{5,4},{6,7},{7,6},{8,9},{9,8},{10,11... | collective-permute-start | bytes 3145736 | tf_op jit(solution)/shard_map/ppermute | solution.py:33
  43.5 25.1 %collective-permute-start.3 = (bf16[1024,512]{1,0:T(8,128)(2,1)}, bf16[1024,512]{1,0:T(8,128)(2,1)}, u32[]{:S(2)}, u32[]{:S(2)}) collective-permute-start(bf16[1024,512]{1,0:T(8,128)(2,1)} %all-gather.8.cloned.1.call-done.refs_3_.refs_8_), channel_id=1, source_target_pairs={{0,4},{4,0},{1,5},{5,1},{2,6},{6,2},{3,7},{7,3},{8,12},{12,8},{9,1... | collective-permute-start | bytes 3145736 | tf_op jit(solution)/shard_map/ppermute | solution.py:41
  69.9 59.0 %all-gather.14.cloned.1.call-start = ((), (), s32[]{:S(2)}) async-start(), calls=%async_computation.3 | async-start | bytes 1310720 | tf_op jit(solution)/shard_map/all_gather | solution.py:1237
  70.9 24.6 %collective-permute-start.6 = (bf16[1024,512]{1,0:T(8,128)(2,1)}, bf16[1024,512]{1,0:T(8,128)(2,1)}, u32[]{:S(2)}, u32[]{:S(2)}) collective-permute-start(bf16[1024,512]{1,0:T(8,128)(2,1)} %all-gather.10.cloned.1.call-done.refs_7_.refs_12_), channel_id=1, source_target_pairs={{0,4},{4,0},{1,5},{5,1},{2,6},{6,2},{3,7},{7,3},{8,12},{12,8},{9,1... | collective-permute-start | bytes 3145736 | tf_op jit(solution)/shard_map/ppermute | solution.py:41
  99.5 93.9 %all-gather.16.cloned.1.call-start = ((), (), s32[]{:S(2)}) async-start(), calls=%async_computation.4 | async-start | bytes 2621440 | tf_op jit(solution)/shard_map/all_gather | solution.py:1237
  100.4 21.6 %collective-permute-start.13 = (bf16[1024,512]{1,0:T(8,128)(2,1)}, bf16[1024,512]{1,0:T(8,128)(2,1)S(1)}, u32[]{:S(2)}, u32[]{:S(2)}) collective-permute-start(bf16[1024,512]{1,0:T(8,128)(2,1)} %all-gather.12.cloned.1.call-done.refs_0_.refs_15_), channel_id=1, source_target_pairs={{0,1},{1,0},{2,3},{3,2},{4,5},{5,4},{6,7},{7,6},{8,9},{9,8},{10,11... | collective-permute-start | bytes 3145736 | tf_op jit(solution)/shard_map/ppermute | solution.py:33
  100.5 24.6 %collective-permute-start.14 = (bf16[1024,512]{1,0:T(8,128)(2,1)}, bf16[1024,512]{1,0:T(8,128)(2,1)}, u32[]{:S(2)}, u32[]{:S(2)}) collective-permute-start(bf16[1024,512]{1,0:T(8,128)(2,1)} %all-gather.12.cloned.1.call-done.refs_0_.refs_15_), channel_id=1, source_target_pairs={{0,2},{2,0},{1,3},{3,1},{4,6},{6,4},{5,7},{7,5},{8,10},{10,8},{9,1... | collective-permute-start | bytes 3145736 | tf_op jit(solution)/shard_map/ppermute | solution.py:37
  101.7 24.3 %collective-permute-start.16 = (bf16[1024,512]{1,0:T(8,128)(2,1)}, bf16[1024,512]{1,0:T(8,128)(2,1)}, u32[]{:S(2)}, u32[]{:S(2)}) collective-permute-start(bf16[1024,512]{1,0:T(8,128)(2,1)} %all-gather.12.cloned.1.call-done.refs_0_.refs_15_), channel_id=1, source_target_pairs={{0,4},{4,0},{1,5},{5,1},{2,6},{6,2},{3,7},{7,3},{8,12},{12,8},{9,1... | collective-permute-start | bytes 3145736 | tf_op jit(solution)/shard_map/ppermute | solution.py:41
  128.9 318.2 %all-gather.18.cloned.1.call-start = ((), (), s32[]{:S(2)}) async-start(), calls=%async_computation.5 | async-start | bytes 3244032 | tf_op jit(solution)/shard_map/all_gather | solution.py:1277
  129.0 24.2 %collective-permute-start.18 = (bf16[1024,512]{1,0:T(8,128)(2,1)}, bf16[1024,512]{1,0:T(8,128)(2,1)S(1)}, u32[]{:S(2)}, u32[]{:S(2)}) collective-permute-start(bf16[1024,512]{1,0:T(8,128)(2,1)} %collective-permute-done.14.refs_2_.refs_17_), channel_id=1, source_target_pairs={{0,4},{4,0},{1,5},{5,1},{2,6},{6,2},{3,7},{7,3},{8,12},{12,8},{9,1... | collective-permute-start | bytes 3145736 | tf_op jit(solution)/shard_map/ppermute | solution.py:41
  130.2 12.6 %collective-permute-start.8 = (bf16[256,1024]{1,0:T(8,128)(2,1)}, bf16[256,1024]{1,0:T(8,128)(2,1)S(1)}, u32[]{:S(2)}, u32[]{:S(2)}) collective-permute-start(bf16[256,1024]{1,0:T(8,128)(2,1)} %copy-done.83), channel_id=1, source_target_pairs={{0,2},{2,0},{1,3},{3,1},{4,6},{6,4},{5,7},{7,5},{8,10},{10,8},{9,1... | collective-permute-start | bytes 1572872 | tf_op jit(solution)/shard_map/ppermute | solution.py:37
  131.4 25.9 %collective-permute-start.15 = (bf16[1024,512]{1,0:T(8,128)(2,1)}, bf16[1024,512]{1,0:T(8,128)(2,1)S(1)}, u32[]{:S(2)}, u32[]{:S(2)}) collective-permute-start(bf16[1024,512]{1,0:T(8,128)(2,1)} %collective-permute-done.14.refs_2_.refs_17_), channel_id=1, source_target_pairs={{0,1},{1,0},{2,3},{3,2},{4,5},{5,4},{6,7},{7,6},{8,9},{9,8},{10,11... | collective-permute-start | bytes 3145736 | tf_op jit(solution)/shard_map/ppermute | solution.py:33
  132.8 24.5 %collective-permute-start.17 = (bf16[1024,512]{1,0:T(8,128)(2,1)}, bf16[1024,512]{1,0:T(8,128)(2,1)S(1)}, u32[]{:S(2)}, u32[]{:S(2)}) collective-permute-start(bf16[1024,512]{1,0:T(8,128)(2,1)} %collective-permute-done.16.refs_4_.refs_19_), channel_id=1, source_target_pairs={{0,1},{1,0},{2,3},{3,2},{4,5},{5,4},{6,7},{7,6},{8,9},{9,8},{10,11... | collective-permute-start | bytes 3145736 | tf_op jit(solution)/shard_map/ppermute | solution.py:33
  156.1 38.8 %collective-permute-start.29 = (bf16[1024,384]{1,0:T(8,128)(2,1)S(1)}, bf16[1024,384]{1,0:T(8,128)(2,1)}, u32[]{:S(2)}, u32[]{:S(2)}) collective-permute-start(bf16[1024,384]{1,0:T(8,128)(2,1)S(1)} %slice.111.refs_8_.refs_6_.refs_7_.refs_23_), channel_id=1, source_target_pairs={{0,4},{4,0},{1,5},{5,1},{2,6},{6,2},{3,7},{7,3},{8,12},{12,8},{9,1... | collective-permute-start | bytes 2359304 | tf_op jit(solution)/shard_map/ppermute | solution.py:41
  169.9 13.3 %collective-permute-start.21 = (bf16[256,768]{1,0:T(8,128)(2,1)S(1)}, bf16[256,768]{1,0:T(8,128)(2,1)S(1)}, u32[]{:S(2)}, u32[]{:S(2)}) collective-permute-start(bf16[256,768]{1,0:T(8,128)(2,1)S(1)} %get-tuple-element.110), channel_id=1, source_target_pairs={{0,4},{4,0},{1,5},{5,1},{2,6},{6,2},{3,7},{7,3},{8,12},{12,8},{9,1... | collective-permute-start | bytes 1179656 | tf_op jit(solution)/shard_map/ppermute | solution.py:41
  170.6 22.1 %collective-permute-start.22 = (bf16[256,768]{1,0:T(8,128)(2,1)S(1)}, bf16[256,768]{1,0:T(8,128)(2,1)S(1)}, u32[]{:S(2)}, u32[]{:S(2)}) collective-permute-start(bf16[256,768]{1,0:T(8,128)(2,1)S(1)} %get-tuple-element.111), channel_id=1, source_target_pairs={{0,6},{1,7},{2,4},{3,5},{4,2},{5,3},{6,0},{7,1},{8,14},{9,15},{10,... | collective-permute-start | bytes 1179656 | tf_op jit(solution)/shard_map/ppermute | solution.py:45
  193.4 65.0 %collective-permute-start.36 = (bf16[1024,1024]{1,0:T(8,128)(2,1)}, bf16[1024,1024]{1,0:T(8,128)(2,1)S(1)}, u32[]{:S(2)}, u32[]{:S(2)}) collective-permute-start(bf16[1024,1024]{1,0:T(8,128)(2,1)} %all-gather.16.cloned.1.call-done.refs_3_.refs_7_.refs_8_.refs_12_), channel_id=1, source_target_pairs={{0,4},{4,0},{1,5},{5,1},{2,6},{6,2},{3,7},{7,3},{8,12},{12,8},{9,1... | collective-permute-start | bytes 6291464 | tf_op jit(solution)/shard_map/ppermute | solution.py:41
  194.6 23.2 %collective-permute-start.27 = (bf16[1024,384]{1,0:T(8,128)(2,1)S(1)}, bf16[1024,384]{1,0:T(8,128)(2,1)}, u32[]{:S(2)}, u32[]{:S(2)}) collective-permute-start(bf16[1024,384]{1,0:T(8,128)(2,1)S(1)} %slice.111.refs_8_.refs_6_.refs_7_.refs_23_), channel_id=1, source_target_pairs={{0,2},{2,0},{1,3},{3,1},{4,6},{6,4},{5,7},{7,5},{8,10},{10,8},{9,1... | collective-permute-start | bytes 2359304 | tf_op jit(solution)/shard_map/ppermute | solution.py:37
  194.9 34.2 %collective-permute-start.31 = (bf16[1024,384]{1,0:T(8,128)(2,1)}, bf16[1024,384]{1,0:T(8,128)(2,1)}, u32[]{:S(2)}, u32[]{:S(2)}) collective-permute-start(bf16[1024,384]{1,0:T(8,128)(2,1)} %collective-permute-done.29.refs_12_.refs_10_.refs_11_.refs_27_), channel_id=1, source_target_pairs={{0,2},{2,0},{1,3},{3,1},{4,6},{6,4},{5,7},{7,5},{8,10},{10,8},{9,1... | collective-permute-start | bytes 2359304 | tf_op jit(solution)/shard_map/ppermute | solution.py:37
  217.1 15.8 %collective-permute-start.23 = (bf16[256,256]{1,0:T(8,128)(2,1)S(1)}, bf16[256,256]{1,0:T(8,128)(2,1)S(1)}, u32[]{:S(2)}, u32[]{:S(2)}) collective-permute-start(bf16[256,256]{1,0:T(8,128)(2,1)S(1)} %get-tuple-element.205), channel_id=1, source_target_pairs={{0,2},{2,0},{1,3},{3,1},{4,6},{6,4},{5,7},{7,5},{8,10},{10,8},{9,1... | collective-permute-start | bytes 393224 | tf_op jit(solution)/shard_map/ppermute | solution.py:37
  217.5 24.8 %collective-permute-start.24 = (bf16[256,256]{1,0:T(8,128)(2,1)S(1)}, bf16[256,256]{1,0:T(8,128)(2,1)S(1)}, u32[]{:S(2)}, u32[]{:S(2)}) collective-permute-start(bf16[256,256]{1,0:T(8,128)(2,1)S(1)} %get-tuple-element.204), channel_id=1, source_target_pairs={{0,4},{4,0},{1,5},{5,1},{2,6},{6,2},{3,7},{7,3},{8,12},{12,8},{9,1... | collective-permute-start | bytes 393224 | tf_op jit(solution)/shard_map/ppermute | solution.py:41
  217.8 28.1 %collective-permute-start.25 = (bf16[256,256]{1,0:T(8,128)(2,1)S(1)}, bf16[256,256]{1,0:T(8,128)(2,1)S(1)}, u32[]{:S(2)}, u32[]{:S(2)}) collective-permute-start(bf16[256,256]{1,0:T(8,128)(2,1)S(1)} %get-tuple-element.203), channel_id=1, source_target_pairs={{0,6},{1,7},{2,4},{3,5},{4,2},{5,3},{6,0},{7,1},{8,14},{9,15},{10,... | collective-permute-start | bytes 393224 | tf_op jit(solution)/shard_map/ppermute | solution.py:45
  229.1 18.2 %collective-permute-start.26 = (bf16[1024,384]{1,0:T(8,128)(2,1)S(1)}, bf16[1024,384]{1,0:T(8,128)(2,1)S(1)}, u32[]{:S(2)}, u32[]{:S(2)}) collective-permute-start(bf16[1024,384]{1,0:T(8,128)(2,1)S(1)} %slice.111.refs_8_.refs_6_.refs_7_.refs_23_), channel_id=1, source_target_pairs={{0,1},{1,0},{2,3},{3,2},{4,5},{5,4},{6,7},{7,6},{8,9},{9,8},{10,11... | collective-permute-start | bytes 2359304 | tf_op jit(solution)/shard_map/ppermute | solution.py:33
  232.9 14.4 %collective-permute-start.28 = (bf16[1024,384]{1,0:T(8,128)(2,1)}, bf16[1024,384]{1,0:T(8,128)(2,1)S(1)}, u32[]{:S(2)}, u32[]{:S(2)}) collective-permute-start(bf16[1024,384]{1,0:T(8,128)(2,1)} %collective-permute-done.27.refs_10_.refs_8_.refs_9_.refs_25_), channel_id=1, source_target_pairs={{0,1},{1,0},{2,3},{3,2},{4,5},{5,4},{6,7},{7,6},{8,9},{9,8},{10,11... | collective-permute-start | bytes 2359304 | tf_op jit(solution)/shard_map/ppermute | solution.py:33
  247.3 39.8 %collective-permute-start.35 = (bf16[1024,1024]{1,0:T(8,128)(2,1)S(1)}, bf16[1024,1024]{1,0:T(8,128)(2,1)S(1)}, u32[]{:S(2)}, u32[]{:S(2)}) collective-permute-start(bf16[1024,1024]{1,0:T(8,128)(2,1)S(1)} %copy-done.2), channel_id=1, source_target_pairs={{0,1},{1,0},{2,3},{3,2},{4,5},{5,4},{6,7},{7,6},{8,9},{9,8},{10,11... | collective-permute-start | bytes 6291464 | tf_op jit(solution)/shard_map/ppermute | solution.py:33
  258.4 28.7 %collective-permute-start.37 = (bf16[1024,1024]{1,0:T(8,128)(2,1)S(1)}, bf16[1024,1024]{1,0:T(8,128)(2,1)}, u32[]{:S(2)}, u32[]{:S(2)}) collective-permute-start(bf16[1024,1024]{1,0:T(8,128)(2,1)S(1)} %collective-permute-done.36.refs_5_.refs_9_.refs_10_.refs_14_), channel_id=1, source_target_pairs={{0,1},{1,0},{2,3},{3,2},{4,5},{5,4},{6,7},{7,6},{8,9},{9,8},{10,11... | collective-permute-start | bytes 6291464 | tf_op jit(solution)/shard_map/ppermute | solution.py:33
  273.6 13.5 %collective-permute-start.34 = (bf16[256,1024]{1,0:T(8,128)(2,1)S(1)}, bf16[256,1024]{1,0:T(8,128)(2,1)S(1)}, u32[]{:S(2)}, u32[]{:S(2)}) collective-permute-start(bf16[256,1024]{1,0:T(8,128)(2,1)S(1)} %get-tuple-element.127.refs_1_.refs_3_), channel_id=1, source_target_pairs={{0,2},{2,0},{1,3},{3,1},{4,6},{6,4},{5,7},{7,5},{8,10},{10,8},{9,1... | collective-permute-start | bytes 1572872 | tf_op jit(solution)/shard_map/ppermute | solution.py:37
  298.3 11.9 %collective-permute-start.38 = (bf16[256,1024]{1,0:T(8,128)(2,1)S(1)}, bf16[256,1024]{1,0:T(8,128)(2,1)S(1)}, u32[]{:S(2)}, u32[]{:S(2)}) collective-permute-start(bf16[256,1024]{1,0:T(8,128)(2,1)S(1)} %get-tuple-element.133), channel_id=1, source_target_pairs={{0,2},{2,0},{1,3},{3,1},{4,6},{6,4},{5,7},{7,5},{8,10},{10,8},{9,1... | collective-permute-start | bytes 1572872 | tf_op jit(solution)/shard_map/ppermute | solution.py:37
  336.3 16.6 %collective-permute-start.50 = (f32[12,32,128]{2,1,0:T(8,128)S(1)}, f32[12,32,128]{2,1,0:T(8,128)S(1)}, u32[]{:S(2)}, u32[]{:S(2)}) collective-permute-start(f32[12,32,128]{2,1,0:T(8,128)S(1)} %slice_bitcast_fusion.5), channel_id=1, source_target_pairs={{0,4},{4,0},{1,5},{5,1},{2,6},{6,2},{3,7},{7,3},{8,12},{12,8},{9,1... | collective-permute-start | bytes 589832 | tf_op jit(solution)/shard_map/ppermute | solution.py:41
  353.7 166.8 %all-gather.20.cloned.1.call-start = ((), (), s32[]{:S(2)}) async-start(), calls=%async_computation.6 | async-start | bytes 3514368 | tf_op jit(solution)/shard_map/all_gather | solution.py:1277
  357.1 21.1 %collective-permute-start.39 = (bf16[256,512]{1,0:T(8,128)(2,1)}, bf16[256,512]{1,0:T(8,128)(2,1)}, u32[]{:S(2)}, u32[]{:S(2)}) collective-permute-start(bf16[256,512]{1,0:T(8,128)(2,1)} %get-tuple-element.202), channel_id=1, source_target_pairs={{0,2},{2,0},{1,3},{3,1},{4,6},{6,4},{5,7},{7,5},{8,10},{10,8},{9,1... | collective-permute-start | bytes 786440 | tf_op jit(solution)/shard_map/ppermute | solution.py:37
  413.1 14.7 %collective-permute-start.47 = (bf16[256,768]{1,0:T(8,128)(2,1)S(1)}, bf16[256,768]{1,0:T(8,128)(2,1)S(1)}, u32[]{:S(2)}, u32[]{:S(2)}) collective-permute-start(bf16[256,768]{1,0:T(8,128)(2,1)S(1)} %get-tuple-element.192), channel_id=1, source_target_pairs={{0,2},{2,0},{1,3},{3,1},{4,6},{6,4},{5,7},{7,5},{8,10},{10,8},{9,1... | collective-permute-start | bytes 1179656 | tf_op jit(solution)/shard_map/ppermute | solution.py:37
  414.3 13.6 %collective-permute-start.48 = (bf16[256,768]{1,0:T(8,128)(2,1)S(1)}, bf16[256,768]{1,0:T(8,128)(2,1)S(1)}, u32[]{:S(2)}, u32[]{:S(2)}) collective-permute-start(bf16[256,768]{1,0:T(8,128)(2,1)S(1)} %get-tuple-element.191), channel_id=1, source_target_pairs={{0,4},{4,0},{1,5},{5,1},{2,6},{6,2},{3,7},{7,3},{8,12},{12,8},{9,1... | collective-permute-start | bytes 1179656 | tf_op jit(solution)/shard_map/ppermute | solution.py:41
  414.4 13.4 %collective-permute-start.49 = (bf16[256,768]{1,0:T(8,128)(2,1)S(1)}, bf16[256,768]{1,0:T(8,128)(2,1)S(1)}, u32[]{:S(2)}, u32[]{:S(2)}) collective-permute-start(bf16[256,768]{1,0:T(8,128)(2,1)S(1)} %get-tuple-element.190), channel_id=1, source_target_pairs={{0,6},{1,7},{2,4},{3,5},{4,2},{5,3},{6,0},{7,1},{8,14},{9,15},{10,... | collective-permute-start | bytes 1179656 | tf_op jit(solution)/shard_map/ppermute | solution.py:45
  471.3 12.6 %collective-permute-start.52 = (bf16[256,1024]{1,0:T(8,128)(2,1)S(1)}, bf16[256,1024]{1,0:T(8,128)(2,1)S(1)}, u32[]{:S(2)}, u32[]{:S(2)}) collective-permute-start(bf16[256,1024]{1,0:T(8,128)(2,1)S(1)} %get-tuple-element.173), channel_id=1, source_target_pairs={{0,2},{2,0},{1,3},{3,1},{4,6},{6,4},{5,7},{7,5},{8,10},{10,8},{9,1... | collective-permute-start | bytes 1572872 | tf_op jit(solution)/shard_map/ppermute | solution.py:37
  486.0 26.5 %collective-permute-start.61 = (bf16[4,10,32,128]{3,2,1,0:T(8,128)(2,1)S(1)}, bf16[4,10,32,128]{3,2,1,0:T(8,128)(2,1)S(1)}, u32[]{:S(2)}, u32[]{:S(2)}) collective-permute-start(bf16[4,10,32,128]{3,2,1,0:T(8,128)(2,1)S(1)} %pad_maximum_fusion.1.refs_3_), channel_id=1, source_target_pairs={{0,2},{2,0},{1,3},{3,1},{4,6},{6,4},{5,7},{7,5},{8,10},{10,8},{9,1... | collective-permute-start | bytes 983048 | tf_op jit(solution)/shard_map/ppermute | solution.py:37
  489.8 25.0 %collective-permute-start.65 = (bf16[4,10,32,128]{3,2,1,0:T(8,128)(2,1)S(1)}, bf16[4,10,32,128]{3,2,1,0:T(8,128)(2,1)S(1)}, u32[]{:S(2)}, u32[]{:S(2)}) collective-permute-start(bf16[4,10,32,128]{3,2,1,0:T(8,128)(2,1)S(1)} %collective-permute-done.63.refs_7_), channel_id=1, source_target_pairs={{0,2},{2,0},{1,3},{3,1},{4,6},{6,4},{5,7},{7,5},{8,10},{10,8},{9,1... | collective-permute-start | bytes 983048 | tf_op jit(solution)/shard_map/ppermute | solution.py:37
  494.7 23.7 %collective-permute-start.54 = (bf16[1,512,256]{2,1,0:T(8,128)(2,1)}, bf16[1,512,256]{2,1,0:T(8,128)(2,1)S(1)}, u32[]{:S(2)}, u32[]{:S(2)}) collective-permute-start(bf16[1,512,256]{2,1,0:T(8,128)(2,1)} %get-tuple-element.196), channel_id=1, source_target_pairs={{0,1},{1,0},{2,3},{3,2},{4,5},{5,4},{6,7},{7,6},{8,9},{9,8},{10,11... | collective-permute-start | bytes 786440 | tf_op jit(solution)/shard_map/ppermute | solution.py:33
  511.9 14.4 %collective-permute-start.60 = (bf16[4,10,32,128]{3,2,1,0:T(8,128)(2,1)S(1)}, bf16[4,10,32,128]{3,2,1,0:T(8,128)(2,1)S(1)}, u32[]{:S(2)}, u32[]{:S(2)}) collective-permute-start(bf16[4,10,32,128]{3,2,1,0:T(8,128)(2,1)S(1)} %pad_maximum_fusion.1.refs_3_), channel_id=1, source_target_pairs={{0,1},{1,0},{2,3},{3,2},{4,5},{5,4},{6,7},{7,6},{8,9},{9,8},{10,11... | collective-permute-start | bytes 983048 | tf_op jit(solution)/shard_map/ppermute | solution.py:33
  511.9 14.4 %collective-permute-start.64 = (bf16[4,10,32,128]{3,2,1,0:T(8,128)(2,1)S(1)}, bf16[4,10,32,128]{3,2,1,0:T(8,128)(2,1)S(1)}, u32[]{:S(2)}, u32[]{:S(2)}) collective-permute-start(bf16[4,10,32,128]{3,2,1,0:T(8,128)(2,1)S(1)} %collective-permute-done.63.refs_7_), channel_id=1, source_target_pairs={{0,1},{1,0},{2,3},{3,2},{4,5},{5,4},{6,7},{7,6},{8,9},{9,8},{10,11... | collective-permute-start | bytes 983048 | tf_op jit(solution)/shard_map/ppermute | solution.py:33
  512.4 13.9 %collective-permute-start.62 = (bf16[4,10,32,128]{3,2,1,0:T(8,128)(2,1)S(1)}, bf16[4,10,32,128]{3,2,1,0:T(8,128)(2,1)S(1)}, u32[]{:S(2)}, u32[]{:S(2)}) collective-permute-start(bf16[4,10,32,128]{3,2,1,0:T(8,128)(2,1)S(1)} %collective-permute-done.61.refs_5_), channel_id=1, source_target_pairs={{0,1},{1,0},{2,3},{3,2},{4,5},{5,4},{6,7},{7,6},{8,9},{9,8},{10,11... | collective-permute-start | bytes 983048 | tf_op jit(solution)/shard_map/ppermute | solution.py:33
  514.8 11.6 %collective-permute-start.66 = (bf16[4,10,32,128]{3,2,1,0:T(8,128)(2,1)S(1)}, bf16[4,10,32,128]{3,2,1,0:T(8,128)(2,1)S(1)}, u32[]{:S(2)}, u32[]{:S(2)}) collective-permute-start(bf16[4,10,32,128]{3,2,1,0:T(8,128)(2,1)S(1)} %collective-permute-done.65.refs_9_), channel_id=1, source_target_pairs={{0,1},{1,0},{2,3},{3,2},{4,5},{5,4},{6,7},{7,6},{8,9},{9,8},{10,11... | collective-permute-start | bytes 983048 | tf_op jit(solution)/shard_map/ppermute | solution.py:33
  (140 other events, 1857.2 us)
Sparse Core Ops, SparseCore 0:
  10.2 29.7 all-gather.7
  42.2 27.5 all-gather.9
  72.0 27.4 all-gather.11
  101.4 27.4 all-gather.13
  130.9 45.5 all-gather.15
  353.8 63.3 all-gather.17
  447.1 72.6 all-gather.19

commit v5 on v4

--- a/solution.py
+++ b/solution.py
@@ -1091,25 +1091,28 @@
     held = refs[-len(plan) - 1 : -1]
     sems = refs[-1]
     copies = []
+    def rows_at(near, block, rows):
+        return [pieces[2 * near + core][:, block, rows, :].reshape(-1, LANES) for core in range(2)]
+
     for item, (wide, kind, slot, group) in enumerate(plan):
         rows = slice(group * RANK, (group + 1) * RANK)
-        order = [0, 1] if not wide else list(range(2, pieces[0].shape[1]))
-        column = len(order) * LANES
+        blocks = [0, 1] if not wide else list(range(4, pieces[0].shape[1]))
+        column = len(blocks) * LANES
+        times = 1 if wide else 2
         for near in range(near_count):
-            parts = [
-                jnp.concatenate(
-                    [pieces[2 * near + core][:, n, rows, :].reshape(-1, LANES) for core in range(2)],
-                    axis=0,
-                )
-                for n in order
-            ]
+            parts = []
+            for n in blocks:
+                found = rows_at(near, n, rows)
+                if not wide:
+                    found += rows_at(near ^ 1, n + 2, rows)
+                parts.append(jnp.concatenate(found, axis=0))
             value = jnp.concatenate(parts, axis=1)
             pair, side = where[0] ^ (near % 2), where[2] ^ (near // 2)
             place = pl.ds(pl.multiple_of((2 * pair + side) * column, column), column)
             if kind % 2 == 0:
-                held[item][place, :] = tn(value, spread[...])
+                held[item][place, :] = tn(value, jnp.concatenate([spread[...]] * times, axis=0))
             else:
-                held[item][:, place] = nn(turned[...], value)
+                held[item][:, place] = nn(jnp.concatenate([turned[...]] * times, axis=1), value)
         at = sorted({k for _, k, _, _ in plan}).index(kind)
         copy = pltpu.make_async_copy(held[item], outs[at].at[slot], sems.at[item])
         copy.start()
@@ -1434,7 +1437,6 @@
         0, 0, 7, after(where, outs[0]), half, other_half, *kept_one, w1_in, w1_out, adapters
     )
     sums_one = sums_one[0] + by_side(sums_one[1].astype(BF)).astype(F32)
-    sums_one = jnp.concatenate([sums_one[:2] + by_pair(sums_one[2:4]), sums_one[4:]], axis=0)
     line = around_shard(sums_one.astype(BF))
     pieces = [line, by_pair(line), by_side(line)]
     pieces.append(by_pair(pieces[2]))
@@ -1449,11 +1451,11 @@
         (kind, slot, rows_of(0, head_blocks, head_rows, g))
         for g, (kind, slot) in enumerate(places)
     ]
-    outs = expand(plan, spread, turned, found_heads, outs)
     outs = expand_near(
         [(False, 0, 0, 0), (False, 1, 7, 1), (True, 2, 0, 0), (True, 3, 0, 1)],
         where, spread_near, turned_near, pieces, outs,
     )
+    outs = expand(plan, spread, turned, found_heads, outs)
     return (output, input_grad, outs[0], outs[2], outs[1], outs[3])
 
 

time: 549 us -> 547 us (level)
    ppermute x23 -> x22, waiting for transfers between devices: 94.8 us -> 92 us  [by_pair(): return lax.ppermute(value, 'tp', PAIR)]
    ppermute x23 -> x22, starting transfers between devices: 22.3 us -> 19.9 us  [by_pair(): return lax.ppermute(value, 'tp', PAIR)]
    unnamed x228 -> x224, local copies, waits for them, and re-layouts: 45.3 us -> 43.6 us
  transfers between devices with their start and end apart: 76 -> 75, of which waited for: 37 -> 35; matrix products, arithmetic and copies ran while one was open for 5% -> 5% of each run, Pallas kernels for 22% -> 22%
where the time goes in v5:
time: 547 us; the launch traced here: 537 us
  waiting for transfers between devices  193 us (35%)
  Pallas kernels  149 us (27%)
  starting transfers between devices  99.6 us (18%)
  local copies, waits for them, and re-layouts  58.3 us (11%)
  between operations  16.6 us (3%)
  other arithmetic  13.2 us (2%)
  blocking collectives  7.87 us (1%)
    pallas_call x13, Pallas kernels, run(): pl.pallas_call(body, name=name, in_specs=specs, out_specs=out_specs or [V...  93.8 us
    ppermute x22, waiting for transfers between devices, by_pair(): return lax.ppermute(value, 'tp', PAIR)  92 us
    ppermute x14, waiting for transfers between devices, by_side(): return lax.ppermute(value, 'ctx', SIDE)  68.5 us
    ppermute x23, starting transfers between devices, by_core(): return lax.ppermute(value, 'tp', CORE)  52.4 us
    unnamed x224, local copies, waits for them, and re-layouts  43.6 us
    pallas_call x1, Pallas kernels, attend_back(): pl.pallas_call(bwd_kernel, grid_spec=pltpu.PrefetchScalarGridSpec(num_sca...  29.4 us
    ppermute x22, starting transfers between devices, by_pair(): return lax.ppermute(value, 'tp', PAIR)  19.9 us
    pallas_call x1, Pallas kernels, attend(): pl.pallas_call(fwd_kernel, grid_spec=pltpu.PrefetchScalarGridSpec(num_sca...  14.8 us
  transfers between devices with their start and end apart: 75, of which 35 were waited for; matrix products, arithmetic and copies ran while one was open for 5% of the time, Pallas kernels for 22%

profile of v5, /device:TPU:1, one launch (start us, length us, event | category | flops | bytes accessed | tf_op | source)
XLA Modules:
  0.0 537.2 jit_solution(8093135993858698482)
XLA Ops:
  12.3 7.9 %all-reduce = s32[8]{0:T(128)S(1)} all-reduce(s32[8]{0:T(128)S(1)} %dynamic-update-slice), channel_id=1, replica_groups=mesh['shard'=4,'ctx'=2,'tp'=4] {'shard'}, use_global_device_ids=true, to_apply=%add | all-reduce | flops 8 | bytes 64
  25.3 9.2 %collective-permute-done.1 = bf16[512,512]{1,0:T(8,128)(2,1)S(1)} collective-permute-done((bf16[512,512]{1,0:T(8,128)(2,1)S(1)}, bf16[512,512]{1,0:T(8,128)(2,1)S(1)}, u32[]{:S(2)}, u32[]{:S(2)}) %collective-permute-start.1) | collective-permute-done | bytes 524320 | tf_op jit(solution)/shard_map/ppermute | solution.py:37
  48.1 7.1 %collective-permute-done.12 = bf16[256,512]{1,0:T(8,128)(2,1)S(1)} collective-permute-done((bf16[256,512]{1,0:T(8,128)(2,1)S(1)}, bf16[256,512]{1,0:T(8,128)(2,1)S(1)}, u32[]{:S(2)}, u32[]{:S(2)}) %collective-permute-start.12) | collective-permute-done | bytes 262176 | tf_op jit(solution)/shard_map/ppermute | solution.py:37
  56.1 12.5 %collective-permute-done.3.refs_5_.refs_10_ = bf16[1024,512]{1,0:T(8,128)(2,1)} collective-permute-done((bf16[1024,512]{1,0:T(8,128)(2,1)}, bf16[1024,512]{1,0:T(8,128)(2,1)}, u32[]{:S(2)}, u32[]{:S(2)}) %collective-permute-start.3) | collective-permute-done | bytes 1048608 | tf_op jit(solution)/shard_map/ppermute | solution.py:41
  75.0 20.5 %collective-permute-done.6.refs_9_.refs_14_ = bf16[1024,512]{1,0:T(8,128)(2,1)} collective-permute-done((bf16[1024,512]{1,0:T(8,128)(2,1)}, bf16[1024,512]{1,0:T(8,128)(2,1)}, u32[]{:S(2)}, u32[]{:S(2)}) %collective-permute-start.6) | collective-permute-done | bytes 1048608 | tf_op jit(solution)/shard_map/ppermute | solution.py:41
  95.5 4.0 all-gather.12.cloned.1.call-done.refs_0_.refs_15_
  108.3 11.2 %hidden_forward.2 = (f32[256,1024]{1,0:T(8,128)S(1)}, bf16[256,1024]{1,0:T(8,128)(2,1)S(1)}, f32[4,512,512]{2,1,0:T(8,128)}, bf16[512,128]{1,0:T(8,128)(2,1)S(1)}, bf16[512,128]{1,0:T(8,128)(2,1)S(1)}) custom-call(s32[4]{0:T(128)S(1)} %pad_add_fusion.where.refs_0_, bf16[256,1024]{1,0:T(8,128)(2,1)S(1)} %get-tuple-element.97.refs_1_.refs_3_, ...), custom_call_target="tpu_custom_call" | custom-call | flops 4294967296 | bytes 16777216 | tf_op jit(solution)/shard_map/hidden_forward/pallas_call | solution.py:320
  122.0 3.1 collective-permute-done.14.refs_2_.refs_17_
  126.0 2.9 all-gather.14.cloned.1.call-done
  132.8 10.1 %collective-permute-done.8.other = bf16[256,1024]{1,0:T(8,128)(2,1)S(1)} collective-permute-done((bf16[256,1024]{1,0:T(8,128)(2,1)}, bf16[256,1024]{1,0:T(8,128)(2,1)S(1)}, u32[]{:S(2)}, u32[]{:S(2)}) %collective-permute-start.8) | collective-permute-done | bytes 524320 | tf_op jit(solution)/shard_map/ppermute | solution.py:37
  142.9 10.3 %collective-permute-done.18.refs_6_.refs_21_ = bf16[1024,512]{1,0:T(8,128)(2,1)S(1)} collective-permute-done((bf16[1024,512]{1,0:T(8,128)(2,1)}, bf16[1024,512]{1,0:T(8,128)(2,1)S(1)}, u32[]{:S(2)}, u32[]{:S(2)}) %collective-permute-start.18) | collective-permute-done | bytes 1048608 | tf_op jit(solution)/shard_map/ppermute | solution.py:41
  159.9 6.3 %heads_forward.1 = (f32[256,1024]{1,0:T(8,128)S(1)}, bf16[256,768]{1,0:T(8,128)(2,1)S(1)}, bf16[256,768]{1,0:T(8,128)(2,1)S(1)}, bf16[256,768]{1,0:T(8,128)(2,1)...) custom-call(s32[4]{0:T(128)S(1)} %pad_add_fusion.where.refs_0_, f32[256,1024]{1,0:T(8,128)S(1)} %copy-done.17, ...), custom_call_target="tpu_custom_call" | custom-call | flops 1610612736 | bytes 16777216 | tf_op jit(solution)/shard_map/heads_forward/pallas_call | solution.py:320
  171.3 7.3 %collective-permute-done.20.s1 = bf16[256,768]{1,0:T(8,128)(2,1)S(1)} collective-permute-done((bf16[256,768]{1,0:T(8,128)(2,1)S(1)}, bf16[256,768]{1,0:T(8,128)(2,1)S(1)}, u32[]{:S(2)}, u32[]{:S(2)}) %collective-permute-start.20) | collective-permute-done | bytes 393248 | tf_op jit(solution)/shard_map/ppermute | solution.py:37
  179.5 3.8 collective-permute-done.21.s2
  184.0 8.6 %collective-permute-done.22.s3 = bf16[256,768]{1,0:T(8,128)(2,1)S(1)} collective-permute-done((bf16[256,768]{1,0:T(8,128)(2,1)S(1)}, bf16[256,768]{1,0:T(8,128)(2,1)S(1)}, u32[]{:S(2)}, u32[]{:S(2)}) %collective-permute-start.22) | collective-permute-done | bytes 393248 | tf_op jit(solution)/shard_map/ppermute | solution.py:45
  200.9 14.8 %attend.1 = (bf16[4,256,256]{2,1,0:T(8,128)(2,1)S(1)}, f32[4,1024,1]{2,1,0:T(8,128)S(1)}) custom-call(s32[1]{0:T(128)} %bitcast.14.b_ref, bf16[256,768]{1,0:T(8,128)(2,1)S(1)} %copy-done.83, bf16[256,768]{1,0:T(8,128)(2,1)S(1)} %copy-done.86, bf16[256,768]{1,0:T(8,128)(2,1)S(1)} %copy-done.89, bf16[256,768]{1,0:T(8,128)(2,1)S(1)} %copy-done.92, ...), custom_call_target="tpu_custom_call" | custom-call | flops 1073741824 | bytes 2097152 | tf_op jit(solution)/shard_map/attend/pallas_call | solution.py:112
  219.8 9.2 %collective-permute-done.31.refs_14_.refs_12_.refs_13_.refs_29_ = bf16[1024,384]{1,0:T(8,128)(2,1)} collective-permute-done((bf16[1024,384]{1,0:T(8,128)(2,1)}, bf16[1024,384]{1,0:T(8,128)(2,1)}, u32[]{:S(2)}, u32[]{:S(2)}) %collective-permute-start.31) | collective-permute-done | bytes 786464 | tf_op jit(solution)/shard_map/ppermute | solution.py:37
  229.0 3.8 collective-permute-start.26
  234.2 8.1 %collective-permute-done.24.m2.refs_12_ = bf16[256,256]{1,0:T(8,128)(2,1)S(1)} collective-permute-done((bf16[256,256]{1,0:T(8,128)(2,1)S(1)}, bf16[256,256]{1,0:T(8,128)(2,1)S(1)}, u32[]{:S(2)}, u32[]{:S(2)}) %collective-permute-start.24) | collective-permute-done | bytes 131104 | tf_op jit(solution)/shard_map/ppermute | solution.py:41
  242.3 3.6 collective-permute-start.30
  249.5 6.8 %pair_forward.1 = (f32[256,1024]{1,0:T(8,128)S(1)}, f32[256,1024]{1,0:T(8,128)S(1)}, f32[256,1024]{1,0:T(8,128)S(1)}, f32[2,2,32,256]{3,2,1,0:T(8,128)S(1)}, bf1...) custom-call(s32[4]{0:T(128)S(1)} %pad_add_fusion.where.refs_0_, f32[256,1024]{1,0:T(8,128)} %copy-done.15, ...), custom_call_target="tpu_custom_call" | custom-call | flops 1610612736 | bytes 16777216 | tf_op jit(solution)/shard_map/pair_forward/pallas_call | solution.py:320
  258.8 3.3 collective-permute-start.33
  262.1 2.5 collective-permute-done.33.refs_4_
  264.7 6.8 %conv_forward.1 = (f32[256,1024]{1,0:T(8,128)S(1)}, f32[256,1024]{1,0:T(8,128)S(1)}, bf16[256,1024]{1,0:T(8,128)(2,1)S(1)}, bf16[256,128]{1,0:T(8,128)(2,1)S(1)}) custom-call(s32[4]{0:T(128)S(1)} %pad_add_fusion.where.refs_0_, f32[256,1024]{1,0:T(8,128)S(1)} %get-tuple-element.122.refs_1_.refs_7_, f32[256,1024]{1,0:T(8,128)} %copy-done.21, ...), custom_call_target="tpu_custom_call" | custom-call | flops 536870912 | bytes 16777216 | tf_op jit(solution)/shard_map/conv_forward/pallas_call | solution.py:320
  275.8 11.3 %collective-permute-done.34.refs_2_.refs_4_ = bf16[256,1024]{1,0:T(8,128)(2,1)S(1)} collective-permute-done((bf16[256,1024]{1,0:T(8,128)(2,1)S(1)}, bf16[256,1024]{1,0:T(8,128)(2,1)S(1)}, u32[]{:S(2)}, u32[]{:S(2)}) %collective-permute-start.34) | collective-permute-done | bytes 524320 | tf_op jit(solution)/shard_map/ppermute | solution.py:37
  287.1 11.2 %hidden_forward.3 = (f32[256,1024]{1,0:T(8,128)S(1)}, bf16[256,1024]{1,0:T(8,128)(2,1)S(1)}, f32[4,512,512]{2,1,0:T(8,128)}, bf16[512,128]{1,0:T(8,128)(2,1)S(1)}, bf16[512,128]{1,0:T(8,128)(2,1)S(1)}) custom-call(s32[4]{0:T(128)S(1)} %pad_add_fusion.where.refs_0_, bf16[256,1024]{1,0:T(8,128)(2,1)S(1)} %get-tuple-element.127.refs_1_.refs_3_, ...), custom_call_target="tpu_custom_call" | custom-call | flops 4294967296 | bytes 16777216 | tf_op jit(solution)/shard_map/hidden_forward/pallas_call | solution.py:320
  299.5 10.7 %collective-permute-done.38.other = bf16[256,1024]{1,0:T(8,128)(2,1)S(1)} collective-permute-done((bf16[256,1024]{1,0:T(8,128)(2,1)S(1)}, bf16[256,1024]{1,0:T(8,128)(2,1)S(1)}, u32[]{:S(2)}, u32[]{:S(2)}) %collective-permute-start.38) | collective-permute-done | bytes 524320 | tf_op jit(solution)/shard_map/ppermute | solution.py:37
  312.5 10.1 %collective-permute-done.41.refs_2_ = bf16[256,1024]{1,0:T(8,128)(2,1)S(1)} collective-permute-done((bf16[256,1024]{1,0:T(8,128)(2,1)S(1)}, bf16[256,1024]{1,0:T(8,128)(2,1)S(1)}, u32[]{:S(2)}, u32[]{:S(2)}) %collective-permute-start.41) | collective-permute-done | bytes 524320 | tf_op jit(solution)/shard_map/ppermute | solution.py:37
  322.6 12.2 %hidden_backward.2 = (f32[256,1024]{1,0:T(8,128)S(1)}, bf16[256,1024]{1,0:T(8,128)(2,1)S(1)}, f32[2,12,32,128]{3,2,1,0:T(8,128)S(1)}) custom-call(s32[4]{0:T(128)S(1)} %pad_add_fusion.where.refs_0_, bf16[256,1024]{1,0:T(8,128)(2,1)S(1)} %get-tuple-element.137.refs_1_, bf16[256,1024]{1,0:T(8,128)(2,1)S(1)} %collective-permute-done.41.refs_2_, ...), custom_call_target="tpu_custom_call" | custom-call | flops 4294967296 | bytes 16777216 | tf_op jit(solution)/shard_map/hidden_backward/pallas_call | solution.py:320
  337.5 8.3 %collective-permute-done.42.refs_3_ = bf16[256,1024]{1,0:T(8,128)(2,1)S(1)} collective-permute-done((bf16[256,1024]{1,0:T(8,128)(2,1)S(1)}, bf16[256,1024]{1,0:T(8,128)(2,1)S(1)}, u32[]{:S(2)}, u32[]{:S(2)}) %collective-permute-start.42) | collective-permute-done | bytes 524320 | tf_op jit(solution)/shard_map/ppermute | solution.py:37
  345.9 5.1 conv_backward.1
  364.1 11.3 %pair_backward.1 = (f32[256,1024]{1,0:T(8,128)}, bf16[256,256]{1,0:T(8,128)(2,1)S(1)}, bf16[256,256]{1,0:T(8,128)(2,1)S(1)}, bf16[256,256]{1,0:T(8,128)(2,1)S(1)...) custom-call(s32[4]{0:T(128)S(1)} %pad_add_fusion.where.refs_0_, ...), custom_call_target="tpu_custom_call" | custom-call | flops 1610612736 | bytes 16777216 | tf_op jit(solution)/shard_map/pair_backward/pallas_call | solution.py:320
  383.5 29.4 %attend_back.1 = bf16[4,256,768]{2,1,0:T(8,128)(2,1)S(1)} custom-call(s32[1]{0:T(128)} %bitcast.14.b_ref, bf16[256,768]{1,0:T(8,128)(2,1)S(1)} %copy-done.84, bf16[256,768]{1,0:T(8,128)(2,1)S(1)} %copy-done.87, bf16[256,768]{1,0:T(8,128)(2,1)S(1)} %copy-done.90, bf16[256,768]{1,0:T(8,128)(2,1)S(1)} %copy-done.93, ...), custom_call_target="tpu_custom_call" | custom-call | flops 2684354560 | bytes 3670016 | tf_op jit(solution)/shard_map/attend_back/pallas_call | solution.py:184
  415.9 9.9 %collective-permute-start.40 = (bf16[1,512,256]{2,1,0:T(8,128)(2,1)S(1)}, bf16[1,512,256]{2,1,0:T(8,128)(2,1)S(1)}, u32[]{:S(2)}, u32[]{:S(2)}) collective-permute-start(bf16[1,512,256]{2,1,0:T(8,128)(2,1)S(1)} %get-tuple-element.200), channel_id=1, source_target_pairs={{0,1},{1,0},{2,3},{3,2},{4,5},{5,4},{6,7},{7,6},{8,9},{9,8},{10,11... | collective-permute-start | bytes 786440 | tf_op jit(solution)/shard_map/ppermute | solution.py:33
  427.9 7.0 %heads_backward.1 = (f32[256,1024]{1,0:T(8,128)S(1)}, bf16[256,1024]{1,0:T(8,128)(2,1)S(1)}, f32[2,2,2,208,128]{4,3,2,1,0:T(8,128)S(1)}) custom-call(s32[4]{0:T(128)S(1)} %pad_add_fusion.where.refs_0_, f32[256,1024]{1,0:T(8,128)S(1)} %copy-done.44, f32[256,1024]{1,0:T(8,128)S(1)} %copy-done.16, bf16[256,384]{1,0:T(8,128)(2,1)S(1)} %copy-done.68, ...), custom_call_target="tpu_custom_call" | custom-call | flops 1610612736 | bytes 16777216 | tf_op jit(solution)/shard_map/heads_backward/pallas_call | solution.py:320
  437.1 3.6 collective-permute-done.55
  441.1 4.3 collective-permute-done.56
  449.1 3.2 expand.2
  455.3 12.2 %hidden_backward.3 = (f32[256,1024]{1,0:T(8,128)S(1)}, bf16[256,1024]{1,0:T(8,128)(2,1)S(1)}, f32[2,12,32,128]{3,2,1,0:T(8,128)S(1)}) custom-call(s32[4]{0:T(128)S(1)} %pad_add_fusion.where.refs_0_, bf16[256,1024]{1,0:T(8,128)(2,1)S(1)} %copy-done.61, bf16[256,1024]{1,0:T(8,128)(2,1)S(1)} %copy-done.63, bf16[256,1024]{1,0:T(8,128)(2,1)S(1)} %copy-done.38, ...), custom_call_target="tpu_custom_call" | custom-call | flops 4294967296 | bytes 16777216 | tf_op jit(solution)/shard_map/hidden_backward/pallas_call | solution.py:320
  471.1 3.5 collective-permute-start.60
  476.2 4.1 collective-permute-done.59
  484.5 5.9 %collective-permute-done.64.refs_7_ = bf16[4,12,32,128]{3,2,1,0:T(8,128)(2,1)S(1)} collective-permute-done((bf16[4,12,32,128]{3,2,1,0:T(8,128)(2,1)S(1)}, bf16[4,12,32,128]{3,2,1,0:T(8,128)(2,1)S(1)}, u32[]{:S(2)}, u32[]{:S(2)}) %collective-permute-start.64) | collective-permute-done | bytes 393248 | tf_op jit(solution)/shard_map/ppermute | solution.py:41
  492.6 12.0 %collective-permute-start.54 = (bf16[1,512,256]{2,1,0:T(8,128)(2,1)}, bf16[1,512,256]{2,1,0:T(8,128)(2,1)}, u32[]{:S(2)}, u32[]{:S(2)}) collective-permute-start(bf16[1,512,256]{2,1,0:T(8,128)(2,1)} %get-tuple-element.196), channel_id=1, source_target_pairs={{0,1},{1,0},{2,3},{3,2},{4,5},{5,4},{6,7},{7,6},{8,9},{9,8},{10,11... | collective-permute-start | bytes 786440 | tf_op jit(solution)/shard_map/ppermute | solution.py:33
  505.1 8.6 %collective-permute-start.63 = (bf16[4,12,32,128]{3,2,1,0:T(8,128)(2,1)S(1)}, bf16[4,12,32,128]{3,2,1,0:T(8,128)(2,1)S(1)}, u32[]{:S(2)}, u32[]{:S(2)}) collective-permute-start(bf16[4,12,32,128]{3,2,1,0:T(8,128)(2,1)S(1)} %collective-permute-done.62.refs_5_), channel_id=1, source_target_pairs={{0,1},{1,0},{2,3},{3,2},{4,5},{5,4},{6,7},{7,6},{8,9},{9,8},{10,11... | collective-permute-start | bytes 1179656 | tf_op jit(solution)/shard_map/ppermute | solution.py:33
  513.7 4.2 collective-permute-start.67
  518.1 2.3 fusion
  520.4 3.7 expand_near.1
  526.1 3.8 expand.3
  (422 shorter events, 138.9 us)
Async XLA Ops:
  7.3 32.8 %all-gather.8.cloned.1.call-start = ((), (), s32[]{:S(2)}) async-start(), calls=%async_computation | async-start | bytes 1310720 | tf_op jit(solution)/shard_map/all_gather | solution.py:1240
  8.5 14.3 %collective-permute-start = (bf16[512,256]{1,0:T(8,128)(2,1)S(1)}, bf16[512,256]{1,0:T(8,128)(2,1)S(1)}, u32[]{:S(2)}, u32[]{:S(2)}) collective-permute-start(bf16[512,256]{1,0:T(8,128)(2,1)S(1)} %get-tuple-element.212), channel_id=1, source_target_pairs={{0,1},{1,0},{2,3},{3,2},{4,5},{5,4},{6,7},{7,6},{8,9},{9,8},{10,11... | collective-permute-start | bytes 786440 | tf_op jit(solution)/shard_map/ppermute | solution.py:33
  9.4 60.4 %all-gather.10.cloned.1.call-start = ((), (), s32[]{:S(2)}) async-start(), calls=%async_computation.1 | async-start | bytes 1310720 | tf_op jit(solution)/shard_map/all_gather | solution.py:1240
  9.5 31.0 %collective-permute-start.9 = (bf16[31,256]{1,0:T(8,128)(2,1)}, bf16[31,256]{1,0:T(8,128)(2,1)}, u32[]{:S(2)}, u32[]{:S(2)}) collective-permute-start(bf16[31,256]{1,0:T(8,128)(2,1)} %param.29), channel_id=1, source_target_pairs={{0,1},{1,0},{2,3},{3,2},{4,5},{5,4},{6,7},{7,6},{8,9},{9,8},{10,11... | collective-permute-start | bytes 47624 | tf_op jit(solution)/shard_map/ppermute | solution.py:33
  10.7 36.5 %collective-permute-start.11 = (bf16[512,256]{1,0:T(8,128)(2,1)}, bf16[512,256]{1,0:T(8,128)(2,1)S(1)}, u32[]{:S(2)}, u32[]{:S(2)}) collective-permute-start(bf16[512,256]{1,0:T(8,128)(2,1)} %get-tuple-element.210), channel_id=1, source_target_pairs={{0,1},{1,0},{2,3},{3,2},{4,5},{5,4},{6,7},{7,6},{8,9},{9,8},{10,11... | collective-permute-start | bytes 786440 | tf_op jit(solution)/shard_map/ppermute | solution.py:33
  23.0 11.5 %collective-permute-start.1 = (bf16[512,512]{1,0:T(8,128)(2,1)S(1)}, bf16[512,512]{1,0:T(8,128)(2,1)S(1)}, u32[]{:S(2)}, u32[]{:S(2)}) collective-permute-start(bf16[512,512]{1,0:T(8,128)(2,1)S(1)} %maximum_select_fusion.1), channel_id=1, source_target_pairs={{0,2},{2,0},{1,3},{3,1},{4,6},{6,4},{5,7},{7,5},{8,10},{10,8},{9,1... | collective-permute-start | bytes 1572872 | tf_op jit(solution)/shard_map/ppermute | solution.py:37
  40.1 59.3 %all-gather.12.cloned.1.call-start = ((), (), s32[]{:S(2)}) async-start(), calls=%async_computation.2 | async-start | bytes 1310720 | tf_op jit(solution)/shard_map/all_gather | solution.py:1240
  42.5 13.6 %collective-permute-start.2 = (bf16[1024,512]{1,0:T(8,128)(2,1)}, bf16[1024,512]{1,0:T(8,128)(2,1)S(1)}, u32[]{:S(2)}, u32[]{:S(2)}) collective-permute-start(bf16[1024,512]{1,0:T(8,128)(2,1)} %all-gather.8.cloned.1.call-done.refs_3_.refs_8_), channel_id=1, source_target_pairs={{0,1},{1,0},{2,3},{3,2},{4,5},{5,4},{6,7},{7,6},{8,9},{9,8},{10,11... | collective-permute-start | bytes 3145736 | tf_op jit(solution)/shard_map/ppermute | solution.py:33
  43.5 25.1 %collective-permute-start.3 = (bf16[1024,512]{1,0:T(8,128)(2,1)}, bf16[1024,512]{1,0:T(8,128)(2,1)}, u32[]{:S(2)}, u32[]{:S(2)}) collective-permute-start(bf16[1024,512]{1,0:T(8,128)(2,1)} %all-gather.8.cloned.1.call-done.refs_3_.refs_8_), channel_id=1, source_target_pairs={{0,4},{4,0},{1,5},{5,1},{2,6},{6,2},{3,7},{7,3},{8,12},{12,8},{9,1... | collective-permute-start | bytes 3145736 | tf_op jit(solution)/shard_map/ppermute | solution.py:41
  69.9 59.0 %all-gather.14.cloned.1.call-start = ((), (), s32[]{:S(2)}) async-start(), calls=%async_computation.3 | async-start | bytes 1310720 | tf_op jit(solution)/shard_map/all_gather | solution.py:1240
  70.9 24.6 %collective-permute-start.6 = (bf16[1024,512]{1,0:T(8,128)(2,1)}, bf16[1024,512]{1,0:T(8,128)(2,1)}, u32[]{:S(2)}, u32[]{:S(2)}) collective-permute-start(bf16[1024,512]{1,0:T(8,128)(2,1)} %all-gather.10.cloned.1.call-done.refs_7_.refs_12_), channel_id=1, source_target_pairs={{0,4},{4,0},{1,5},{5,1},{2,6},{6,2},{3,7},{7,3},{8,12},{12,8},{9,1... | collective-permute-start | bytes 3145736 | tf_op jit(solution)/shard_map/ppermute | solution.py:41
  99.5 93.9 %all-gather.16.cloned.1.call-start = ((), (), s32[]{:S(2)}) async-start(), calls=%async_computation.4 | async-start | bytes 2621440 | tf_op jit(solution)/shard_map/all_gather | solution.py:1240
  100.4 21.6 %collective-permute-start.13 = (bf16[1024,512]{1,0:T(8,128)(2,1)}, bf16[1024,512]{1,0:T(8,128)(2,1)S(1)}, u32[]{:S(2)}, u32[]{:S(2)}) collective-permute-start(bf16[1024,512]{1,0:T(8,128)(2,1)} %all-gather.12.cloned.1.call-done.refs_0_.refs_15_), channel_id=1, source_target_pairs={{0,1},{1,0},{2,3},{3,2},{4,5},{5,4},{6,7},{7,6},{8,9},{9,8},{10,11... | collective-permute-start | bytes 3145736 | tf_op jit(solution)/shard_map/ppermute | solution.py:33
  100.5 24.6 %collective-permute-start.14 = (bf16[1024,512]{1,0:T(8,128)(2,1)}, bf16[1024,512]{1,0:T(8,128)(2,1)}, u32[]{:S(2)}, u32[]{:S(2)}) collective-permute-start(bf16[1024,512]{1,0:T(8,128)(2,1)} %all-gather.12.cloned.1.call-done.refs_0_.refs_15_), channel_id=1, source_target_pairs={{0,2},{2,0},{1,3},{3,1},{4,6},{6,4},{5,7},{7,5},{8,10},{10,8},{9,1... | collective-permute-start | bytes 3145736 | tf_op jit(solution)/shard_map/ppermute | solution.py:37
  101.7 24.3 %collective-permute-start.16 = (bf16[1024,512]{1,0:T(8,128)(2,1)}, bf16[1024,512]{1,0:T(8,128)(2,1)}, u32[]{:S(2)}, u32[]{:S(2)}) collective-permute-start(bf16[1024,512]{1,0:T(8,128)(2,1)} %all-gather.12.cloned.1.call-done.refs_0_.refs_15_), channel_id=1, source_target_pairs={{0,4},{4,0},{1,5},{5,1},{2,6},{6,2},{3,7},{7,3},{8,12},{12,8},{9,1... | collective-permute-start | bytes 3145736 | tf_op jit(solution)/shard_map/ppermute | solution.py:41
  128.9 318.2 %all-gather.18.cloned.1.call-start = ((), (), s32[]{:S(2)}) async-start(), calls=%async_computation.5 | async-start | bytes 3244032 | tf_op jit(solution)/shard_map/all_gather | solution.py:1280
  129.0 24.2 %collective-permute-start.18 = (bf16[1024,512]{1,0:T(8,128)(2,1)}, bf16[1024,512]{1,0:T(8,128)(2,1)S(1)}, u32[]{:S(2)}, u32[]{:S(2)}) collective-permute-start(bf16[1024,512]{1,0:T(8,128)(2,1)} %collective-permute-done.14.refs_2_.refs_17_), channel_id=1, source_target_pairs={{0,4},{4,0},{1,5},{5,1},{2,6},{6,2},{3,7},{7,3},{8,12},{12,8},{9,1... | collective-permute-start | bytes 3145736 | tf_op jit(solution)/shard_map/ppermute | solution.py:41
  130.2 12.6 %collective-permute-start.8 = (bf16[256,1024]{1,0:T(8,128)(2,1)}, bf16[256,1024]{1,0:T(8,128)(2,1)S(1)}, u32[]{:S(2)}, u32[]{:S(2)}) collective-permute-start(bf16[256,1024]{1,0:T(8,128)(2,1)} %copy-done.81), channel_id=1, source_target_pairs={{0,2},{2,0},{1,3},{3,1},{4,6},{6,4},{5,7},{7,5},{8,10},{10,8},{9,1... | collective-permute-start | bytes 1572872 | tf_op jit(solution)/shard_map/ppermute | solution.py:37
  131.4 25.9 %collective-permute-start.15 = (bf16[1024,512]{1,0:T(8,128)(2,1)}, bf16[1024,512]{1,0:T(8,128)(2,1)S(1)}, u32[]{:S(2)}, u32[]{:S(2)}) collective-permute-start(bf16[1024,512]{1,0:T(8,128)(2,1)} %collective-permute-done.14.refs_2_.refs_17_), channel_id=1, source_target_pairs={{0,1},{1,0},{2,3},{3,2},{4,5},{5,4},{6,7},{7,6},{8,9},{9,8},{10,11... | collective-permute-start | bytes 3145736 | tf_op jit(solution)/shard_map/ppermute | solution.py:33
  132.8 24.5 %collective-permute-start.17 = (bf16[1024,512]{1,0:T(8,128)(2,1)}, bf16[1024,512]{1,0:T(8,128)(2,1)S(1)}, u32[]{:S(2)}, u32[]{:S(2)}) collective-permute-start(bf16[1024,512]{1,0:T(8,128)(2,1)} %collective-permute-done.16.refs_4_.refs_19_), channel_id=1, source_target_pairs={{0,1},{1,0},{2,3},{3,2},{4,5},{5,4},{6,7},{7,6},{8,9},{9,8},{10,11... | collective-permute-start | bytes 3145736 | tf_op jit(solution)/shard_map/ppermute | solution.py:33
  156.1 38.8 %collective-permute-start.29 = (bf16[1024,384]{1,0:T(8,128)(2,1)S(1)}, bf16[1024,384]{1,0:T(8,128)(2,1)}, u32[]{:S(2)}, u32[]{:S(2)}) collective-permute-start(bf16[1024,384]{1,0:T(8,128)(2,1)S(1)} %slice.99.refs_8_.refs_6_.refs_7_.refs_23_), channel_id=1, source_target_pairs={{0,4},{4,0},{1,5},{5,1},{2,6},{6,2},{3,7},{7,3},{8,12},{12,8},{9,1... | collective-permute-start | bytes 2359304 | tf_op jit(solution)/shard_map/ppermute | solution.py:41
  169.9 13.4 %collective-permute-start.21 = (bf16[256,768]{1,0:T(8,128)(2,1)S(1)}, bf16[256,768]{1,0:T(8,128)(2,1)S(1)}, u32[]{:S(2)}, u32[]{:S(2)}) collective-permute-start(bf16[256,768]{1,0:T(8,128)(2,1)S(1)} %get-tuple-element.110), channel_id=1, source_target_pairs={{0,4},{4,0},{1,5},{5,1},{2,6},{6,2},{3,7},{7,3},{8,12},{12,8},{9,1... | collective-permute-start | bytes 1179656 | tf_op jit(solution)/shard_map/ppermute | solution.py:41
  170.5 22.1 %collective-permute-start.22 = (bf16[256,768]{1,0:T(8,128)(2,1)S(1)}, bf16[256,768]{1,0:T(8,128)(2,1)S(1)}, u32[]{:S(2)}, u32[]{:S(2)}) collective-permute-start(bf16[256,768]{1,0:T(8,128)(2,1)S(1)} %get-tuple-element.111), channel_id=1, source_target_pairs={{0,6},{1,7},{2,4},{3,5},{4,2},{5,3},{6,0},{7,1},{8,14},{9,15},{10,... | collective-permute-start | bytes 1179656 | tf_op jit(solution)/shard_map/ppermute | solution.py:45
  193.4 65.0 %collective-permute-start.36 = (bf16[1024,1024]{1,0:T(8,128)(2,1)}, bf16[1024,1024]{1,0:T(8,128)(2,1)S(1)}, u32[]{:S(2)}, u32[]{:S(2)}) collective-permute-start(bf16[1024,1024]{1,0:T(8,128)(2,1)} %all-gather.16.cloned.1.call-done.refs_3_.refs_7_.refs_8_.refs_12_), channel_id=1, source_target_pairs={{0,4},{4,0},{1,5},{5,1},{2,6},{6,2},{3,7},{7,3},{8,12},{12,8},{9,1... | collective-permute-start | bytes 6291464 | tf_op jit(solution)/shard_map/ppermute | solution.py:41
  194.6 23.2 %collective-permute-start.27 = (bf16[1024,384]{1,0:T(8,128)(2,1)S(1)}, bf16[1024,384]{1,0:T(8,128)(2,1)}, u32[]{:S(2)}, u32[]{:S(2)}) collective-permute-start(bf16[1024,384]{1,0:T(8,128)(2,1)S(1)} %slice.99.refs_8_.refs_6_.refs_7_.refs_23_), channel_id=1, source_target_pairs={{0,2},{2,0},{1,3},{3,1},{4,6},{6,4},{5,7},{7,5},{8,10},{10,8},{9,1... | collective-permute-start | bytes 2359304 | tf_op jit(solution)/shard_map/ppermute | solution.py:37
  194.8 34.2 %collective-permute-start.31 = (bf16[1024,384]{1,0:T(8,128)(2,1)}, bf16[1024,384]{1,0:T(8,128)(2,1)}, u32[]{:S(2)}, u32[]{:S(2)}) collective-permute-start(bf16[1024,384]{1,0:T(8,128)(2,1)} %collective-permute-done.29.refs_12_.refs_10_.refs_11_.refs_27_), channel_id=1, source_target_pairs={{0,2},{2,0},{1,3},{3,1},{4,6},{6,4},{5,7},{7,5},{8,10},{10,8},{9,1... | collective-permute-start | bytes 2359304 | tf_op jit(solution)/shard_map/ppermute | solution.py:37
  217.1 15.8 %collective-permute-start.23 = (bf16[256,256]{1,0:T(8,128)(2,1)S(1)}, bf16[256,256]{1,0:T(8,128)(2,1)S(1)}, u32[]{:S(2)}, u32[]{:S(2)}) collective-permute-start(bf16[256,256]{1,0:T(8,128)(2,1)S(1)} %get-tuple-element.205), channel_id=1, source_target_pairs={{0,2},{2,0},{1,3},{3,1},{4,6},{6,4},{5,7},{7,5},{8,10},{10,8},{9,1... | collective-permute-start | bytes 393224 | tf_op jit(solution)/shard_map/ppermute | solution.py:37
  217.5 24.8 %collective-permute-start.24 = (bf16[256,256]{1,0:T(8,128)(2,1)S(1)}, bf16[256,256]{1,0:T(8,128)(2,1)S(1)}, u32[]{:S(2)}, u32[]{:S(2)}) collective-permute-start(bf16[256,256]{1,0:T(8,128)(2,1)S(1)} %get-tuple-element.204), channel_id=1, source_target_pairs={{0,4},{4,0},{1,5},{5,1},{2,6},{6,2},{3,7},{7,3},{8,12},{12,8},{9,1... | collective-permute-start | bytes 393224 | tf_op jit(solution)/shard_map/ppermute | solution.py:41
  217.7 28.1 %collective-permute-start.25 = (bf16[256,256]{1,0:T(8,128)(2,1)S(1)}, bf16[256,256]{1,0:T(8,128)(2,1)S(1)}, u32[]{:S(2)}, u32[]{:S(2)}) collective-permute-start(bf16[256,256]{1,0:T(8,128)(2,1)S(1)} %get-tuple-element.203), channel_id=1, source_target_pairs={{0,6},{1,7},{2,4},{3,5},{4,2},{5,3},{6,0},{7,1},{8,14},{9,15},{10,... | collective-permute-start | bytes 393224 | tf_op jit(solution)/shard_map/ppermute | solution.py:45
  229.0 18.2 %collective-permute-start.26 = (bf16[1024,384]{1,0:T(8,128)(2,1)S(1)}, bf16[1024,384]{1,0:T(8,128)(2,1)S(1)}, u32[]{:S(2)}, u32[]{:S(2)}) collective-permute-start(bf16[1024,384]{1,0:T(8,128)(2,1)S(1)} %slice.99.refs_8_.refs_6_.refs_7_.refs_23_), channel_id=1, source_target_pairs={{0,1},{1,0},{2,3},{3,2},{4,5},{5,4},{6,7},{7,6},{8,9},{9,8},{10,11... | collective-permute-start | bytes 2359304 | tf_op jit(solution)/shard_map/ppermute | solution.py:33
  232.9 14.4 %collective-permute-start.28 = (bf16[1024,384]{1,0:T(8,128)(2,1)}, bf16[1024,384]{1,0:T(8,128)(2,1)S(1)}, u32[]{:S(2)}, u32[]{:S(2)}) collective-permute-start(bf16[1024,384]{1,0:T(8,128)(2,1)} %collective-permute-done.27.refs_10_.refs_8_.refs_9_.refs_25_), channel_id=1, source_target_pairs={{0,1},{1,0},{2,3},{3,2},{4,5},{5,4},{6,7},{7,6},{8,9},{9,8},{10,11... | collective-permute-start | bytes 2359304 | tf_op jit(solution)/shard_map/ppermute | solution.py:33
  247.2 39.9 %collective-permute-start.35 = (bf16[1024,1024]{1,0:T(8,128)(2,1)S(1)}, bf16[1024,1024]{1,0:T(8,128)(2,1)S(1)}, u32[]{:S(2)}, u32[]{:S(2)}) collective-permute-start(bf16[1024,1024]{1,0:T(8,128)(2,1)S(1)} %copy-done.2), channel_id=1, source_target_pairs={{0,1},{1,0},{2,3},{3,2},{4,5},{5,4},{6,7},{7,6},{8,9},{9,8},{10,11... | collective-permute-start | bytes 6291464 | tf_op jit(solution)/shard_map/ppermute | solution.py:33
  258.4 28.7 %collective-permute-start.37 = (bf16[1024,1024]{1,0:T(8,128)(2,1)S(1)}, bf16[1024,1024]{1,0:T(8,128)(2,1)}, u32[]{:S(2)}, u32[]{:S(2)}) collective-permute-start(bf16[1024,1024]{1,0:T(8,128)(2,1)S(1)} %collective-permute-done.36.refs_5_.refs_9_.refs_10_.refs_14_), channel_id=1, source_target_pairs={{0,1},{1,0},{2,3},{3,2},{4,5},{5,4},{6,7},{7,6},{8,9},{9,8},{10,11... | collective-permute-start | bytes 6291464 | tf_op jit(solution)/shard_map/ppermute | solution.py:33
  273.6 13.5 %collective-permute-start.34 = (bf16[256,1024]{1,0:T(8,128)(2,1)S(1)}, bf16[256,1024]{1,0:T(8,128)(2,1)S(1)}, u32[]{:S(2)}, u32[]{:S(2)}) collective-permute-start(bf16[256,1024]{1,0:T(8,128)(2,1)S(1)} %get-tuple-element.127.refs_1_.refs_3_), channel_id=1, source_target_pairs={{0,2},{2,0},{1,3},{3,1},{4,6},{6,4},{5,7},{7,5},{8,10},{10,8},{9,1... | collective-permute-start | bytes 1572872 | tf_op jit(solution)/shard_map/ppermute | solution.py:37
  298.3 11.9 %collective-permute-start.38 = (bf16[256,1024]{1,0:T(8,128)(2,1)S(1)}, bf16[256,1024]{1,0:T(8,128)(2,1)S(1)}, u32[]{:S(2)}, u32[]{:S(2)}) collective-permute-start(bf16[256,1024]{1,0:T(8,128)(2,1)S(1)} %get-tuple-element.133), channel_id=1, source_target_pairs={{0,2},{2,0},{1,3},{3,1},{4,6},{6,4},{5,7},{7,5},{8,10},{10,8},{9,1... | collective-permute-start | bytes 1572872 | tf_op jit(solution)/shard_map/ppermute | solution.py:37
  336.3 16.6 %collective-permute-start.50 = (f32[12,32,128]{2,1,0:T(8,128)S(1)}, f32[12,32,128]{2,1,0:T(8,128)S(1)}, u32[]{:S(2)}, u32[]{:S(2)}) collective-permute-start(f32[12,32,128]{2,1,0:T(8,128)S(1)} %slice_bitcast_fusion.5), channel_id=1, source_target_pairs={{0,4},{4,0},{1,5},{5,1},{2,6},{6,2},{3,7},{7,3},{8,12},{12,8},{9,1... | collective-permute-start | bytes 589832 | tf_op jit(solution)/shard_map/ppermute | solution.py:41
  353.7 170.4 %all-gather.20.cloned.1.call-start = ((), (), s32[]{:S(2)}) async-start(), calls=%async_computation.6 | async-start | bytes 3514368 | tf_op jit(solution)/shard_map/all_gather | solution.py:1280
  357.1 21.1 %collective-permute-start.39 = (bf16[256,512]{1,0:T(8,128)(2,1)}, bf16[256,512]{1,0:T(8,128)(2,1)}, u32[]{:S(2)}, u32[]{:S(2)}) collective-permute-start(bf16[256,512]{1,0:T(8,128)(2,1)} %get-tuple-element.202), channel_id=1, source_target_pairs={{0,2},{2,0},{1,3},{3,1},{4,6},{6,4},{5,7},{7,5},{8,10},{10,8},{9,1... | collective-permute-start | bytes 786440 | tf_op jit(solution)/shard_map/ppermute | solution.py:37
  413.1 14.7 %collective-permute-start.47 = (bf16[256,768]{1,0:T(8,128)(2,1)S(1)}, bf16[256,768]{1,0:T(8,128)(2,1)S(1)}, u32[]{:S(2)}, u32[]{:S(2)}) collective-permute-start(bf16[256,768]{1,0:T(8,128)(2,1)S(1)} %get-tuple-element.192), channel_id=1, source_target_pairs={{0,2},{2,0},{1,3},{3,1},{4,6},{6,4},{5,7},{7,5},{8,10},{10,8},{9,1... | collective-permute-start | bytes 1179656 | tf_op jit(solution)/shard_map/ppermute | solution.py:37
  414.3 13.5 %collective-permute-start.48 = (bf16[256,768]{1,0:T(8,128)(2,1)S(1)}, bf16[256,768]{1,0:T(8,128)(2,1)S(1)}, u32[]{:S(2)}, u32[]{:S(2)}) collective-permute-start(bf16[256,768]{1,0:T(8,128)(2,1)S(1)} %get-tuple-element.191), channel_id=1, source_target_pairs={{0,4},{4,0},{1,5},{5,1},{2,6},{6,2},{3,7},{7,3},{8,12},{12,8},{9,1... | collective-permute-start | bytes 1179656 | tf_op jit(solution)/shard_map/ppermute | solution.py:41
  414.4 13.4 %collective-permute-start.49 = (bf16[256,768]{1,0:T(8,128)(2,1)S(1)}, bf16[256,768]{1,0:T(8,128)(2,1)S(1)}, u32[]{:S(2)}, u32[]{:S(2)}) collective-permute-start(bf16[256,768]{1,0:T(8,128)(2,1)S(1)} %get-tuple-element.190), channel_id=1, source_target_pairs={{0,6},{1,7},{2,4},{3,5},{4,2},{5,3},{6,0},{7,1},{8,14},{9,15},{10,... | collective-permute-start | bytes 1179656 | tf_op jit(solution)/shard_map/ppermute | solution.py:45
  468.8 12.9 %collective-permute-start.52 = (bf16[256,1024]{1,0:T(8,128)(2,1)S(1)}, bf16[256,1024]{1,0:T(8,128)(2,1)S(1)}, u32[]{:S(2)}, u32[]{:S(2)}) collective-permute-start(bf16[256,1024]{1,0:T(8,128)(2,1)S(1)} %get-tuple-element.173), channel_id=1, source_target_pairs={{0,2},{2,0},{1,3},{3,1},{4,6},{6,4},{5,7},{7,5},{8,10},{10,8},{9,1... | collective-permute-start | bytes 1572872 | tf_op jit(solution)/shard_map/ppermute | solution.py:37
  483.3 21.8 %collective-permute-start.62 = (bf16[4,12,32,128]{3,2,1,0:T(8,128)(2,1)S(1)}, bf16[4,12,32,128]{3,2,1,0:T(8,128)(2,1)S(1)}, u32[]{:S(2)}, u32[]{:S(2)}) collective-permute-start(bf16[4,12,32,128]{3,2,1,0:T(8,128)(2,1)S(1)} %pad_maximum_fusion.1.refs_3_), channel_id=1, source_target_pairs={{0,2},{2,0},{1,3},{3,1},{4,6},{6,4},{5,7},{7,5},{8,10},{10,8},{9,1... | collective-permute-start | bytes 1179656 | tf_op jit(solution)/shard_map/ppermute | solution.py:37
  490.4 23.3 %collective-permute-start.66 = (bf16[4,12,32,128]{3,2,1,0:T(8,128)(2,1)S(1)}, bf16[4,12,32,128]{3,2,1,0:T(8,128)(2,1)S(1)}, u32[]{:S(2)}, u32[]{:S(2)}) collective-permute-start(bf16[4,12,32,128]{3,2,1,0:T(8,128)(2,1)S(1)} %collective-permute-done.64.refs_7_), channel_id=1, source_target_pairs={{0,2},{2,0},{1,3},{3,1},{4,6},{6,4},{5,7},{7,5},{8,10},{10,8},{9,1... | collective-permute-start | bytes 1179656 | tf_op jit(solution)/shard_map/ppermute | solution.py:37
  492.6 25.4 %collective-permute-start.54 = (bf16[1,512,256]{2,1,0:T(8,128)(2,1)}, bf16[1,512,256]{2,1,0:T(8,128)(2,1)}, u32[]{:S(2)}, u32[]{:S(2)}) collective-permute-start(bf16[1,512,256]{2,1,0:T(8,128)(2,1)} %get-tuple-element.196), channel_id=1, source_target_pairs={{0,1},{1,0},{2,3},{3,2},{4,5},{5,4},{6,7},{7,6},{8,9},{9,8},{10,11... | collective-permute-start | bytes 786440 | tf_op jit(solution)/shard_map/ppermute | solution.py:33
  504.6 15.8 %collective-permute-start.61 = (bf16[4,12,32,128]{3,2,1,0:T(8,128)(2,1)S(1)}, bf16[4,12,32,128]{3,2,1,0:T(8,128)(2,1)S(1)}, u32[]{:S(2)}, u32[]{:S(2)}) collective-permute-start(bf16[4,12,32,128]{3,2,1,0:T(8,128)(2,1)S(1)} %pad_maximum_fusion.1.refs_3_), channel_id=1, source_target_pairs={{0,1},{1,0},{2,3},{3,2},{4,5},{5,4},{6,7},{7,6},{8,9},{9,8},{10,11... | collective-permute-start | bytes 1179656 | tf_op jit(solution)/shard_map/ppermute | solution.py:33
  504.6 15.8 %collective-permute-start.65 = (bf16[4,12,32,128]{3,2,1,0:T(8,128)(2,1)S(1)}, bf16[4,12,32,128]{3,2,1,0:T(8,128)(2,1)S(1)}, u32[]{:S(2)}, u32[]{:S(2)}) collective-permute-start(bf16[4,12,32,128]{3,2,1,0:T(8,128)(2,1)S(1)} %collective-permute-done.64.refs_7_), channel_id=1, source_target_pairs={{0,1},{1,0},{2,3},{3,2},{4,5},{5,4},{6,7},{7,6},{8,9},{9,8},{10,11... | collective-permute-start | bytes 1179656 | tf_op jit(solution)/shard_map/ppermute | solution.py:33
  505.1 15.3 %collective-permute-start.63 = (bf16[4,12,32,128]{3,2,1,0:T(8,128)(2,1)S(1)}, bf16[4,12,32,128]{3,2,1,0:T(8,128)(2,1)S(1)}, u32[]{:S(2)}, u32[]{:S(2)}) collective-permute-start(bf16[4,12,32,128]{3,2,1,0:T(8,128)(2,1)S(1)} %collective-permute-done.62.refs_5_), channel_id=1, source_target_pairs={{0,1},{1,0},{2,3},{3,2},{4,5},{5,4},{6,7},{7,6},{8,9},{9,8},{10,11... | collective-permute-start | bytes 1179656 | tf_op jit(solution)/shard_map/ppermute | solution.py:33
  (137 other events, 1852.8 us)
Sparse Core Ops, SparseCore 0:
  10.2 29.7 all-gather.7
  42.2 27.5 all-gather.9
  72.0 27.4 all-gather.11
  101.4 27.4 all-gather.13
  130.9 45.5 all-gather.15
  353.8 63.3 all-gather.17
  447.1 74.1 all-gather.19
